TPU v7x, 256 devices: a whole 4x4x8 slice. The times are simulated.
256 devices in a mesh: slab: 64 (over y, x, z_hi), pt: 4 (over z_lo, core).
Axes of the slice: x: 4, y: 4, z: 8 (z_hi: 4, z_lo: 2; z = z_hi * 2 + z_lo), core: 2. Of those that a mesh axis runs over, the one named last changes fastest.
Arguments:
- orbitals: bfloat16 [131072, 256], P('slab'), may hold values from -6 to 6
- potential: float32 [131072], P('slab'), may hold values from -1 to 1
- fit_matrix: bfloat16 [131072, 8192], P('slab', 'pt'), may hold values from -0.00390625 to 0.00390625
- owner_rows: int32 [4, 64, 64], P(None, 'slab'), may hold values from 0 to 2047, as said below
- owner_count: int32 [4, 64], replicated, may hold values from 0 to 64, as said below
Outputs:
- filtered: bfloat16 [131072, 256], P('slab')
Inputs may be any that keep to these rules, and one draw needn't show every extreme that they name: `owner_count`: for each block p the counts over slabs sum to 2048, and in every block some slab lists exactly 64 points. `owner_rows`: the listed entries (c < owner_count[p, s]) of slab s are distinct over all blocks p and slots c; the other entries are 0.
All inputs are finite; a program needn't handle non-finite values.
Results may differ from a plain program's by a relative error of at most 0.0054.
Values may be sent and summed in bfloat16 or wider, within the bound.
No kernel may reach another device: no remote copies, remote signals or barrier semaphores. Data moves between devices by JAX's collectives and lax.ppermute only.
A program may use at most 64 MiB of HBM per device.

v0:
```python
import jax
import jax.numpy as jnp
from jax import lax
from jax.sharding import PartitionSpec as P

DEG = 2
CZ = 8
NY = 8
NX = 32


stencil_coef = (-205.0 / 72.0, 8.0 / 5.0, -1.0 / 5.0, 8.0 / 315.0, -1.0 / 560.0)


def extended(cells, sides, width):
    for axis, dim in sides:
        count = lax.axis_size(axis)
        head = lax.slice_in_dim(cells, 0, width, axis=dim)
        tail = lax.slice_in_dim(cells, cells.shape[dim] - width, cells.shape[dim], axis=dim)
        cells = jnp.concatenate(
            [
                lax.ppermute(tail, axis, [(i, (i + 1) % count) for i in range(count)]),
                cells,
                lax.ppermute(head, axis, [((i + 1) % count, i) for i in range(count)]),
            ],
            axis=dim,
        )
    return cells


def plane_table():
    cell_ids = jnp.arange(NY * NX, dtype=jnp.int32)
    row_y = cell_ids // NX
    col_x = cell_ids % NX
    diff_y = (row_y[:, None] - row_y[None, :]) % NY
    diff_x = (col_x[:, None] - col_x[None, :]) % NX
    same_y = row_y[:, None] == row_y[None, :]
    same_x = col_x[:, None] == col_x[None, :]
    table = jnp.zeros((NY * NX, NY * NX), jnp.float32)
    for offset in range(1, 5):
        along_x = (same_y & (diff_x == offset % NX)).astype(jnp.float32) + (
            same_y & (diff_x == -offset % NX)
        ).astype(jnp.float32)
        along_y = (same_x & (diff_y == offset % NY)).astype(jnp.float32) + (
            same_x & (diff_y == -offset % NY)
        ).astype(jnp.float32)
        table = table + stencil_coef[offset] * (along_x + along_y)
    return table


def local_terms(vectors, potential):
    share_cols = vectors.shape[1]
    blocked = vectors.reshape(CZ, NY * NX, share_cols)
    padded = extended(blocked, (("slab", 0),), 4)
    center = blocked.astype(jnp.float32)
    in_plane = jnp.einsum(
        "pq,zqb->zpb",
        plane_table(),
        center,
        precision=lax.Precision.HIGHEST,
        preferred_element_type=jnp.float32,
    )
    summed = 3.0 * stencil_coef[0] * center + in_plane
    for offset in range(1, 5):
        upper = padded[4 + offset : 4 + offset + CZ].astype(jnp.float32)
        lower = padded[4 - offset : 4 - offset + CZ].astype(jnp.float32)
        summed = summed + stencil_coef[offset] * (upper + lower)
    kinetic = (-0.5 * summed).reshape(CZ * NY * NX, share_cols)
    return kinetic + potential[:, None] * center.reshape(CZ * NY * NX, share_cols)


def point_positions(count_row, capacity, point_total):
    inclusive = jnp.cumsum(count_row)
    point_ranks = jnp.arange(point_total, dtype=jnp.int32)
    before = (inclusive[None, :] <= point_ranks[:, None]).astype(jnp.int32)
    slab_of = jnp.sum(before, axis=1)
    base_count = jnp.sum(before * count_row[None, :], axis=1)
    return slab_of * capacity + point_ranks - base_count


def chebyshev(column_part, first_points, apply_op, next_points):
    previous = column_part
    current = column_part
    field_points = first_points
    for turn_number in range(DEG):
        applied = apply_op(current, field_points)
        scaled = applied - 3.5 * current.astype(jnp.float32)
        if turn_number == 0:
            upcoming = (scaled / 4.0).astype(jnp.bfloat16)
        else:
            upcoming = (0.5 * scaled - previous.astype(jnp.float32)).astype(jnp.bfloat16)
        previous, current = (current, upcoming)
        if turn_number + 1 < DEG:
            field_points = next_points(current)
    return current


def body(orbitals, potential, fit_matrix, owner_rows, owner_count):
    block_index = lax.axis_index("pt")
    capacity = owner_rows.shape[2]
    all_rows = owner_rows[:, 0, :]
    mine_rows = lax.dynamic_index_in_dim(all_rows, block_index, 0, keepdims=False)
    count_row = lax.dynamic_index_in_dim(owner_count, block_index, 0, keepdims=False)
    positions = point_positions(count_row, capacity, fit_matrix.shape[1])

    def gather_points(vectors):
        picked = jnp.take(vectors, mine_rows, axis=0)
        gathered = lax.all_gather(picked, "slab", axis=0, tiled=True)
        return jnp.take(gathered, positions, axis=0)

    psi_points = gather_points(orbitals)
    density = lax.dot_general(
        orbitals, psi_points, (((1,), (1,)), ((), ())), preferred_element_type=jnp.float32
    )
    kernel = (fit_matrix.astype(jnp.float32) * density).astype(jnp.bfloat16)

    def apply_whole(vectors, field_points):
        partial_value = jnp.dot(kernel, field_points, preferred_element_type=jnp.float32)
        exch_term = lax.psum(partial_value, "pt")
        return local_terms(vectors, potential) - exch_term

    return chebyshev(orbitals, psi_points, apply_whole, gather_points)


def solution(mesh):
    placed = (P("slab", None), P("slab"), P("slab", "pt"), P(None, "slab", None), P())
    return jax.shard_map(
        body, mesh=mesh, in_specs=placed, out_specs=P("slab", None), check_vma=False
    )
```

profile of v0, /device:TPU:1, one launch (start us, length us, event | category | flops | bytes accessed | tf_op | source)
XLA Modules:
  0.0 368.9 jit_solution(4444609752312211204)
XLA Ops:
  7.2 2.0 gather_fusion
  10.0 12.3 %copy.10 = bf16[2048,2048]{0,1:T(8,128)(2,1)} copy(bf16[2048,2048]{1,0:T(8,128)(2,1)} %param.11) | data formatting | bytes 16777216 | tf_op args[2]
  23.5 67.2 %all-gather.3.cloned.1.call-done = bf16[4096,256]{1,0:T(8,128)(2,1)} async-done(((bf16[64,256]{1,0:T(8,128)(2,1)}), bf16[4096,256]{1,0:T(8,128)(2,1)}) %all-gather.3.cloned.1.call-update) | async-done | bytes 2097168 | tf_op jit(solution)/shard_map/all_gather | solution.py:108
  90.7 8.5 %gather_fusion.1 = bf16[2048,256]{1,0:T(8,128)(2,1)S(1)} fusion(bf16[4096,256]{1,0:T(8,128)(2,1)} %all-gather.3.cloned.1.call-done, s32[2048]{0:T(1024)S(1)} %broadcast_clamp_fusion), kind=kCustom, calls=%fused_computation.1.clone | custom fusion | bytes 2105344 | tf_op jit(solution)/shard_map/jit(_take)/gather | solution.py:109
  99.3 4.8 %fusion = bf16[2048,2048]{0,1:T(8,128)(2,1)S(1)} fusion(bf16[2048,2048]{0,1:T(8,128)(2,1)} %copy.10, bf16[2048,256]{1,0:T(8,128)(2,1)S(1)} %copy-done.1, bf16[2048,256]{1,0:T(8,128)(2,1)S(1)} %gather_fusion.1, pred[2048]{0:T(1024)(128)(4,1)S(1)} %compare_and_fusion.15), kind=kOutput, calls=%fused_computation.5 | convolution fusion | flops 2160590848 | bytes 18876416 | tf_op jit(solution)/shard_map/dot_general | solution.py:112
  104.1 3.2 copy-done
  107.3 4.2 %fusion.37 = f32[2048,256]{1,0:T(8,128)} fusion(bf16[2048,2048]{0,1:T(8,128)(2,1)S(1)} %fusion, bf16[2048,256]{1,0:T(8,128)(2,1)S(1)} %gather_fusion.1, pred[2048]{0:T(1024)(128)(4,1)S(1)} %compare_and_fusion.15), kind=kOutput, calls=%fused_computation.102 | convolution fusion | flops 2148007936 | bytes 11536384 | tf_op jit(solution)/shard_map/dot_general | solution.py:118
  111.7 2.5 collective-permute-start.1
  114.3 5.3 %collective-permute-start = (bf16[4,256,256]{2,1,0:T(8,128)(2,1)S(1)}, bf16[4,256,256]{2,1,0:T(8,128)(2,1)S(1)}, u32[]{:S(2)}, u32[]{:S(2)}) collective-permute-start(bf16[4,256,256]{2,1,0:T(8,128)(2,1)S(1)} %bitcast.61), channel_id=1, source_target_pairs={{4,0},{8,4},{12,8},{16,12},{20,16},{24,20},{28,24},{32,28},{36,32}... | collective-permute-start | bytes 1572872 | tf_op jit(solution)/shard_map/ppermute | solution.py:24
  119.6 9.3 %collective-permute-done.1 = bf16[4,256,256]{2,1,0:T(8,128)(2,1)S(1)} collective-permute-done((bf16[4,256,256]{2,1,0:T(8,128)(2,1)S(1)}, bf16[4,256,256]{2,1,0:T(8,128)(2,1)S(1)}, u32[]{:S(2)}, u32[]{:S(2)}) %collective-permute-start.1) | collective-permute-done | bytes 524320 | tf_op jit(solution)/shard_map/ppermute | solution.py:22
  128.9 5.9 %collective-permute-done = bf16[4,256,256]{2,1,0:T(8,128)(2,1)S(1)} collective-permute-done((bf16[4,256,256]{2,1,0:T(8,128)(2,1)S(1)}, bf16[4,256,256]{2,1,0:T(8,128)(2,1)S(1)}, u32[]{:S(2)}, u32[]{:S(2)}) %collective-permute-start) | collective-permute-done | bytes 524320 | tf_op jit(solution)/shard_map/ppermute | solution.py:24
  134.8 5.7 %fusion.20 = f32[8,256,256]{2,1,0:T(8,128)} fusion(bf16[8,256,256]{2,1,0:T(8,128)(2,1)S(1)} %bitcast.59, bf16[4,256,256]{2,1,0:T(8,128)(2,1)S(1)} %collective-permute-done.1, bf16[4,256,256]{2,1,0:T(8,128)(2,1)S(1)} %collective-permute-done, s32[256]{0:T(256)S(1)} %get-tuple-element.17, s32[256]{0:T(256)S(1)} %get-tuple-element.18), kind=kOutput, calls=%fused_computation.44 | convolution fusion | flops 1633288192 | bytes 5246976 | tf_op jit(solution)/shard_map/pq,zqb->zpb/dot_general | solution.py:56
  140.5 46.3 %all-reduce.3.cloned.1.call-done = f32[2048,256]{1,0:T(8,128)} async-done(((f32[2048,256]{1,0:T(8,128)}), f32[2048,256]{1,0:T(8,128)}) %all-reduce.3.cloned.1.call-update) | async-done | bytes 2097168 | tf_op jit(solution)/shard_map/psum | solution.py:119
  186.8 2.8 fusion.9
  191.2 76.1 %all-gather.5.cloned.1.call-done = bf16[4096,256]{1,0:T(8,128)(2,1)} async-done(((bf16[64,256]{1,0:T(8,128)(2,1)}), bf16[4096,256]{1,0:T(8,128)(2,1)}) %all-gather.5.cloned.1.call-update) | async-done | bytes 2097168 | tf_op jit(solution)/shard_map/all_gather | solution.py:108
  267.3 8.5 %gather_fusion.3 = bf16[2048,256]{1,0:T(8,128)(2,1)S(1)} fusion(bf16[4096,256]{1,0:T(8,128)(2,1)} %all-gather.5.cloned.1.call-done, s32[2048]{0:T(1024)S(1)} %broadcast_clamp_fusion), kind=kCustom, calls=%fused_computation.3.clone | custom fusion | bytes 2105344 | tf_op jit(solution)/shard_map/jit(_take)/gather | solution.py:109
  275.8 7.5 %fusion.33 = f32[2048,256]{1,0:T(8,128)} fusion(bf16[2048,2048]{0,1:T(8,128)(2,1)} %copy-done, bf16[2048,256]{1,0:T(8,128)(2,1)S(1)} %gather_fusion.3, pred[2048]{0:T(1024)(128)(4,1)S(1)} %compare_and_fusion.15), kind=kOutput, calls=%fused_computation.73 | convolution fusion | flops 2148007936 | bytes 11536384 | tf_op jit(solution)/shard_map/dot_general | solution.py:118
  283.4 2.5 collective-permute-start.3
  285.9 5.3 %collective-permute-start.2 = (bf16[4,256,256]{2,1,0:T(8,128)(2,1)S(1)}, bf16[4,256,256]{2,1,0:T(8,128)(2,1)S(1)}, u32[]{:S(2)}, u32[]{:S(2)}) collective-permute-start(bf16[4,256,256]{2,1,0:T(8,128)(2,1)S(1)} %bitcast.63), channel_id=1, source_target_pairs={{4,0},{8,4},{12,8},{16,12},{20,16},{24,20},{28,24},{32,28},{36,32}... | collective-permute-start | bytes 1572872 | tf_op jit(solution)/shard_map/ppermute | solution.py:24
  291.3 9.3 %collective-permute-done.3 = bf16[4,256,256]{2,1,0:T(8,128)(2,1)S(1)} collective-permute-done((bf16[4,256,256]{2,1,0:T(8,128)(2,1)S(1)}, bf16[4,256,256]{2,1,0:T(8,128)(2,1)S(1)}, u32[]{:S(2)}, u32[]{:S(2)}) %collective-permute-start.3) | collective-permute-done | bytes 524320 | tf_op jit(solution)/shard_map/ppermute | solution.py:22
  300.6 6.0 %collective-permute-done.2 = bf16[4,256,256]{2,1,0:T(8,128)(2,1)S(1)} collective-permute-done((bf16[4,256,256]{2,1,0:T(8,128)(2,1)S(1)}, bf16[4,256,256]{2,1,0:T(8,128)(2,1)S(1)}, u32[]{:S(2)}, u32[]{:S(2)}) %collective-permute-start.2) | collective-permute-done | bytes 524320 | tf_op jit(solution)/shard_map/ppermute | solution.py:24
  306.5 4.7 %fusion.15 = f32[8,256,256]{2,1,0:T(8,128)} fusion(bf16[8,256,256]{2,1,0:T(8,128)(2,1)S(1)} %bitcast.60, bf16[4,256,256]{2,1,0:T(8,128)(2,1)S(1)} %collective-permute-done.3, bf16[4,256,256]{2,1,0:T(8,128)(2,1)S(1)} %collective-permute-done.2, s32[256]{0:T(256)S(1)} %get-tuple-element.17, s32[256]{0:T(256)S(1)} %get-tuple-element.18), kind=kOutput, calls=%fused_computation.38 | convolution fusion | flops 1633288192 | bytes 5246976 | tf_op jit(solution)/shard_map/pq,zqb->zpb/dot_general | solution.py:56
  311.2 47.2 %all-reduce.5.cloned.1.call-done = f32[2048,256]{1,0:T(8,128)} async-done(((f32[2048,256]{1,0:T(8,128)}), f32[2048,256]{1,0:T(8,128)}) %all-reduce.5.cloned.1.call-update) | async-done | bytes 2097168 | tf_op jit(solution)/shard_map/psum | solution.py:119
  358.4 3.9 %fusion.10 = bf16[2048,256]{1,0:T(8,128)(2,1)} fusion(bf16[2048,256]{1,0:T(8,128)(2,1)S(1)} %copy-done.1, f32[2048,256]{1,0:T(8,128)} %all-reduce.5.cloned.1.call-done, bf16[2048,256]{1,0:T(8,128)(2,1)S(1)} %fusion.9, f32[8,256,256]{2,1,0:T(8,128)} %fusion.15, f32[2048]{0:T(1024)S(1)} %copy-done.2), kind=kLoop, calls=%fused_computation.32 | loop fusion | flops 5242880 | bytes 7348224 | tf_op jit(solution)/shard_map/convert_element_type | solution.py:91
  (28 shorter events, 4.5 us)
Async XLA Ops:
  6.5 84.2 %all-gather.3.cloned.1.call-start = ((), (), s32[]{:S(2)}) async-start(), calls=%async_computation | async-start | bytes 2129920 | tf_op jit(solution)/shard_map/all_gather | solution.py:108
  9.9 176.8 %all-reduce.3.cloned.1.call-start = ((), (), s32[]{:S(2)}) async-start(), calls=%async_computation.1 | async-start | bytes 4194304 | tf_op jit(solution)/shard_map/psum | solution.py:119
  23.5 75.7 %copy-start.1 = (bf16[2048,256]{1,0:T(8,128)(2,1)S(1)}, bf16[2048,256]{1,0:T(8,128)(2,1)}, u32[]{:S(2)}) copy-start(bf16[2048,256]{1,0:T(8,128)(2,1)} %param.9) | copy-start | bytes 3145732
  104.1 3.2 copy-start
  111.6 155.7 %all-gather.5.cloned.1.call-start = ((), (), s32[]{:S(2)}) async-start(), calls=%async_computation.2 | async-start | bytes 2129920 | tf_op jit(solution)/shard_map/all_gather | solution.py:108
  111.7 17.2 %collective-permute-start.1 = (bf16[4,256,256]{2,1,0:T(8,128)(2,1)S(1)}, bf16[4,256,256]{2,1,0:T(8,128)(2,1)S(1)}, u32[]{:S(2)}, u32[]{:S(2)}) collective-permute-start(bf16[4,256,256]{2,1,0:T(8,128)(2,1)S(1)} %bitcast.62), channel_id=1, source_target_pairs={{0,4},{4,8},{8,12},{12,16},{16,20},{20,24},{24,28},{28,32},{32,36}... | collective-permute-start | bytes 1572872 | tf_op jit(solution)/shard_map/ppermute | solution.py:22
  114.3 20.5 %collective-permute-start = (bf16[4,256,256]{2,1,0:T(8,128)(2,1)S(1)}, bf16[4,256,256]{2,1,0:T(8,128)(2,1)S(1)}, u32[]{:S(2)}, u32[]{:S(2)}) collective-permute-start(bf16[4,256,256]{2,1,0:T(8,128)(2,1)S(1)} %bitcast.61), channel_id=1, source_target_pairs={{4,0},{8,4},{12,8},{16,12},{20,16},{24,20},{28,24},{32,28},{36,32}... | collective-permute-start | bytes 1572872 | tf_op jit(solution)/shard_map/ppermute | solution.py:24
  134.8 52.0 %copy-start.2 = (f32[2048]{0:T(1024)S(1)}, f32[2048]{0:T(1024)}, u32[]{:S(2)}) copy-start(f32[2048]{0:T(1024)} %param.10) | copy-start | bytes 24580
  191.0 167.4 %all-reduce.5.cloned.1.call-start = ((), (), s32[]{:S(2)}) async-start(), calls=%async_computation.3 | async-start | bytes 4194304 | tf_op jit(solution)/shard_map/psum | solution.py:119
  283.4 17.2 %collective-permute-start.3 = (bf16[4,256,256]{2,1,0:T(8,128)(2,1)S(1)}, bf16[4,256,256]{2,1,0:T(8,128)(2,1)S(1)}, u32[]{:S(2)}, u32[]{:S(2)}) collective-permute-start(bf16[4,256,256]{2,1,0:T(8,128)(2,1)S(1)} %bitcast.64), channel_id=1, source_target_pairs={{0,4},{4,8},{8,12},{12,16},{16,20},{20,24},{24,28},{28,32},{32,36}... | collective-permute-start | bytes 1572872 | tf_op jit(solution)/shard_map/ppermute | solution.py:22
  285.9 20.6 %collective-permute-start.2 = (bf16[4,256,256]{2,1,0:T(8,128)(2,1)S(1)}, bf16[4,256,256]{2,1,0:T(8,128)(2,1)S(1)}, u32[]{:S(2)}, u32[]{:S(2)}) collective-permute-start(bf16[4,256,256]{2,1,0:T(8,128)(2,1)S(1)} %bitcast.63), channel_id=1, source_target_pairs={{4,0},{8,4},{12,8},{16,12},{20,16},{24,20},{28,24},{32,28},{36,32}... | collective-permute-start | bytes 1572872 | tf_op jit(solution)/shard_map/ppermute | solution.py:24
Sparse Core Ops, SparseCore 0:
  10.6 80.0 all-gather.2
  111.7 74.9 all-reduce.2
  191.1 76.1 all-gather.4
  283.4 74.9 all-reduce.4
where the time goes:
time: 369 us
  waiting for transfers between devices  267 us (72%)
  local copies, waits for them, and re-layouts  36.2 us (10%)
  matrix products  27 us (7%)
  starting transfers between devices  16.1 us (4%)
  between operations  13.2 us (4%)
  other arithmetic  9.22 us (2%)
    all_gather x2, waiting for transfers between devices, gather_points(): gathered = lax.all_gather(picked, 'slab', axis=0, tiled=True)  143 us
    psum x2, waiting for transfers between devices, apply_whole(): exch_term = lax.psum(partial_value, 'pt')  93.5 us
    ppermute x2, waiting for transfers between devices, extended(): lax.ppermute(tail, axis, [(i, (i + 1) % count) for i in range(count)])  18.6 us
    gather x2, local copies, waits for them, and re-layouts, gather_points(): return jnp.take(gathered, positions, axis=0)  17 us
    unnamed x7, local copies, waits for them, and re-layouts  15.5 us
    ppermute x2, waiting for transfers between devices, extended(): lax.ppermute(head, axis, [((i + 1) % count, i) for i in range(count)])  11.9 us
    dot_general x2, matrix products, apply_whole(): jnp.dot(kernel, field_points, preferred_element_type=jnp.float32)  11.7 us
    ppermute x2, starting transfers between devices, extended(): lax.ppermute(head, axis, [((i + 1) % count, i) for i in range(count)])  10.7 us
  transfers between devices with their start and end apart: 8, of which 8 were waited for; matrix products, arithmetic and copies ran while one was open for 7% of the time, Pallas kernels for 0%

commit v1 on v0

v1 whole, which is shorter than its diff:
```python
import functools

import jax
import jax.numpy as jnp
from jax import lax
from jax.experimental import pallas as pl
from jax.experimental.pallas import tpu as pltpu
from jax.sharding import PartitionSpec as P

NB = 256
HALF = 128
CZ = 8
NY = 8
NX = 32
PLANE = NY * NX
ROWS = CZ * PLANE
PTS = 2048
CAP = 64
WIN = 272
TILE = 256
STEPS = ROWS // TILE
BF = jnp.bfloat16
F32 = jnp.float32

stencil_coef = (-205.0 / 72.0, 8.0 / 5.0, -1.0 / 5.0, 8.0 / 315.0, -1.0 / 560.0)


def slab_id(y, x, z):
    return ((y % 4) * 4 + (x % 4)) * 4 + (z % 4)


def z_shift(d):
    return [(slab_id(y, x, z), slab_id(y, x, z - d)) for y in range(4) for x in range(4) for z in range(4)]


XY_GROUPS = [[slab_id(y, x, z) for y in range(4) for x in range(4)] for z in range(4)]
CORE_SWAP = [(i, i ^ 1) for i in range(4)]
CHIP_SWAP = [(i, i ^ 2) for i in range(4)]
EDGE_SWAP = [(s * 4 + 2 + c, ((s + 1) % 64) * 4 + c) for s in range(64) for c in range(2)] + [
    (s * 4 + c, ((s - 1) % 64) * 4 + 2 + c) for s in range(64) for c in range(2)
]


def plane_table():
    cell_ids = jnp.arange(PLANE, dtype=jnp.int32)
    row_y = cell_ids // NX
    col_x = cell_ids % NX
    diff_y = (row_y[:, None] - row_y[None, :]) % NY
    diff_x = (col_x[:, None] - col_x[None, :]) % NX
    same_y = row_y[:, None] == row_y[None, :]
    same_x = col_x[:, None] == col_x[None, :]
    table = jnp.zeros((PLANE, PLANE), F32)
    for offset in range(1, 5):
        along_x = (same_y & (diff_x == offset % NX)).astype(F32) + (same_y & (diff_x == -offset % NX)).astype(F32)
        along_y = (same_x & (diff_y == offset % NY)).astype(F32) + (same_x & (diff_y == -offset % NY)).astype(F32)
        table = table + stencil_coef[offset] * (along_x + along_y)
    return table


def local_terms(lower, own, upper, potential):
    planes = jnp.concatenate([lower, own, upper], axis=0).reshape(12, PLANE, HALF).astype(F32)
    center = own.reshape(4, PLANE, HALF).astype(F32)
    in_plane = jnp.einsum(
        "pq,zqb->zpb", plane_table(), center, precision=lax.Precision.HIGHEST, preferred_element_type=F32
    )
    summed = 3.0 * stencil_coef[0] * center + in_plane
    for offset in range(1, 5):
        summed = summed + stencil_coef[offset] * (planes[4 + offset : 8 + offset] + planes[4 - offset : 8 - offset])
    return (-0.5 * summed).reshape(1024, HALF) + potential[:, None] * own.astype(F32)


def pick_kernel(rows_ref, field_ref, out_ref):
    cols = lax.broadcasted_iota(jnp.int32, (CAP, ROWS), 1)
    hot = jnp.where(rows_ref[...] == cols, 1.0, 0.0).astype(BF)
    out_ref[...] = jnp.dot(hot, field_ref[...], preferred_element_type=F32).astype(BF)


def pick_rows(rows, field):
    return pl.pallas_call(
        pick_kernel, out_shape=jax.ShapeDtypeStruct((CAP, NB), BF), name="pick_rows"
    )(rows, field)


def compact(base_ref, where_ref, got_ref, sum_ref, psi_ref):
    sum_ref[...] = jnp.zeros_like(sum_ref)
    line = lax.broadcasted_iota(jnp.int32, (WIN, TILE), 0)
    for g in range(16):
        hot = jnp.where(where_ref[g : g + 1, :] == line, 1.0, 0.0).astype(BF)
        placed = jnp.dot(hot, got_ref[g], preferred_element_type=F32)
        at = pl.multiple_of(base_ref[g], 8)
        sum_ref[pl.ds(at, WIN), :] += placed
    psi_ref[...] = sum_ref[pl.ds(0, PTS), :].astype(BF)


def first_kernel(base_ref, where_ref, got_ref, orb_ref, fit_ref, local_ref, rows_ref,
                 kern_ref, keep_ref, send_ref, pick_ref, sum_ref, psi_ref, acc_ref):
    step = pl.program_id(0)
    core = base_ref[16]
    chip = base_ref[17]

    @pl.when(step == 0)
    def _():
        compact(base_ref, where_ref, got_ref, sum_ref, psi_ref)
        acc_ref[...] = jnp.zeros_like(acc_ref)

    density = lax.dot_general(
        orb_ref[...], psi_ref[...], (((1,), (1,)), ((), ())), preferred_element_type=F32
    )
    kern = (fit_ref[...].astype(F32) * density).astype(BF)
    kern_ref[...] = kern
    part = -jnp.dot(kern, psi_ref[...], preferred_element_type=F32)
    left, right = part[:, :HALF], part[:, HALF:]
    keep_ref[...] = jnp.where(core == 0, left, right)
    send_ref[...] = jnp.where(core == 0, right, left).astype(BF)
    local = local_ref[pl.ds(pl.multiple_of((step % 4) * TILE, TILE), TILE), :]
    local = jnp.where(step // 4 == chip, local, 0.0)
    whole = jnp.concatenate(
        [left + jnp.where(core == 0, local, 0.0), right + jnp.where(core == 0, 0.0, local)], axis=1
    ).astype(BF)
    lanes = lax.broadcasted_iota(jnp.int32, (4 * CAP, TILE), 1) + step * TILE
    hot = jnp.where(rows_ref[...] == lanes, 1.0, 0.0).astype(BF)
    acc_ref[...] += jnp.dot(hot, whole, preferred_element_type=F32)

    @pl.when(step == STEPS - 1)
    def _():
        pick_ref[...] = acc_ref[...].astype(BF)


def whole_block(shape):
    return pl.BlockSpec(shape, lambda i, *_: (0,) * len(shape))


def row_block(cols):
    return pl.BlockSpec((TILE, cols), lambda i, *_: (i, 0))


def first_apply(base, where, got, orbitals, fit_matrix, local, rows):
    return pl.pallas_call(
        first_kernel,
        name="first_apply",
        grid_spec=pltpu.PrefetchScalarGridSpec(
            num_scalar_prefetch=1,
            grid=(STEPS,),
            in_specs=[
                whole_block((16, TILE)),
                whole_block((16, TILE, NB)),
                row_block(NB),
                row_block(PTS),
                whole_block((1024, HALF)),
                whole_block((4 * CAP, 1)),
            ],
            out_specs=[row_block(PTS), row_block(HALF), row_block(HALF), whole_block((4 * CAP, NB))],
            scratch_shapes=[
                pltpu.VMEM((PTS + WIN, NB), F32),
                pltpu.VMEM((PTS, NB), BF),
                pltpu.VMEM((4 * CAP, NB), F32),
            ],
        ),
        out_shape=[
            jax.ShapeDtypeStruct((ROWS, PTS), BF),
            jax.ShapeDtypeStruct((ROWS, HALF), F32),
            jax.ShapeDtypeStruct((ROWS, HALF), BF),
            jax.ShapeDtypeStruct((4 * CAP, NB), BF),
        ],
    )(base, where, got, orbitals, fit_matrix, local, rows)


def second_kernel(base_ref, where_ref, got_ref, kern_ref, keep_ref, send_ref, sum_ref, psi_ref):
    core = base_ref[16]

    @pl.when(pl.program_id(0) == 0)
    def _():
        compact(base_ref, where_ref, got_ref, sum_ref, psi_ref)

    part = -jnp.dot(kern_ref[...], psi_ref[...], preferred_element_type=F32)
    left, right = part[:, :HALF], part[:, HALF:]
    keep_ref[...] = jnp.where(core == 0, left, right)
    send_ref[...] = jnp.where(core == 0, right, left).astype(BF)


def second_apply(base, where, got, kern):
    return pl.pallas_call(
        second_kernel,
        name="second_apply",
        grid_spec=pltpu.PrefetchScalarGridSpec(
            num_scalar_prefetch=1,
            grid=(STEPS,),
            in_specs=[whole_block((16, TILE)), whole_block((16, TILE, NB)), row_block(PTS)],
            out_specs=[row_block(HALF), row_block(HALF)],
            scratch_shapes=[pltpu.VMEM((PTS + WIN, NB), F32), pltpu.VMEM((PTS, NB), BF)],
        ),
        out_shape=[jax.ShapeDtypeStruct((ROWS, HALF), F32), jax.ShapeDtypeStruct((ROWS, HALF), BF)],
    )(base, where, got, kern)


def gather_points(own):
    along_z = [own] + [lax.ppermute(own, "slab", z_shift(d)) for d in (1, 2, 3)]
    column = jnp.concatenate(along_z, axis=0)
    spread = jnp.broadcast_to(column[None], (16, TILE, NB))
    return lax.all_to_all(spread, "slab", 0, 0, axis_index_groups=XY_GROUPS)


def body(orbitals, potential, fit_matrix, owner_rows, owner_count):
    point_block = lax.axis_index("pt")
    slab = lax.axis_index("slab")
    core = point_block % 2
    chip = point_block // 2
    my_z = slab % 4
    row0 = chip * 1024

    mine_rows = lax.dynamic_index_in_dim(owner_rows[:, 0, :], point_block, 0, keepdims=False)
    own0 = pick_rows(mine_rows.reshape(CAP, 1), orbitals)
    got0 = gather_points(own0)

    counts = lax.dynamic_index_in_dim(owner_count, point_block, 0, keepdims=False)
    group = jnp.arange(16, dtype=jnp.int32)
    slabs = group[:, None] * 4 + (my_z + jnp.arange(4, dtype=jnp.int32)[None, :]) % 4
    every = jnp.arange(64, dtype=jnp.int32)
    start = jnp.sum(jnp.where(every < slabs[:, :, None], counts, 0), axis=2)
    size = jnp.sum(jnp.where(every == slabs[:, :, None], counts, 0), axis=2)
    base = jnp.sum(jnp.where(every[None, :] < group[:, None] * 4, counts, 0), axis=1) // 8 * 8
    slot = jnp.arange(CAP, dtype=jnp.int32)
    where = jnp.where(slot < size[:, :, None], start[:, :, None] - base[:, None, None] + slot, -1).reshape(16, TILE)
    base = jnp.concatenate([base, core[None], chip[None]]).astype(jnp.int32)
    all_rows = owner_rows.reshape(4 * CAP, 1)

    def quadrant(field):
        return lax.dynamic_slice(field, (row0, core * HALF), (1024, HALF))

    potential_piece = lax.dynamic_slice(potential, (row0,), (1024,))
    field0 = quadrant(orbitals)
    inner0 = lax.dynamic_slice(orbitals, ((1 - chip) * 1024, core * HALF), (1024, HALF))

    def stencil(field, inner):
        outer = lax.ppermute(field, ("slab", "pt"), EDGE_SWAP)
        lower = jnp.where(chip == 0, outer, inner)
        upper = jnp.where(chip == 0, inner, outer)
        return local_terms(lower, field, upper, potential_piece)

    local0 = stencil(field0, inner0)

    kern, keep0, send0, picked = first_apply(base, where, got0, orbitals, fit_matrix, local0, all_rows)

    pieces = lax.all_to_all(picked.reshape(4, CAP, NB), "pt", 0, 0)
    applied = jnp.sum(pieces.astype(F32), axis=0)
    own1 = ((applied - 3.5 * own0.astype(F32)) / 4.0).astype(BF)
    got1 = gather_points(own1)

    def reduce_piece(keep, send):
        columns = keep + lax.ppermute(send, "pt", CORE_SWAP).astype(F32)
        away = lax.dynamic_slice(columns, ((1 - chip) * 1024, 0), (1024, HALF)).astype(BF)
        return lax.dynamic_slice(columns, (row0, 0), (1024, HALF)) + lax.ppermute(away, "pt", CHIP_SWAP).astype(F32)

    applied0 = local0 + reduce_piece(keep0, send0)
    field1 = ((applied0 - 3.5 * field0.astype(F32)) / 4.0).astype(BF)
    local1 = stencil(field1, lax.ppermute(field1, "pt", CHIP_SWAP))

    keep1, send1 = second_apply(base, where, got1, kern)
    applied1 = local1 + reduce_piece(keep1, send1)
    field2 = (0.5 * (applied1 - 3.5 * field1.astype(F32)) - field0.astype(F32)).astype(BF)

    other = lax.ppermute(field2, "pt", CHIP_SWAP)
    column = jnp.concatenate([jnp.where(chip == 0, field2, other), jnp.where(chip == 0, other, field2)], axis=0)
    other = lax.ppermute(column, "pt", CORE_SWAP)
    return jnp.concatenate([jnp.where(core == 0, column, other), jnp.where(core == 0, other, column)], axis=1)


def solution(mesh):
    placed = (P("slab", None), P("slab"), P("slab", "pt"), P(None, "slab", None), P())
    return jax.shard_map(
        body, mesh=mesh, in_specs=placed, out_specs=P("slab", None), check_vma=False
    )
```

time: 369 us -> 174 us (0.47)
  waiting for transfers between devices: 267 us -> 48.7 us
  Pallas kernels: 0 us -> 28.9 us
  starting transfers between devices: 16.1 us -> 44.9 us
  matrix products: 27 us -> 5.35 us
  between operations: 13.2 us -> 0.29 us
  local copies, waits for them, and re-layouts: 36.2 us -> 27.9 us
  other arithmetic: 9.22 us -> 16.8 us
    all_gather x2 -> x0, waiting for transfers between devices: 143 us -> none  [gather_points(): gathered = lax.all_gather(picked, 'slab', axis=0, tiled=True)]
    psum x2 -> x0, waiting for transfers between devices: 93.5 us -> none  [apply_whole(): exch_term = lax.psum(partial_value, 'pt')]
    pallas_call x0 -> x3, Pallas kernels: none -> 28.9 us  [the longest x1 15.8 us: first_apply(): pl.pallas_call(first_kernel, name='first_apply', grid_spec=pltpu.Prefetch...]
    gather x4 -> x0, local copies, waits for them, and re-layouts: 19.7 us -> none  [the longest x2 17 us: gather_points(): return jnp.take(gathered, positions, axis=0)]
    all_to_all x0 -> x3, waiting for transfers between devices: none -> 19.5 us  [the longest x2 16 us: gather_points(): return lax.all_to_all(spread, 'slab', 0, 0, axis_index_groups=XY_GROUPS)]
    dot_general x3 -> x0, matrix products: 16.5 us -> none  [the longest x2 11.7 us: apply_whole(): jnp.dot(kernel, field_points, preferred_element_type=jnp.float32)]
    ppermute x4 -> x15, starting transfers between devices: 15.7 us -> 31 us  [the longest x6 15.8 us: gather_points(): along_z = [own] + [lax.ppermute(own, 'slab', z_shift(d)) for d in (1, 2, 3)]]
    all_to_all x0 -> x3, starting transfers between devices: none -> 13.9 us  [the longest x2 7.75 us: gather_points(): return lax.all_to_all(spread, 'slab', 0, 0, axis_index_groups=XY_GROUPS)]
  transfers between devices with their start and end apart: 8 -> 18, of which waited for: 8 -> 11; matrix products, arithmetic and copies ran while one was open for 7% -> 23% of each run, Pallas kernels for 0% -> 0%
where the time goes in v1:
time: 174 us; the launch traced here: 173 us
  waiting for transfers between devices  48.7 us (28%)
  starting transfers between devices  44.9 us (26%)
  Pallas kernels  28.9 us (17%)
  local copies, waits for them, and re-layouts  27.9 us (16%)
  other arithmetic  16.8 us (10%)
  matrix products  5.35 us (3%)
    all_to_all x2, waiting for transfers between devices, gather_points(): return lax.all_to_all(spread, 'slab', 0, 0, axis_index_groups=XY_GROUPS)  16 us
    ppermute x6, starting transfers between devices, gather_points(): along_z = [own] + [lax.ppermute(own, 'slab', z_shift(d)) for d in (1, 2, 3)]  15.8 us
    pallas_call x1, Pallas kernels, first_apply(): pl.pallas_call(first_kernel, name='first_apply', grid_spec=pltpu.Prefetch...  15.8 us
    mul x8, local copies, waits for them, and re-layouts, local_terms(): stencil_coef[offset]  12.2 us
    ppermute x2, waiting for transfers between devices, reduce_piece(): lax.ppermute(away, 'pt', CHIP_SWAP).astype(F32)  11.4 us
    pallas_call x1, Pallas kernels, second_apply(): pl.pallas_call(second_kernel, name='second_apply', grid_spec=pltpu.Prefet...  10.9 us
    ppermute x2, starting transfers between devices, stencil(): outer = lax.ppermute(field, ('slab', 'pt'), EDGE_SWAP)  10 us
    all_to_all x2, starting transfers between devices, gather_points(): return lax.all_to_all(spread, 'slab', 0, 0, axis_index_groups=XY_GROUPS)  7.75 us
  transfers between devices with their start and end apart: 18, of which 11 were waited for; matrix products, arithmetic and copies ran while one was open for 23% of the time, Pallas kernels for 0%

profile of v1, /device:TPU:1, one launch (start us, length us, event | category | flops | bytes accessed | tf_op | source)
XLA Modules:
  0.0 172.9 jit_solution(2712025156278556450)
XLA Ops:
  1.4 2.2 %pick_rows.1 = bf16[64,256]{1,0:T(8,128)(2,1)} custom-call(s32[64,1]{1,0:T(8,128)} %copy.44.rows_ref, bf16[2048,256]{1,0:T(8,128)(2,1)} %orb_ref.1), custom_call_target="tpu_custom_call" | custom-call | tf_op jit(solution)/shard_map/pick_rows/pallas_call | solution.py:79
  3.6 3.8 %collective-permute-start.3 = (bf16[64,256]{1,0:T(8,128)(2,1)}, bf16[64,256]{1,0:T(8,128)(2,1)S(1)}, u32[]{:S(2)}, u32[]{:S(2)}) collective-permute-start(bf16[64,256]{1,0:T(8,128)(2,1)} %pick_rows.1), channel_id=1, source_target_pairs={{0,4},{4,8},{8,12},{12,0},{16,20},{20,24},{24,28},{28,16},{32,36},... | collective-permute-start | bytes 98312 | tf_op jit(solution)/shard_map/ppermute | solution.py:197
  7.4 5.1 %collective-permute-start.2 = (bf16[64,256]{1,0:T(8,128)(2,1)}, bf16[64,256]{1,0:T(8,128)(2,1)S(1)}, u32[]{:S(2)}, u32[]{:S(2)}) collective-permute-start(bf16[64,256]{1,0:T(8,128)(2,1)} %pick_rows.1), channel_id=1, source_target_pairs={{0,8},{4,12},{8,0},{12,4},{16,24},{20,28},{24,16},{28,20},{32,40},... | collective-permute-start | bytes 98312 | tf_op jit(solution)/shard_map/ppermute | solution.py:197
  12.5 2.4 %collective-permute-start.1 = (bf16[64,256]{1,0:T(8,128)(2,1)}, bf16[64,256]{1,0:T(8,128)(2,1)S(1)}, u32[]{:S(2)}, u32[]{:S(2)}) collective-permute-start(bf16[64,256]{1,0:T(8,128)(2,1)} %pick_rows.1), channel_id=1, source_target_pairs={{0,12},{4,0},{8,4},{12,8},{16,28},{20,16},{24,20},{28,24},{32,44},... | collective-permute-start | bytes 98312 | tf_op jit(solution)/shard_map/ppermute | solution.py:197
  15.9 4.3 %collective-permute-start = (bf16[1024,128]{1,0:T(8,128)(2,1)S(1)}, bf16[1024,128]{1,0:T(8,128)(2,1)}, u32[]{:S(2)}, u32[]{:S(2)}) collective-permute-start(bf16[1024,128]{1,0:T(8,128)(2,1)S(1)} %dynamic_slice.28), channel_id=1, source_target_pairs={{2,4},{3,5},{6,8},{7,9},{10,12},{11,13},{14,16},{15,17},{18,20},{1... | collective-permute-start | bytes 786440 | tf_op jit(solution)/shard_map/ppermute | solution.py:235
  23.1 3.8 %all-to-all-start = ((bf16[16,256,256]{2,1,0:T(8,128)(2,1)}), bf16[16,256,256]{2,1,0:T(8,128)(2,1)S(1)}, u32[]{:S(2)}, u32[]{:S(2)}) async-start(bf16[16,256,256]{2,1,0:T(8,128)(2,1)} %broadcast_in_dim.37), calls=%async_computation | async-start | bytes 4194304 | tf_op jit(solution)/shard_map/all_to_all | solution.py:200
  36.2 2.0 %copy.38 = f32[4,256,128]{1,2,0:T(8,128)} copy(f32[4,256,128]{2,1,0:T(8,128)} %bitcast.64) | data formatting | bytes 1048576 | tf_op jit(solution)/shard_map/mul | solution.py:68
  38.3 2.1 %copy.39 = f32[4,256,128]{1,2,0:T(8,128)} copy(f32[4,256,128]{2,1,0:T(8,128)} %bitcast.62) | data formatting | bytes 1048576 | tf_op jit(solution)/shard_map/mul | solution.py:68
  42.4 3.9 %fusion.5 = f32[4,256,128]{1,2,0:T(8,128)} fusion(f32[4,256,128]{1,2,0:T(8,128)} %copy.40, f32[4,256,128]{1,2,0:T(8,128)} %copy.39, f32[4,256,128]{1,2,0:T(8,128)} %copy.38, f32[4,256,128]{1,2,0:T(8,128)} %copy.37, bf16[4,256,128]{2,1,0:T(8,128)(2,1)S(1)} %bitcast.59, bf16[4,256,128]{1,2,0:T(8,128)(2,1)} %copy.35, s32[256]{0:T(256)S(1)} %get-tuple-element.35, ...), kind=kOutput, calls=%fused_computation.7 | convolution fusion | flops 409600000 | bytes 3147776 | tf_op jit(solution)/shard_map/pq,zqb->zpb/dot_general | solution.py:63
  46.2 2.0 %copy.41 = f32[4,256,128]{2,1,0:T(8,128)} copy(f32[4,256,128]{1,2,0:T(8,128)} %fusion.5) | data formatting | bytes 1048576 | tf_op jit(solution)/shard_map/mul | solution.py:69
  48.3 2.1 %fusion.16.local_ref = f32[1024,128]{1,0:T(8,128)} fusion(f32[4,256,128]{2,1,0:T(8,128)} %copy.41, f32[1024]{0:T(1024)S(1)} %dynamic_slice.30, bf16[2048,256]{1,0:T(8,128)(2,1)S(1)} %copy-done.1, s32[]{:T(128)S(6)} %select_n.167, s32[]{:T(128)S(6)} %select_n.168), kind=kLoop, calls=%fused_computation.43 | loop fusion | flops 393216 | bytes 1314824 | tf_op jit(solution)/shard_map/add | solution.py:69
  50.3 5.6 %all-to-all-done.got_ref = bf16[16,256,256]{2,1,0:T(8,128)(2,1)S(1)} async-done(((bf16[16,256,256]{2,1,0:T(8,128)(2,1)}), bf16[16,256,256]{2,1,0:T(8,128)(2,1)S(1)}, u32[]{:S(2)}, u32[]{:S(2)}) %all-to-all-start) | async-done | bytes 2097184 | tf_op jit(solution)/shard_map/all_to_all | solution.py:200
  57.3 15.8 %first_apply.1 = (bf16[2048,2048]{1,0:T(8,128)(2,1)}, f32[2048,128]{1,0:T(8,128)}, bf16[2048,128]{1,0:T(8,128)(2,1)}, bf16[256,256]{1,0:T(8,128)(2,1)}) custom-call(s32[18]{0:T(128)} %pad_add_fusion.base_ref, s32[16,256]{1,0:T(8,128)} %add_select_fusion.2.where_ref, bf16[16,256,256]{2,1,0:T(8,128)(2,1)} %copy-done.3, bf16[2048,256]{1,0:T(8,128)(2,1)} %orb_ref.1, ...), custom_call_target="tpu_custom_call" | custom-call | tf_op jit(solution)/shard_map/first_apply/pallas_call | solution.py:138
  73.1 6.1 %all-to-all-start.1 = ((bf16[4,64,256]{2,1,0:T(8,128)(2,1)}), bf16[4,64,256]{2,1,0:T(8,128)(2,1)S(1)}, u32[]{:S(2)}, u32[]{:S(2)}) async-start(bf16[4,64,256]{2,1,0:T(8,128)(2,1)} %bitcast.68), calls=%async_computation.1 | async-start | bytes 262144 | tf_op jit(solution)/shard_map/all_to_all | solution.py:244
  79.4 3.4 %all-to-all-done.1 = bf16[4,64,256]{2,1,0:T(8,128)(2,1)S(1)} async-done(((bf16[4,64,256]{2,1,0:T(8,128)(2,1)}), bf16[4,64,256]{2,1,0:T(8,128)(2,1)S(1)}, u32[]{:S(2)}, u32[]{:S(2)}) %all-to-all-start.1) | async-done | bytes 131104 | tf_op jit(solution)/shard_map/all_to_all | solution.py:244
  83.3 4.0 %collective-permute-start.9 = (bf16[64,256]{1,0:T(8,128)(2,1)S(1)}, bf16[64,256]{1,0:T(8,128)(2,1)S(1)}, u32[]{:S(2)}, u32[]{:S(2)}) collective-permute-start(bf16[64,256]{1,0:T(8,128)(2,1)S(1)} %multiply_convert_fusion), channel_id=1, source_target_pairs={{0,8},{4,12},{8,0},{12,4},{16,24},{20,28},{24,16},{28,20},{32,40},... | collective-permute-start | bytes 98312 | tf_op jit(solution)/shard_map/ppermute | solution.py:197
  92.8 3.9 %all-to-all-start.2 = ((bf16[16,256,256]{2,1,0:T(8,128)(2,1)}), bf16[16,256,256]{2,1,0:T(8,128)(2,1)S(1)}, u32[]{:S(2)}, u32[]{:S(2)}) async-start(bf16[16,256,256]{2,1,0:T(8,128)(2,1)} %broadcast_in_dim.38), calls=%async_computation.2 | async-start | bytes 4194304 | tf_op jit(solution)/shard_map/all_to_all | solution.py:200
  99.8 4.9 %collective-permute-done.5 = bf16[1024,128]{1,0:T(8,128)(2,1)S(1)} collective-permute-done((bf16[1024,128]{1,0:T(8,128)(2,1)S(1)}, bf16[1024,128]{1,0:T(8,128)(2,1)S(1)}, u32[]{:S(2)}, u32[]{:S(2)}) %collective-permute-start.5) | collective-permute-done | bytes 262176 | tf_op jit(solution)/shard_map/ppermute | solution.py:252
  105.9 5.7 %collective-permute-start.6 = (bf16[1024,128]{1,0:T(8,128)(2,1)S(1)}, bf16[1024,128]{1,0:T(8,128)(2,1)}, u32[]{:S(2)}, u32[]{:S(2)}) collective-permute-start(bf16[1024,128]{1,0:T(8,128)(2,1)S(1)} %fusion.19), channel_id=1, source_target_pairs={{2,4},{3,5},{6,8},{7,9},{10,12},{11,13},{14,16},{15,17},{18,20},{1... | collective-permute-start | bytes 786440 | tf_op jit(solution)/shard_map/ppermute | solution.py:235
  112.5 5.8 %collective-permute-done.6 = bf16[1024,128]{1,0:T(8,128)(2,1)} collective-permute-done((bf16[1024,128]{1,0:T(8,128)(2,1)S(1)}, bf16[1024,128]{1,0:T(8,128)(2,1)}, u32[]{:S(2)}, u32[]{:S(2)}) %collective-permute-start.6) | collective-permute-done | bytes 262176 | tf_op jit(solution)/shard_map/ppermute | solution.py:235
  120.1 10.4 %all-to-all-done.2.got_ref = bf16[16,256,256]{2,1,0:T(8,128)(2,1)S(1)} async-done(((bf16[16,256,256]{2,1,0:T(8,128)(2,1)}), bf16[16,256,256]{2,1,0:T(8,128)(2,1)S(1)}, u32[]{:S(2)}, u32[]{:S(2)}) %all-to-all-start.2) | async-done | bytes 2097184 | tf_op jit(solution)/shard_map/all_to_all | solution.py:200
  131.9 10.9 %second_apply.1 = (f32[2048,128]{1,0:T(8,128)}, bf16[2048,128]{1,0:T(8,128)(2,1)}) custom-call(s32[18]{0:T(128)} %pad_add_fusion.base_ref, s32[16,256]{1,0:T(8,128)} %add_select_fusion.2.where_ref, bf16[16,256,256]{2,1,0:T(8,128)(2,1)} %copy-done.4, bf16[2048,2048]{1,0:T(8,128)(2,1)} %get-tuple-element.14.kern_ref), custom_call_target="tpu_custom_call" | custom-call | tf_op jit(solution)/shard_map/second_apply/pallas_call | solution.py:182
  153.3 6.4 %collective-permute-done.12 = bf16[1024,128]{1,0:T(8,128)(2,1)} collective-permute-done((bf16[1024,128]{1,0:T(8,128)(2,1)}, bf16[1024,128]{1,0:T(8,128)(2,1)}, u32[]{:S(2)}, u32[]{:S(2)}) %collective-permute-start.12) | collective-permute-done | bytes 262176 | tf_op jit(solution)/shard_map/ppermute | solution.py:252
  161.4 6.7 %collective-permute-done.13 = bf16[1024,128]{1,0:T(8,128)(2,1)S(1)} collective-permute-done((bf16[1024,128]{1,0:T(8,128)(2,1)S(1)}, bf16[1024,128]{1,0:T(8,128)(2,1)S(1)}, u32[]{:S(2)}, u32[]{:S(2)}) %collective-permute-start.13) | collective-permute-done | bytes 262176 | tf_op jit(solution)/shard_map/ppermute | solution.py:262
  (110 shorter events, 49.1 us)
Async XLA Ops:
  0.0 20.2 %copy-start = (s32[4,64]{1,0:T(4,128)S(1)}, s32[4,64]{1,0:T(4,128)}, u32[]{:S(2)}) copy-start(s32[4,64]{1,0:T(4,128)} %param.9) | copy-start | bytes 3076
  3.6 17.2 %collective-permute-start.3 = (bf16[64,256]{1,0:T(8,128)(2,1)}, bf16[64,256]{1,0:T(8,128)(2,1)S(1)}, u32[]{:S(2)}, u32[]{:S(2)}) collective-permute-start(bf16[64,256]{1,0:T(8,128)(2,1)} %pick_rows.1), channel_id=1, source_target_pairs={{0,4},{4,8},{8,12},{12,0},{16,20},{20,24},{24,28},{28,16},{32,36},... | collective-permute-start | bytes 98312 | tf_op jit(solution)/shard_map/ppermute | solution.py:197
  7.4 13.4 %collective-permute-start.2 = (bf16[64,256]{1,0:T(8,128)(2,1)}, bf16[64,256]{1,0:T(8,128)(2,1)S(1)}, u32[]{:S(2)}, u32[]{:S(2)}) collective-permute-start(bf16[64,256]{1,0:T(8,128)(2,1)} %pick_rows.1), channel_id=1, source_target_pairs={{0,8},{4,12},{8,0},{12,4},{16,24},{20,28},{24,16},{28,20},{32,40},... | collective-permute-start | bytes 98312 | tf_op jit(solution)/shard_map/ppermute | solution.py:197
  12.5 8.3 %collective-permute-start.1 = (bf16[64,256]{1,0:T(8,128)(2,1)}, bf16[64,256]{1,0:T(8,128)(2,1)S(1)}, u32[]{:S(2)}, u32[]{:S(2)}) collective-permute-start(bf16[64,256]{1,0:T(8,128)(2,1)} %pick_rows.1), channel_id=1, source_target_pairs={{0,12},{4,0},{8,4},{12,8},{16,28},{20,16},{24,20},{28,24},{32,44},... | collective-permute-start | bytes 98312 | tf_op jit(solution)/shard_map/ppermute | solution.py:197
  15.9 15.8 %collective-permute-start = (bf16[1024,128]{1,0:T(8,128)(2,1)S(1)}, bf16[1024,128]{1,0:T(8,128)(2,1)}, u32[]{:S(2)}, u32[]{:S(2)}) collective-permute-start(bf16[1024,128]{1,0:T(8,128)(2,1)S(1)} %dynamic_slice.28), channel_id=1, source_target_pairs={{2,4},{3,5},{6,8},{7,9},{10,12},{11,13},{14,16},{15,17},{18,20},{1... | collective-permute-start | bytes 786440 | tf_op jit(solution)/shard_map/ppermute | solution.py:235
  23.1 5.7 %copy-start.14 = (f32[2048]{0:T(1024)S(1)}, f32[2048]{0:T(1024)}, u32[]{:S(2)}) copy-start(f32[2048]{0:T(1024)} %param.6) | copy-start | bytes 24580
  23.1 8.5 %copy-start.1 = (bf16[2048,256]{1,0:T(8,128)(2,1)S(1)}, bf16[2048,256]{1,0:T(8,128)(2,1)}, u32[]{:S(2)}) copy-start(bf16[2048,256]{1,0:T(8,128)(2,1)} %orb_ref.1) | copy-start | bytes 3145732
  23.1 32.8 %all-to-all-start = ((bf16[16,256,256]{2,1,0:T(8,128)(2,1)}), bf16[16,256,256]{2,1,0:T(8,128)(2,1)S(1)}, u32[]{:S(2)}, u32[]{:S(2)}) async-start(bf16[16,256,256]{2,1,0:T(8,128)(2,1)} %broadcast_in_dim.37), calls=%async_computation | async-start | bytes 4194304 | tf_op jit(solution)/shard_map/all_to_all | solution.py:200
  50.3 32.5 %copy-start.12 = (bf16[64,256]{1,0:T(8,128)(2,1)S(1)}, bf16[64,256]{1,0:T(8,128)(2,1)}, u32[]{:S(2)}) copy-start(bf16[64,256]{1,0:T(8,128)(2,1)} %pick_rows.1) | copy-start | bytes 98308
  73.1 9.7 %all-to-all-start.1 = ((bf16[4,64,256]{2,1,0:T(8,128)(2,1)}), bf16[4,64,256]{2,1,0:T(8,128)(2,1)S(1)}, u32[]{:S(2)}, u32[]{:S(2)}) async-start(bf16[4,64,256]{2,1,0:T(8,128)(2,1)} %bitcast.68), calls=%async_computation.1 | async-start | bytes 262144 | tf_op jit(solution)/shard_map/all_to_all | solution.py:244
  79.3 17.5 %collective-permute-start.4 = (bf16[2048,128]{1,0:T(8,128)(2,1)}, bf16[2048,128]{1,0:T(8,128)(2,1)S(1)}, u32[]{:S(2)}, u32[]{:S(2)}) collective-permute-start(bf16[2048,128]{1,0:T(8,128)(2,1)} %get-tuple-element.12), channel_id=1, source_target_pairs={{0,1},{1,0},{2,3},{3,2},{4,5},{5,4},{6,7},{7,6},{8,9},{9,8},{10,11... | collective-permute-start | bytes 1572872 | tf_op jit(solution)/shard_map/ppermute | solution.py:250
  82.9 5.4 %collective-permute-start.10 = (bf16[64,256]{1,0:T(8,128)(2,1)S(1)}, bf16[64,256]{1,0:T(8,128)(2,1)S(1)}, u32[]{:S(2)}, u32[]{:S(2)}) collective-permute-start(bf16[64,256]{1,0:T(8,128)(2,1)S(1)} %multiply_convert_fusion), channel_id=1, source_target_pairs={{0,4},{4,8},{8,12},{12,0},{16,20},{20,24},{24,28},{28,16},{32,36},... | collective-permute-start | bytes 98312 | tf_op jit(solution)/shard_map/ppermute | solution.py:197
  83.3 6.9 %collective-permute-start.9 = (bf16[64,256]{1,0:T(8,128)(2,1)S(1)}, bf16[64,256]{1,0:T(8,128)(2,1)S(1)}, u32[]{:S(2)}, u32[]{:S(2)}) collective-permute-start(bf16[64,256]{1,0:T(8,128)(2,1)S(1)} %multiply_convert_fusion), channel_id=1, source_target_pairs={{0,8},{4,12},{8,0},{12,4},{16,24},{20,28},{24,16},{28,20},{32,40},... | collective-permute-start | bytes 98312 | tf_op jit(solution)/shard_map/ppermute | solution.py:197
  87.3 4.0 %collective-permute-start.8 = (bf16[64,256]{1,0:T(8,128)(2,1)S(1)}, bf16[64,256]{1,0:T(8,128)(2,1)S(1)}, u32[]{:S(2)}, u32[]{:S(2)}) collective-permute-start(bf16[64,256]{1,0:T(8,128)(2,1)S(1)} %multiply_convert_fusion), channel_id=1, source_target_pairs={{0,12},{4,0},{8,4},{12,8},{16,28},{20,16},{24,20},{28,24},{32,44},... | collective-permute-start | bytes 98312 | tf_op jit(solution)/shard_map/ppermute | solution.py:197
  92.8 37.7 %all-to-all-start.2 = ((bf16[16,256,256]{2,1,0:T(8,128)(2,1)}), bf16[16,256,256]{2,1,0:T(8,128)(2,1)S(1)}, u32[]{:S(2)}, u32[]{:S(2)}) async-start(bf16[16,256,256]{2,1,0:T(8,128)(2,1)} %broadcast_in_dim.38), calls=%async_computation.2 | async-start | bytes 4194304 | tf_op jit(solution)/shard_map/all_to_all | solution.py:200
  97.5 7.2 %copy-start.2 = (bf16[2048,256]{1,0:T(8,128)(2,1)S(1)}, bf16[2048,256]{1,0:T(8,128)(2,1)}, u32[]{:S(2)}) copy-start(bf16[2048,256]{1,0:T(8,128)(2,1)} %orb_ref.1) | copy-start | bytes 3145732
  97.5 7.2 %copy-start.5 = (f32[1024,128]{1,0:T(8,128)S(1)}, f32[1024,128]{1,0:T(8,128)}, u32[]{:S(2)}) copy-start(f32[1024,128]{1,0:T(8,128)} %fusion.16.local_ref) | copy-start | bytes 1572868
  99.2 5.6 %collective-permute-start.5 = (bf16[1024,128]{1,0:T(8,128)(2,1)S(1)}, bf16[1024,128]{1,0:T(8,128)(2,1)S(1)}, u32[]{:S(2)}, u32[]{:S(2)}) collective-permute-start(bf16[1024,128]{1,0:T(8,128)(2,1)S(1)} %dynamic-slice_convert_fusion.1), channel_id=1, source_target_pairs={{0,2},{1,3},{2,0},{3,1},{4,6},{5,7},{6,4},{7,5},{8,10},{9,11},{10,... | collective-permute-start | bytes 786440 | tf_op jit(solution)/shard_map/ppermute | solution.py:252
  104.9 7.6 %collective-permute-start.7 = (bf16[1024,128]{1,0:T(8,128)(2,1)S(1)}, bf16[1024,128]{1,0:T(8,128)(2,1)}, u32[]{:S(2)}, u32[]{:S(2)}) collective-permute-start(bf16[1024,128]{1,0:T(8,128)(2,1)S(1)} %fusion.19), channel_id=1, source_target_pairs={{0,2},{1,3},{2,0},{3,1},{4,6},{5,7},{6,4},{7,5},{8,10},{9,11},{10,... | collective-permute-start | bytes 786440 | tf_op jit(solution)/shard_map/ppermute | solution.py:256
  105.9 12.4 %collective-permute-start.6 = (bf16[1024,128]{1,0:T(8,128)(2,1)S(1)}, bf16[1024,128]{1,0:T(8,128)(2,1)}, u32[]{:S(2)}, u32[]{:S(2)}) collective-permute-start(bf16[1024,128]{1,0:T(8,128)(2,1)S(1)} %fusion.19), channel_id=1, source_target_pairs={{2,4},{3,5},{6,8},{7,9},{10,12},{11,13},{14,16},{15,17},{18,20},{1... | collective-permute-start | bytes 786440 | tf_op jit(solution)/shard_map/ppermute | solution.py:235
  142.8 6.6 %collective-permute-start.11 = (bf16[2048,128]{1,0:T(8,128)(2,1)}, bf16[2048,128]{1,0:T(8,128)(2,1)}, u32[]{:S(2)}, u32[]{:S(2)}) collective-permute-start(bf16[2048,128]{1,0:T(8,128)(2,1)} %get-tuple-element.16), channel_id=1, source_target_pairs={{0,1},{1,0},{2,3},{3,2},{4,5},{5,4},{6,7},{7,6},{8,9},{9,8},{10,11... | collective-permute-start | bytes 1572872 | tf_op jit(solution)/shard_map/ppermute | solution.py:250
  151.6 8.2 %collective-permute-start.12 = (bf16[1024,128]{1,0:T(8,128)(2,1)}, bf16[1024,128]{1,0:T(8,128)(2,1)}, u32[]{:S(2)}, u32[]{:S(2)}) collective-permute-start(bf16[1024,128]{1,0:T(8,128)(2,1)} %dynamic-slice_convert_fusion), channel_id=1, source_target_pairs={{0,2},{1,3},{2,0},{3,1},{4,6},{5,7},{6,4},{7,5},{8,10},{9,11},{10,... | collective-permute-start | bytes 786440 | tf_op jit(solution)/shard_map/ppermute | solution.py:252
  161.0 7.1 %collective-permute-start.13 = (bf16[1024,128]{1,0:T(8,128)(2,1)S(1)}, bf16[1024,128]{1,0:T(8,128)(2,1)S(1)}, u32[]{:S(2)}, u32[]{:S(2)}) collective-permute-start(bf16[1024,128]{1,0:T(8,128)(2,1)S(1)} %fusion.20), channel_id=1, source_target_pairs={{0,2},{1,3},{2,0},{3,1},{4,6},{5,7},{6,4},{7,5},{8,10},{9,11},{10,... | collective-permute-start | bytes 786440 | tf_op jit(solution)/shard_map/ppermute | solution.py:262
  168.2 3.3 %collective-permute-start.14 = (bf16[2048,128]{1,0:T(8,128)(2,1)S(1)}, bf16[2048,128]{1,0:T(8,128)(2,1)S(1)}, u32[]{:S(2)}, u32[]{:S(2)}) collective-permute-start(bf16[2048,128]{1,0:T(8,128)(2,1)S(1)} %pad_maximum_fusion.1), channel_id=1, source_target_pairs={{0,1},{1,0},{2,3},{3,2},{4,5},{5,4},{6,7},{7,6},{8,9},{9,8},{10,11... | collective-permute-start | bytes 1572872 | tf_op jit(solution)/shard_map/ppermute | solution.py:264
  (10 other events, 21.1 us)

commit v2 on v0

v2 whole, which is shorter than its diff:
```python
import jax
import jax.numpy as jnp
import numpy as np
from jax import lax
from jax.experimental import pallas as pl
from jax.experimental.pallas import tpu as pltpu
from jax.sharding import PartitionSpec as P


NB = 256
HALF = 128
NY = 8
NX = 32
PLANE = NY * NX
ROWS = 2048
SHARE = 1024
PTS = 2048
CAP = 64
ALL = 4 * CAP
WIN = 272
TILE = 256
BF = jnp.bfloat16
F32 = jnp.float32

stencil_coef = (-205.0 / 72.0, 8.0 / 5.0, -1.0 / 5.0, 8.0 / 315.0, -1.0 / 560.0)


def slab_id(y, x, z):
    return ((y % 4) * 4 + (x % 4)) * 4 + (z % 4)


def z_shift(d):
    return [(slab_id(y, x, z), slab_id(y, x, z - d)) for y in range(4) for x in range(4) for z in range(4)]


def plane_shift(d, second):
    pairs = []
    for y in range(4):
        for x in range(4):
            for z in range(4):
                for p in range(4):
                    along_x = (p % 2 == 0) != second
                    target = slab_id(y, x - d, z) if along_x else slab_id(y - d, x, z)
                    pairs.append((slab_id(y, x, z) * 4 + p, target * 4 + p))
    return pairs


BOTH = ("slab", "pt")
CORE_SWAP = [(i, i ^ 1) for i in range(4)]
CHIP_SWAP = [(i, i ^ 2) for i in range(4)]
EDGE_SWAP = [(s * 4 + 2 + c, ((s + 1) % 64) * 4 + c) for s in range(64) for c in range(2)] + [
    (s * 4 + c, ((s - 1) % 64) * 4 + 2 + c) for s in range(64) for c in range(2)
]


def plane_table():
    cell_ids = np.arange(PLANE)
    row_y = cell_ids // NX
    col_x = cell_ids % NX
    diff_y = (row_y[:, None] - row_y[None, :]) % NY
    diff_x = (col_x[:, None] - col_x[None, :]) % NX
    same_y = row_y[:, None] == row_y[None, :]
    same_x = col_x[:, None] == col_x[None, :]
    table = np.zeros((PLANE, PLANE), np.float32)
    for offset in range(1, 5):
        coef = np.float32(stencil_coef[offset])
        table += coef * (same_y & (diff_x == offset % NX)) + coef * (same_y & (diff_x == -offset % NX))
        table += coef * (same_x & (diff_y == offset % NY)) + coef * (same_x & (diff_y == -offset % NY))
    return table


def split_table():
    table = jnp.asarray(plane_table())
    high = table.astype(BF)
    low = (table - high.astype(F32)).astype(BF)
    return jnp.concatenate([high, low], axis=0)


VMEM = pl.BlockSpec(memory_space=pltpu.VMEM)


def near(value):
    return pltpu.with_memory_space_constraint(value, pltpu.VMEM)


def call(kernel, scalars, args, specs, out_shape, out_specs=None, grid=(1,), scratch=(), aliases=None):
    if out_specs is None:
        out_specs = [VMEM] * len(out_shape)
    args = [near(a) if spec is VMEM else a for a, spec in zip(args, specs)]
    out_shape = [pltpu.VMEM(o.shape, o.dtype) if spec is VMEM else o for o, spec in zip(out_shape, out_specs)]
    return pl.pallas_call(
        kernel,
        grid_spec=pltpu.PrefetchScalarGridSpec(
            num_scalar_prefetch=1, grid=grid, in_specs=specs, out_specs=out_specs, scratch_shapes=list(scratch)
        ),
        out_shape=out_shape,
        input_output_aliases=aliases or {},
        compiler_params=pltpu.CompilerParams(vmem_limit_bytes=16 << 20),
    )(scalars, *args)


def array(shape, kind):
    return jax.ShapeDtypeStruct(shape, kind)


def as_column(row):
    size = row.shape[1]
    diag = lax.broadcasted_iota(jnp.int32, (size, size), 0) == lax.broadcasted_iota(jnp.int32, (size, size), 1)
    spread = jnp.broadcast_to(row.astype(F32), (size, size))
    return jnp.sum(jnp.where(diag, spread, 0.0), axis=1, keepdims=True).astype(jnp.int32)


def selection(column, start, width):
    lanes = lax.broadcasted_iota(jnp.int32, (column.shape[0], width), 1) + start
    return jnp.where(column == lanes, 1.0, 0.0).astype(BF)


def all_columns(rows_ref):
    return jnp.concatenate([as_column(rows_ref[p]) for p in range(4)], axis=0)


def pick_own_kernel(meta_ref, rows_ref, field_ref, out_ref):
    hot = selection(as_column(rows_ref[0]), 0, ROWS)
    out_ref[...] = jnp.dot(hot, field_ref[...], preferred_element_type=F32).astype(BF)


def pick_own(meta, rows, field):
    return call(
        pick_own_kernel, meta, (rows, field),
        [pl.BlockSpec((1, 1, CAP), lambda i, m: (m[0], 0, 0)), pl.BlockSpec((ROWS, NB), lambda i, m: (0, 0))],
        [array((CAP, NB), BF)],
    )[0]


def pick_all_kernel(meta_ref, rows_ref, field_ref, fit_ref, orb_out, fit_out, hot_ref):
    @pl.when(pl.program_id(0) == 0)
    def _():
        hot_ref[...] = selection(all_columns(rows_ref), 0, ROWS)
        orb_out[...] = jnp.dot(hot_ref[...], field_ref[...], preferred_element_type=F32).astype(BF)

    fit_out[...] = jnp.dot(hot_ref[...], fit_ref[...], preferred_element_type=F32).astype(BF)


def pick_all(meta, rows, field, fit):
    return call(
        pick_all_kernel, meta, (rows, field, fit),
        [VMEM, VMEM, pl.BlockSpec((ROWS, 512), lambda i, m: (0, i))],
        [array((ALL, NB), BF), array((ALL, PTS), BF)],
        [pl.BlockSpec((ALL, NB), lambda i, m: (0, 0)), pl.BlockSpec((ALL, 512), lambda i, m: (0, i))],
        grid=(4,), scratch=[pltpu.VMEM((ALL, ROWS), BF)],
    )


def stencil_kernel(meta_ref, rows_ref, own_ref, inner_ref, outer_ref, pot_ref, table_ref, local_ref, *picked):
    first = meta_ref[2] == 0
    planes = []
    for k in range(4):
        part = pl.ds(k * PLANE, PLANE)
        planes.append(jnp.where(first, outer_ref[part, :], inner_ref[part, :]).astype(F32))
    planes += [own_ref[pl.ds(k * PLANE, PLANE), :].astype(F32) for k in range(4)]
    for k in range(4):
        part = pl.ds(k * PLANE, PLANE)
        planes.append(jnp.where(first, inner_ref[part, :], outer_ref[part, :]).astype(F32))
    for k in range(4):
        part = pl.ds(k * PLANE, PLANE)
        own = own_ref[part, :]
        center = planes[4 + k]
        total = jnp.dot(table_ref[pl.ds(0, PLANE), :], own, preferred_element_type=F32)
        total += jnp.dot(table_ref[pl.ds(PLANE, PLANE), :], own, preferred_element_type=F32)
        total += 3.0 * stencil_coef[0] * center
        for offset in range(1, 5):
            total += stencil_coef[offset] * (planes[4 + k + offset] + planes[4 + k - offset])
        local_ref[part, :] = -0.5 * total + pot_ref[part, :] * center
    if picked:
        hot = selection(all_columns(rows_ref), meta_ref[2] * SHARE, SHARE)
        picked[0][...] = jnp.dot(hot, local_ref[...].astype(BF), preferred_element_type=F32)


def stencil(meta, rows, own, inner, outer, potential, table, with_pick):
    shapes = [array((SHARE, HALF), F32)]
    if with_pick:
        shapes.append(array((ALL, HALF), F32))
    return call(stencil_kernel, meta, (rows, own, inner, outer, potential, table), [VMEM] * 6, shapes)


def place(meta_ref, where_ref, sum_ref, group, rows):
    line = lax.broadcasted_iota(jnp.int32, (WIN, TILE), 0)
    hot = jnp.where(where_ref[group : group + 1, :] == line, 1.0, 0.0).astype(BF)
    at = pl.multiple_of(meta_ref[4 + group], 8)
    sum_ref[pl.ds(at, WIN), :] += jnp.dot(hot, rows, preferred_element_type=F32)


def place_early_kernel(meta_ref, where_ref, line_ref, up_ref, down_ref, sum_ref):
    sum_ref[...] = jnp.zeros_like(sum_ref)
    for part, ref in ((0, line_ref), (1, up_ref), (3, down_ref)):
        for e in range(4):
            place(meta_ref, where_ref, sum_ref, part * 4 + e, ref[pl.ds(e * TILE, TILE), :])


def place_early(meta, where, line, up, down):
    return call(place_early_kernel, meta, (where, line, up, down), [VMEM] * 4, [array((PTS + WIN, NB), F32)])[0]


def place_late(meta_ref, where_ref, left_ref, right_ref, sum_ref, psi_ref):
    for e in range(4):
        ref = left_ref if e < 2 else right_ref
        place(meta_ref, where_ref, sum_ref, 8 + e, ref[pl.ds((e % 2) * TILE, TILE), :])
    psi_ref[...] = sum_ref[pl.ds(0, PTS), :].astype(BF)


def place_late_kernel(meta_ref, where_ref, left_ref, right_ref, early_ref, sum_ref, psi_ref):
    place_late(meta_ref, where_ref, left_ref, right_ref, sum_ref, psi_ref)


def listed_kernel(meta_ref, where_ref, left_ref, right_ref, early_ref, orb_ref, fit_ref, local_ref,
                  sum_ref, psi_ref, pick_ref):
    place_late(meta_ref, where_ref, left_ref, right_ref, sum_ref, psi_ref)
    density = lax.dot_general(orb_ref[...], psi_ref[...], (((1,), (1,)), ((), ())), preferred_element_type=F32)
    kern = (fit_ref[...].astype(F32) * density).astype(BF)
    part = -jnp.dot(kern, psi_ref[...], preferred_element_type=F32)
    core = meta_ref[1]
    local = local_ref[...]
    pick_ref[:, :HALF] = (part[:, :HALF] + jnp.where(core == 0, local, 0.0)).astype(BF)
    pick_ref[:, HALF:] = (part[:, HALF:] + jnp.where(core == 0, 0.0, local)).astype(BF)


def listed(meta, where, left, right, early, orb, fit, local):
    return call(
        listed_kernel, meta, (where, left, right, early, orb, fit, local), [VMEM] * 7,
        [array((PTS + WIN, NB), F32), array((PTS, NB), BF), array((ALL, NB), BF)], aliases={4: 0},
    )[1:]


def finish_points(meta, where, left, right, early):
    return call(
        place_late_kernel, meta, (where, left, right, early), [VMEM] * 4,
        [array((PTS + WIN, NB), F32), array((PTS, NB), BF)], aliases={4: 0},
    )[1]


def emit(meta_ref, part, keep_ref, send_ref, at):
    core = meta_ref[1]
    left, right = part[:, :HALF], part[:, HALF:]
    keep_ref[at, :] = jnp.where(core == 0, left, right)
    send_ref[at, :] = jnp.where(core == 0, right, left).astype(BF)


def build_kernel(meta_ref, psi_ref, orb_ref, fit_ref, kern_ref, keep_ref, send_ref):
    at = pl.ds(pl.multiple_of(pl.program_id(0) * TILE, TILE), TILE)
    density = lax.dot_general(orb_ref[...], psi_ref[...], (((1,), (1,)), ((), ())), preferred_element_type=F32)
    kern = (fit_ref[...].astype(F32) * density).astype(BF)
    kern_ref[at, :] = kern
    emit(meta_ref, -jnp.dot(kern, psi_ref[...], preferred_element_type=F32), keep_ref, send_ref, at)


def build(meta, psi, orb, fit, away):
    def mapped(i, m):
        return (i + 4 * (1 - m[2] if away else m[2]), 0)

    return call(
        build_kernel, meta, (psi, orb, fit),
        [VMEM, pl.BlockSpec((TILE, NB), mapped), pl.BlockSpec((TILE, PTS), mapped)],
        [array((SHARE, PTS), BF), array((SHARE, HALF), F32), array((SHARE, HALF), BF)], grid=(4,),
    )


def apply_kernel(meta_ref, psi_ref, kern_ref, keep_ref, send_ref):
    for step in range(4):
        at = pl.ds(step * TILE, TILE)
        part = -jnp.dot(kern_ref[at, :], psi_ref[...], preferred_element_type=F32)
        emit(meta_ref, part, keep_ref, send_ref, at)


def apply(meta, psi, kern):
    return call(
        apply_kernel, meta, (psi, kern), [VMEM, VMEM],
        [array((SHARE, HALF), F32), array((SHARE, HALF), BF)],
    )


def after(value, *earlier):
    return lax.optimization_barrier((value,) + earlier)[0]


def gather_column(own):
    parts = [own] + [lax.ppermute(own, "slab", z_shift(d)) for d in (1, 2, 3)]
    return jnp.concatenate(parts, axis=0)


def gather_line(column):
    parts = [column] + [lax.ppermute(column, BOTH, plane_shift(d, False)) for d in (1, 2, 3)]
    return jnp.concatenate(parts, axis=0)


def gather_sides(line):
    return (lax.ppermute(line, BOTH, plane_shift(1, True)), lax.ppermute(line, BOTH, plane_shift(-1, True)))


def gather_far(up, down):
    left = lax.ppermute(up[: 2 * TILE], BOTH, plane_shift(1, True))
    right = lax.ppermute(down[2 * TILE :], BOTH, plane_shift(-1, True))
    return left, right


def body(orbitals, potential, fit_matrix, owner_rows, owner_count):
    point_block = lax.axis_index("pt")
    slab = lax.axis_index("slab")
    core = point_block % 2
    chip = point_block // 2
    my_z = slab % 4
    my_x = (slab // 4) % 4
    my_y = slab // 16

    counts = lax.dynamic_index_in_dim(owner_count, point_block, 0, keepdims=False)
    four = jnp.arange(4, dtype=jnp.int32)
    outer_step = four[:, None, None]
    inner_step = four[None, :, None]
    y_id = jnp.where(core == 0, my_y + outer_step, my_y + inner_step) % 4
    x_id = jnp.where(core == 0, my_x + inner_step, my_x + outer_step) % 4
    z_id = (my_z + four[None, None, :]) % 4
    column_id = y_id * 4 + x_id
    slabs = (column_id * 4 + z_id).reshape(16, 4)
    first = (column_id * 4).reshape(16)
    every = jnp.arange(64, dtype=jnp.int32)
    start = jnp.sum(jnp.where(every < slabs[:, :, None], counts, 0), axis=2)
    size = jnp.sum(jnp.where(every == slabs[:, :, None], counts, 0), axis=2)
    base = jnp.sum(jnp.where(every[None, :] < first[:, None], counts, 0), axis=1) // 8 * 8
    slot = jnp.arange(CAP, dtype=jnp.int32)
    where = jnp.where(slot < size[:, :, None], start[:, :, None] - base[:, None, None] + slot, -1).reshape(16, TILE)
    ids = jnp.stack([point_block, core, chip, slab]).astype(jnp.int32)
    meta = jnp.concatenate([ids, base.astype(jnp.int32)])
    table = split_table()
    row0 = chip * SHARE

    own0 = pick_own(ids, owner_rows, orbitals)
    column0 = gather_column(own0)
    line0 = gather_line(column0)
    up0, down0 = gather_sides(line0)
    left0, right0 = gather_far(up0, down0)

    field0 = lax.dynamic_slice(orbitals, (row0, core * HALF), (SHARE, HALF))
    inner0 = lax.dynamic_slice(orbitals, (SHARE - row0, core * HALF), (SHARE, HALF))
    potential_piece = lax.dynamic_slice(potential, (row0,), (SHARE,)).reshape(SHARE, 1)
    outer0 = lax.ppermute(after(field0, column0), BOTH, EDGE_SWAP)
    orb_listed, fit_listed = pick_all(ids, after(owner_rows, column0), orbitals, fit_matrix)
    local0, local_listed = stencil(ids, owner_rows, field0, inner0, outer0, potential_piece, table, True)

    early0 = place_early(meta, where, line0, up0, down0)
    psi0, picked = listed(meta, where, left0, right0, early0, orb_listed, fit_listed, local_listed)

    pieces = lax.all_to_all(picked.reshape(4, CAP, NB), "pt", 0, 0)
    applied = jnp.sum(pieces.astype(F32), axis=0)
    own1 = ((applied - 3.5 * own0.astype(F32)) / 4.0).astype(BF)
    column1 = gather_column(own1)
    line1 = gather_line(column1)
    up1, down1 = gather_sides(line1)
    left1, right1 = gather_far(up1, down1)

    def send_away(keep, gone):
        total = keep + lax.ppermute(gone, "pt", CORE_SWAP).astype(F32)
        return lax.ppermute(total.astype(BF), "pt", CHIP_SWAP)

    def join_own(keep, gone, away):
        return keep + lax.ppermute(gone, "pt", CORE_SWAP).astype(F32) + away.astype(F32)

    kern_away, keep, gone = build(meta, after(psi0, own1), orbitals, fit_matrix, True)
    away = send_away(keep, gone)
    kern_own, keep, gone = build(meta, after(psi0, column1), orbitals, fit_matrix, False)
    applied0 = local0 + join_own(keep, gone, away)
    field1 = ((applied0 - 3.5 * field0.astype(F32)) / 4.0).astype(BF)
    inner1 = lax.ppermute(field1, "pt", CHIP_SWAP)
    outer1 = lax.ppermute(field1, BOTH, EDGE_SWAP)
    local1 = stencil(ids, owner_rows, field1, inner1, outer1, potential_piece, table, False)[0]

    early1 = place_early(meta, where, line1, up1, down1)
    psi1 = finish_points(meta, where, left1, right1, early1)
    keep, gone = apply(meta, psi1, kern_away)
    away = send_away(keep, gone)
    keep, gone = apply(meta, after(psi1, keep), kern_own)
    applied1 = local1 + join_own(keep, gone, away)
    field2 = (0.5 * (applied1 - 3.5 * field1.astype(F32)) - field0.astype(F32)).astype(BF)

    other = lax.ppermute(field2, "pt", CHIP_SWAP)
    column = jnp.concatenate([jnp.where(chip == 0, field2, other), jnp.where(chip == 0, other, field2)], axis=0)
    other = lax.ppermute(column, "pt", CORE_SWAP)
    return jnp.concatenate([jnp.where(core == 0, column, other), jnp.where(core == 0, other, column)], axis=1)


def solution(mesh):
    placed = (P("slab", None), P("slab"), P("slab", "pt"), P(None, "slab", None), P())
    return jax.shard_map(body, mesh=mesh, in_specs=placed, out_specs=P("slab", None), check_vma=False)
```

time: 369 us -> 145 us (0.39)
  waiting for transfers between devices: 267 us -> 50.1 us
  starting transfers between devices: 16.1 us -> 44.1 us
  local copies, waits for them, and re-layouts: 36.2 us -> 8.35 us
  Pallas kernels: 0 us -> 27.7 us
  matrix products: 27 us -> 0 us
  between operations: 13.2 us -> 0.44 us
  blocking collectives: 0 us -> 11.2 us
  other arithmetic: 9.22 us -> 2.62 us
    all_gather x2 -> x0, waiting for transfers between devices: 143 us -> none  [gather_points(): gathered = lax.all_gather(picked, 'slab', axis=0, tiled=True)]
    psum x2 -> x0, waiting for transfers between devices: 93.5 us -> none  [apply_whole(): exch_term = lax.psum(partial_value, 'pt')]
    ppermute x4 -> x31, starting transfers between devices: 15.7 us -> 44.1 us  [the longest x6 12.6 us: gather_column(): parts = [own] + [lax.ppermute(own, 'slab', z_shift(d)) for d in (1, 2, 3)]]
    pallas_call x0 -> x12, Pallas kernels: none -> 27.7 us  [call(): pl.pallas_call(kernel, grid_spec=pltpu.PrefetchScalarGridSpec(num_scalar_...]
    dot_general x5 -> x0, matrix products: 27 us -> none  [the longest x2 11.7 us: apply_whole(): jnp.dot(kernel, field_points, preferred_element_type=jnp.float32)]
    gather x4 -> x0, local copies, waits for them, and re-layouts: 19.7 us -> none  [the longest x2 17 us: gather_points(): return jnp.take(gathered, positions, axis=0)]
    ppermute x4 -> x31, waiting for transfers between devices: 30.4 us -> 50.1 us  [the longest x6 11.3 us: gather_line(): lax.ppermute(column, BOTH, plane_shift(d, False))]
    all_to_all x0 -> x1, blocking collectives: none -> 11.2 us  [body(): pieces = lax.all_to_all(picked.reshape(4, CAP, NB), 'pt', 0, 0)]
  transfers between devices with their start and end apart: 8 -> 31, of which waited for: 8 -> 18; matrix products, arithmetic and copies ran while one was open for 7% -> 3% of each run, Pallas kernels for 0% -> 17%
where the time goes in v2:
time: 145 us
  waiting for transfers between devices  50.1 us (35%)
  starting transfers between devices  44.1 us (30%)
  Pallas kernels  27.7 us (19%)
  blocking collectives  11.2 us (8%)
  local copies, waits for them, and re-layouts  8.35 us (6%)
  other arithmetic  2.62 us (2%)
    pallas_call x12, Pallas kernels, call(): pl.pallas_call(kernel, grid_spec=pltpu.PrefetchScalarGridSpec(num_scalar_...  27.7 us
    ppermute x6, starting transfers between devices, gather_column(): parts = [own] + [lax.ppermute(own, 'slab', z_shift(d)) for d in (1, 2, 3)]  12.6 us
    ppermute x6, waiting for transfers between devices, gather_line(): lax.ppermute(column, BOTH, plane_shift(d, False))  11.3 us
    all_to_all x1, blocking collectives, body(): pieces = lax.all_to_all(picked.reshape(4, CAP, NB), 'pt', 0, 0)  11.2 us
    ppermute x2, waiting for transfers between devices, gather_sides(): lax.ppermute(line, BOTH, plane_shift(-1, True))  11.2 us
    ppermute x6, waiting for transfers between devices, gather_column(): parts = [own] + [lax.ppermute(own, 'slab', z_shift(d)) for d in (1, 2, 3)]  7.92 us
    ppermute x1, waiting for transfers between devices, body(): other = lax.ppermute(field2, 'pt', CHIP_SWAP)  6.7 us
    ppermute x1, waiting for transfers between devices, body(): outer1 = lax.ppermute(field1, BOTH, EDGE_SWAP)  5.53 us
  transfers between devices with their start and end apart: 31, of which 18 were waited for; matrix products, arithmetic and copies ran while one was open for 3% of the time, Pallas kernels for 17%

profile of v2, /device:TPU:1, one launch (start us, length us, event | category | flops | bytes accessed | tf_op | source)
XLA Modules:
  0.0 144.6 jit_solution(610730974853990222)
XLA Ops:
  2.9 6.9 %collective-permute-start = (bf16[64,256]{1,0:T(8,128)(2,1)S(1)}, bf16[64,256]{1,0:T(8,128)(2,1)S(1)}, u32[]{:S(2)}, u32[]{:S(2)}) collective-permute-start(bf16[64,256]{1,0:T(8,128)(2,1)S(1)} %shard_map.64), channel_id=1, source_target_pairs={{0,12},{4,0},{8,4},{12,8},{16,28},{20,16},{24,20},{28,24},{32,44},... | collective-permute-start | bytes 98312 | tf_op jit(solution)/shard_map/ppermute | solution.py:286
  10.8 2.3 %collective-permute-start.2 = (bf16[64,256]{1,0:T(8,128)(2,1)S(1)}, bf16[64,256]{1,0:T(8,128)(2,1)S(1)}, u32[]{:S(2)}, u32[]{:S(2)}) collective-permute-start(bf16[64,256]{1,0:T(8,128)(2,1)S(1)} %shard_map.64), channel_id=1, source_target_pairs={{0,4},{4,8},{8,12},{12,0},{16,20},{20,24},{24,28},{28,16},{32,36},... | collective-permute-start | bytes 98312 | tf_op jit(solution)/shard_map/ppermute | solution.py:286
  13.7 2.8 %collective-permute-done.1 = bf16[64,256]{1,0:T(8,128)(2,1)S(1)} collective-permute-done((bf16[64,256]{1,0:T(8,128)(2,1)S(1)}, bf16[64,256]{1,0:T(8,128)(2,1)S(1)}, u32[]{:S(2)}, u32[]{:S(2)}) %collective-permute-start.1) | collective-permute-done | bytes 32800 | tf_op jit(solution)/shard_map/ppermute | solution.py:286
  16.5 2.8 %collective-permute-start.4 = (bf16[256,256]{1,0:T(8,128)(2,1)S(1)}, bf16[256,256]{1,0:T(8,128)(2,1)S(1)}, u32[]{:S(2)}, u32[]{:S(2)}) collective-permute-start(bf16[256,256]{1,0:T(8,128)(2,1)S(1)} %pad_maximum_fusion.2), channel_id=1, source_target_pairs={{0,48},{1,193},{2,50},{3,195},{4,52},{5,197},{6,54},{7,199},{8,56}... | collective-permute-start | bytes 393224 | tf_op jit(solution)/shard_map/ppermute | solution.py:291
  20.4 2.3 %collective-permute-done.4 = bf16[256,256]{1,0:T(8,128)(2,1)S(1)} collective-permute-done((bf16[256,256]{1,0:T(8,128)(2,1)S(1)}, bf16[256,256]{1,0:T(8,128)(2,1)S(1)}, u32[]{:S(2)}, u32[]{:S(2)}) %collective-permute-start.4) | collective-permute-done | bytes 131104 | tf_op jit(solution)/shard_map/ppermute | solution.py:291
  26.4 2.3 %collective-permute-start.7 = (bf16[1024,256]{1,0:T(8,128)(2,1)S(1)}, bf16[1024,256]{1,0:T(8,128)(2,1)S(1)}, u32[]{:S(2)}, u32[]{:S(2)}) collective-permute-start(bf16[1024,256]{1,0:T(8,128)(2,1)S(1)} %constant_dynamic-update-slice_fusion.line_ref), channel_id=1, source_target_pairs={{0,192},{1,49},{2,194},{3,51},{4,196},{5,53},{6,198},{7,55},{8,200... | collective-permute-start | bytes 1572872 | tf_op jit(solution)/shard_map/ppermute | solution.py:296
  29.2 3.5 %collective-permute-start.3 = (bf16[1024,128]{1,0:T(8,128)(2,1)S(1)}, bf16[1024,128]{1,0:T(8,128)(2,1)}, u32[]{:S(2)}, u32[]{:S(2)}) collective-permute-start(bf16[1024,128]{1,0:T(8,128)(2,1)S(1)} %get-tuple-element.27.own_ref), channel_id=1, source_target_pairs={{2,4},{3,5},{6,8},{7,9},{10,12},{11,13},{14,16},{15,17},{18,20},{1... | collective-permute-start | bytes 786440 | tf_op jit(solution)/shard_map/ppermute | solution.py:344
  32.7 11.2 %collective-permute-done.9.down_ref = bf16[1024,256]{1,0:T(8,128)(2,1)S(1)} collective-permute-done((bf16[1024,256]{1,0:T(8,128)(2,1)S(1)}, bf16[1024,256]{1,0:T(8,128)(2,1)S(1)}, u32[]{:S(2)}, u32[]{:S(2)}) %collective-permute-start.9) | collective-permute-done | bytes 524320 | tf_op jit(solution)/shard_map/ppermute | solution.py:296
  45.4 2.7 %collective-permute-start.8 = (bf16[512,256]{1,0:T(8,128)(2,1)}, bf16[512,256]{1,0:T(8,128)(2,1)}, u32[]{:S(2)}, u32[]{:S(2)}) collective-permute-start(bf16[512,256]{1,0:T(8,128)(2,1)} %slice.16), channel_id=1, source_target_pairs={{0,192},{1,49},{2,194},{3,51},{4,196},{5,53},{6,198},{7,55},{8,200... | collective-permute-start | bytes 786440 | tf_op jit(solution)/shard_map/ppermute | solution.py:300
  49.0 3.4 %copy-done.1 = bf16[2048,2048]{1,0:T(8,128)(2,1)S(1)} copy-done((bf16[2048,2048]{1,0:T(8,128)(2,1)S(1)}, bf16[2048,2048]{1,0:T(8,128)(2,1)}, u32[]{:S(2)}) %copy-start.1) | copy-done | bytes 8388632
  52.4 4.9 %shard_map.67 = (bf16[256,256]{1,0:T(8,128)(2,1)S(1)}, bf16[256,2048]{1,0:T(8,128)(2,1)S(1)}) custom-call(s32[4]{0:T(128)S(1)} %pad_add_fusion.meta_ref, s32[4,1,64]{2,1,0:T(1,128)S(1)} %copy-done.8, bf16[2048,256]{1,0:T(8,128)(2,1)S(1)} %copy-done.3, bf16[2048,2048]{1,0:T(8,128)(2,1)S(1)} %copy-done.1), custom_call_target="tpu_custom_call" | custom-call | tf_op jit(solution)/shard_map/pallas_call | solution.py:91
  57.3 2.7 %shard_map.65 = (f32[1024,128]{1,0:T(8,128)S(1)}, f32[256,128]{1,0:T(8,128)S(1)}) custom-call(s32[4]{0:T(128)S(1)} %pad_add_fusion.meta_ref, s32[4,1,64]{2,1,0:T(1,128)S(1)} %copy-done.8, bf16[1024,128]{1,0:T(8,128)(2,1)S(1)} %get-tuple-element.27.own_ref, bf16[1024,128]{1,0:T(8,128)(2,1)S(1)} %get-tuple-element.55.inner_ref, ...), custom_call_target="tpu_custom_call" | custom-call | tf_op jit(solution)/shard_map/pallas_call | solution.py:91
  61.4 2.8 %shard_map.68 = (f32[2320,256]{1,0:T(8,128)S(1)}, bf16[2048,256]{1,0:T(8,128)(2,1)S(1)}, bf16[256,256]{1,0:T(8,128)(2,1)S(1)}) custom-call(s32[20]{0:T(128)S(1)} %concatenate.29.meta_ref, s32[16,256]{1,0:T(8,128)S(1)} %add_select_fusion.where_ref, bf16[512,256]{1,0:T(8,128)(2,1)} %collective-permute-done.8.left_ref, ...), custom_call_target="tpu_custom_call", output_to_operand_aliasing={{0}: (4, {})} | custom-call | tf_op jit(solution)/shard_map/pallas_call | solution.py:91
  64.2 11.2 %all_to_all.5 = bf16[4,64,256]{2,1,0:T(8,128)(2,1)S(1)} all-to-all(bf16[4,64,256]{2,1,0:T(8,128)(2,1)S(1)} %bitcast.14), channel_id=1, replica_groups=mesh['slab'=64,'pt'=4] {'pt'}, dimensions={0} | all-to-all | bytes 262144 | tf_op jit(solution)/shard_map/all_to_all | solution.py:351
  79.2 3.4 %collective-permute-done.12 = bf16[64,256]{1,0:T(8,128)(2,1)S(1)} collective-permute-done((bf16[64,256]{1,0:T(8,128)(2,1)S(1)}, bf16[64,256]{1,0:T(8,128)(2,1)S(1)}, u32[]{:S(2)}, u32[]{:S(2)}) %collective-permute-start.12) | collective-permute-done | bytes 32800 | tf_op jit(solution)/shard_map/ppermute | solution.py:286
  84.6 2.3 %collective-permute-done.19 = bf16[256,256]{1,0:T(8,128)(2,1)S(1)} collective-permute-done((bf16[256,256]{1,0:T(8,128)(2,1)S(1)}, bf16[256,256]{1,0:T(8,128)(2,1)S(1)}, u32[]{:S(2)}, u32[]{:S(2)}) %collective-permute-start.19) | collective-permute-done | bytes 131104 | tf_op jit(solution)/shard_map/ppermute | solution.py:291
  91.5 4.0 %shard_map.70 = (bf16[1024,2048]{1,0:T(8,128)(2,1)S(1)}, f32[1024,128]{1,0:T(8,128)S(1)}, bf16[1024,128]{1,0:T(8,128)(2,1)S(1)}) custom-call(s32[20]{0:T(128)S(1)} %concatenate.29.meta_ref, bf16[2048,256]{1,0:T(8,128)(2,1)S(1)} %get-tuple-element.35.psi_ref, bf16[2048,256]{1,0:T(8,128)(2,1)S(1)} %copy-done.3, bf16[2048,2048]{1,0:T(8,128)(2,1)S(1)} %bitcast.13), custom_call_target="tpu_custom_call" | custom-call | tf_op jit(solution)/shard_map/pallas_call | solution.py:91
  95.5 5.0 %collective-permute-start.15 = (bf16[1024,128]{1,0:T(8,128)(2,1)S(1)}, bf16[1024,128]{1,0:T(8,128)(2,1)S(1)}, u32[]{:S(2)}, u32[]{:S(2)}) collective-permute-start(bf16[1024,128]{1,0:T(8,128)(2,1)S(1)} %get-tuple-element.40), channel_id=1, source_target_pairs={{0,1},{1,0},{2,3},{3,2},{4,5},{5,4},{6,7},{7,6},{8,9},{9,8},{10,11... | collective-permute-start | bytes 786440 | tf_op jit(solution)/shard_map/ppermute | solution.py:360
  100.5 4.0 %shard_map.69 = (bf16[1024,2048]{1,0:T(8,128)(2,1)S(1)}, f32[1024,128]{1,0:T(8,128)S(1)}, bf16[1024,128]{1,0:T(8,128)(2,1)S(1)}) custom-call(s32[20]{0:T(128)S(1)} %concatenate.29.meta_ref, bf16[2048,256]{1,0:T(8,128)(2,1)S(1)} %get-tuple-element.35.psi_ref, bf16[2048,256]{1,0:T(8,128)(2,1)S(1)} %copy-done.3, bf16[2048,2048]{1,0:T(8,128)(2,1)S(1)} %bitcast.13), custom_call_target="tpu_custom_call" | custom-call | tf_op jit(solution)/shard_map/pallas_call | solution.py:91
  104.8 2.6 %collective-permute-start.23 = (bf16[512,256]{1,0:T(8,128)(2,1)S(1)}, bf16[512,256]{1,0:T(8,128)(2,1)S(1)}, u32[]{:S(2)}, u32[]{:S(2)}) collective-permute-start(bf16[512,256]{1,0:T(8,128)(2,1)S(1)} %slice.18), channel_id=1, source_target_pairs={{0,192},{1,49},{2,194},{3,51},{4,196},{5,53},{6,198},{7,55},{8,200... | collective-permute-start | bytes 786440 | tf_op jit(solution)/shard_map/ppermute | solution.py:300
  110.8 3.2 %collective-permute-done.25.right_ref = bf16[512,256]{1,0:T(8,128)(2,1)S(1)} collective-permute-done((bf16[512,256]{1,0:T(8,128)(2,1)S(1)}, bf16[512,256]{1,0:T(8,128)(2,1)S(1)}, u32[]{:S(2)}, u32[]{:S(2)}) %collective-permute-start.25) | collective-permute-done | bytes 262176 | tf_op jit(solution)/shard_map/ppermute | solution.py:301
  117.6 3.8 %collective-permute-start.18 = (bf16[1024,128]{1,0:T(8,128)(2,1)S(1)}, bf16[1024,128]{1,0:T(8,128)(2,1)S(1)}, u32[]{:S(2)}, u32[]{:S(2)}) collective-permute-start(bf16[1024,128]{1,0:T(8,128)(2,1)S(1)} %fusion.2.own_ref), channel_id=1, source_target_pairs={{2,4},{3,5},{6,8},{7,9},{10,12},{11,13},{14,16},{15,17},{18,20},{1... | collective-permute-start | bytes 786440 | tf_op jit(solution)/shard_map/ppermute | solution.py:372
  125.3 5.5 %collective-permute-done.18.outer_ref = bf16[1024,128]{1,0:T(8,128)(2,1)S(1)} collective-permute-done((bf16[1024,128]{1,0:T(8,128)(2,1)S(1)}, bf16[1024,128]{1,0:T(8,128)(2,1)S(1)}, u32[]{:S(2)}, u32[]{:S(2)}) %collective-permute-start.18) | collective-permute-done | bytes 262176 | tf_op jit(solution)/shard_map/ppermute | solution.py:372
  133.1 6.7 %collective-permute-done.29 = bf16[1024,128]{1,0:T(8,128)(2,1)S(1)} collective-permute-done((bf16[1024,128]{1,0:T(8,128)(2,1)S(1)}, bf16[1024,128]{1,0:T(8,128)(2,1)S(1)}, u32[]{:S(2)}, u32[]{:S(2)}) %collective-permute-start.29) | collective-permute-done | bytes 262176 | tf_op jit(solution)/shard_map/ppermute | solution.py:383
  (136 shorter events, 41.9 us)
Async XLA Ops:
  2.9 10.8 %collective-permute-start = (bf16[64,256]{1,0:T(8,128)(2,1)S(1)}, bf16[64,256]{1,0:T(8,128)(2,1)S(1)}, u32[]{:S(2)}, u32[]{:S(2)}) collective-permute-start(bf16[64,256]{1,0:T(8,128)(2,1)S(1)} %shard_map.64), channel_id=1, source_target_pairs={{0,12},{4,0},{8,4},{12,8},{16,28},{20,16},{24,20},{28,24},{32,44},... | collective-permute-start | bytes 98312 | tf_op jit(solution)/shard_map/ppermute | solution.py:286
  9.8 6.7 %collective-permute-start.1 = (bf16[64,256]{1,0:T(8,128)(2,1)S(1)}, bf16[64,256]{1,0:T(8,128)(2,1)S(1)}, u32[]{:S(2)}, u32[]{:S(2)}) collective-permute-start(bf16[64,256]{1,0:T(8,128)(2,1)S(1)} %shard_map.64), channel_id=1, source_target_pairs={{0,8},{4,12},{8,0},{12,4},{16,24},{20,28},{24,16},{28,20},{32,40},... | collective-permute-start | bytes 98312 | tf_op jit(solution)/shard_map/ppermute | solution.py:286
  16.5 6.1 %collective-permute-start.4 = (bf16[256,256]{1,0:T(8,128)(2,1)S(1)}, bf16[256,256]{1,0:T(8,128)(2,1)S(1)}, u32[]{:S(2)}, u32[]{:S(2)}) collective-permute-start(bf16[256,256]{1,0:T(8,128)(2,1)S(1)} %pad_maximum_fusion.2), channel_id=1, source_target_pairs={{0,48},{1,193},{2,50},{3,195},{4,52},{5,197},{6,54},{7,199},{8,56}... | collective-permute-start | bytes 393224 | tf_op jit(solution)/shard_map/ppermute | solution.py:291
  19.7 6.7 %collective-permute-start.6 = (bf16[256,256]{1,0:T(8,128)(2,1)S(1)}, bf16[256,256]{1,0:T(8,128)(2,1)S(1)}, u32[]{:S(2)}, u32[]{:S(2)}) collective-permute-start(bf16[256,256]{1,0:T(8,128)(2,1)S(1)} %pad_maximum_fusion.2), channel_id=1, source_target_pairs={{0,16},{1,65},{2,18},{3,67},{4,20},{5,69},{6,22},{7,71},{8,24},{9,... | collective-permute-start | bytes 393224 | tf_op jit(solution)/shard_map/ppermute | solution.py:291
  26.4 18.2 %collective-permute-start.7 = (bf16[1024,256]{1,0:T(8,128)(2,1)S(1)}, bf16[1024,256]{1,0:T(8,128)(2,1)S(1)}, u32[]{:S(2)}, u32[]{:S(2)}) collective-permute-start(bf16[1024,256]{1,0:T(8,128)(2,1)S(1)} %constant_dynamic-update-slice_fusion.line_ref), channel_id=1, source_target_pairs={{0,192},{1,49},{2,194},{3,51},{4,196},{5,53},{6,198},{7,55},{8,200... | collective-permute-start | bytes 1572872 | tf_op jit(solution)/shard_map/ppermute | solution.py:296
  28.6 15.3 %collective-permute-start.9 = (bf16[1024,256]{1,0:T(8,128)(2,1)S(1)}, bf16[1024,256]{1,0:T(8,128)(2,1)S(1)}, u32[]{:S(2)}, u32[]{:S(2)}) collective-permute-start(bf16[1024,256]{1,0:T(8,128)(2,1)S(1)} %constant_dynamic-update-slice_fusion.line_ref), channel_id=1, source_target_pairs={{0,64},{1,17},{2,66},{3,19},{4,68},{5,21},{6,70},{7,23},{8,72},{9,... | collective-permute-start | bytes 1572872 | tf_op jit(solution)/shard_map/ppermute | solution.py:296
  29.2 28.1 %collective-permute-start.3 = (bf16[1024,128]{1,0:T(8,128)(2,1)S(1)}, bf16[1024,128]{1,0:T(8,128)(2,1)}, u32[]{:S(2)}, u32[]{:S(2)}) collective-permute-start(bf16[1024,128]{1,0:T(8,128)(2,1)S(1)} %get-tuple-element.27.own_ref), channel_id=1, source_target_pairs={{2,4},{3,5},{6,8},{7,9},{10,12},{11,13},{14,16},{15,17},{18,20},{1... | collective-permute-start | bytes 786440 | tf_op jit(solution)/shard_map/ppermute | solution.py:344
  44.6 16.8 %collective-permute-start.10 = (bf16[512,256]{1,0:T(8,128)(2,1)}, bf16[512,256]{1,0:T(8,128)(2,1)S(1)}, u32[]{:S(2)}, u32[]{:S(2)}) collective-permute-start(bf16[512,256]{1,0:T(8,128)(2,1)} %slice.17), channel_id=1, source_target_pairs={{0,64},{1,17},{2,66},{3,19},{4,68},{5,21},{6,70},{7,23},{8,72},{9,... | collective-permute-start | bytes 786440 | tf_op jit(solution)/shard_map/ppermute | solution.py:301
  45.4 16.1 %collective-permute-start.8 = (bf16[512,256]{1,0:T(8,128)(2,1)}, bf16[512,256]{1,0:T(8,128)(2,1)}, u32[]{:S(2)}, u32[]{:S(2)}) collective-permute-start(bf16[512,256]{1,0:T(8,128)(2,1)} %slice.16), channel_id=1, source_target_pairs={{0,192},{1,49},{2,194},{3,51},{4,196},{5,53},{6,198},{7,55},{8,200... | collective-permute-start | bytes 786440 | tf_op jit(solution)/shard_map/ppermute | solution.py:300
  75.6 7.1 %collective-permute-start.12 = (bf16[64,256]{1,0:T(8,128)(2,1)S(1)}, bf16[64,256]{1,0:T(8,128)(2,1)S(1)}, u32[]{:S(2)}, u32[]{:S(2)}) collective-permute-start(bf16[64,256]{1,0:T(8,128)(2,1)S(1)} %get-tuple-element.52), channel_id=1, source_target_pairs={{0,8},{4,12},{8,0},{12,4},{16,24},{20,28},{24,16},{28,20},{32,40},... | collective-permute-start | bytes 98312 | tf_op jit(solution)/shard_map/ppermute | solution.py:286
  75.7 7.4 %collective-permute-start.13 = (bf16[64,256]{1,0:T(8,128)(2,1)S(1)}, bf16[64,256]{1,0:T(8,128)(2,1)S(1)}, u32[]{:S(2)}, u32[]{:S(2)}) collective-permute-start(bf16[64,256]{1,0:T(8,128)(2,1)S(1)} %get-tuple-element.52), channel_id=1, source_target_pairs={{0,4},{4,8},{8,12},{12,0},{16,20},{20,24},{24,28},{28,16},{32,36},... | collective-permute-start | bytes 98312 | tf_op jit(solution)/shard_map/ppermute | solution.py:286
  83.5 6.5 %collective-permute-start.21 = (bf16[256,256]{1,0:T(8,128)(2,1)S(1)}, bf16[256,256]{1,0:T(8,128)(2,1)S(1)}, u32[]{:S(2)}, u32[]{:S(2)}) collective-permute-start(bf16[256,256]{1,0:T(8,128)(2,1)S(1)} %pad_maximum_fusion.3), channel_id=1, source_target_pairs={{0,16},{1,65},{2,18},{3,67},{4,20},{5,69},{6,22},{7,71},{8,24},{9,... | collective-permute-start | bytes 393224 | tf_op jit(solution)/shard_map/ppermute | solution.py:291
  90.0 14.8 %collective-permute-start.22 = (bf16[1024,256]{1,0:T(8,128)(2,1)S(1)}, bf16[1024,256]{1,0:T(8,128)(2,1)S(1)}, u32[]{:S(2)}, u32[]{:S(2)}) collective-permute-start(bf16[1024,256]{1,0:T(8,128)(2,1)S(1)} %constant_dynamic-update-slice_fusion.7.line_ref), channel_id=1, source_target_pairs={{0,192},{1,49},{2,194},{3,51},{4,196},{5,53},{6,198},{7,55},{8,200... | collective-permute-start | bytes 1572872 | tf_op jit(solution)/shard_map/ppermute | solution.py:296
  90.1 17.4 %collective-permute-start.24 = (bf16[1024,256]{1,0:T(8,128)(2,1)S(1)}, bf16[1024,256]{1,0:T(8,128)(2,1)S(1)}, u32[]{:S(2)}, u32[]{:S(2)}) collective-permute-start(bf16[1024,256]{1,0:T(8,128)(2,1)S(1)} %constant_dynamic-update-slice_fusion.7.line_ref), channel_id=1, source_target_pairs={{0,64},{1,17},{2,66},{3,19},{4,68},{5,21},{6,70},{7,23},{8,72},{9,... | collective-permute-start | bytes 1572872 | tf_op jit(solution)/shard_map/ppermute | solution.py:296
  95.5 12.1 %collective-permute-start.15 = (bf16[1024,128]{1,0:T(8,128)(2,1)S(1)}, bf16[1024,128]{1,0:T(8,128)(2,1)S(1)}, u32[]{:S(2)}, u32[]{:S(2)}) collective-permute-start(bf16[1024,128]{1,0:T(8,128)(2,1)S(1)} %get-tuple-element.40), channel_id=1, source_target_pairs={{0,1},{1,0},{2,3},{3,2},{4,5},{5,4},{6,7},{7,6},{8,9},{9,8},{10,11... | collective-permute-start | bytes 786440 | tf_op jit(solution)/shard_map/ppermute | solution.py:360
  104.5 12.8 %collective-permute-start.14 = (bf16[1024,128]{1,0:T(8,128)(2,1)S(1)}, bf16[1024,128]{1,0:T(8,128)(2,1)S(1)}, u32[]{:S(2)}, u32[]{:S(2)}) collective-permute-start(bf16[1024,128]{1,0:T(8,128)(2,1)S(1)} %get-tuple-element.37), channel_id=1, source_target_pairs={{0,1},{1,0},{2,3},{3,2},{4,5},{5,4},{6,7},{7,6},{8,9},{9,8},{10,11... | collective-permute-start | bytes 786440 | tf_op jit(solution)/shard_map/ppermute | solution.py:364
  107.5 6.5 %collective-permute-start.25 = (bf16[512,256]{1,0:T(8,128)(2,1)S(1)}, bf16[512,256]{1,0:T(8,128)(2,1)S(1)}, u32[]{:S(2)}, u32[]{:S(2)}) collective-permute-start(bf16[512,256]{1,0:T(8,128)(2,1)S(1)} %slice.19), channel_id=1, source_target_pairs={{0,64},{1,17},{2,66},{3,19},{4,68},{5,21},{6,70},{7,23},{8,72},{9,... | collective-permute-start | bytes 786440 | tf_op jit(solution)/shard_map/ppermute | solution.py:301
  107.7 9.6 %collective-permute-start.16 = (bf16[1024,128]{1,0:T(8,128)(2,1)S(1)}, bf16[1024,128]{1,0:T(8,128)(2,1)S(1)}, u32[]{:S(2)}, u32[]{:S(2)}) collective-permute-start(bf16[1024,128]{1,0:T(8,128)(2,1)S(1)} %add_convert_fusion.1), channel_id=1, source_target_pairs={{0,2},{1,3},{2,0},{3,1},{4,6},{5,7},{6,4},{7,5},{8,10},{9,11},{10,... | collective-permute-start | bytes 786440 | tf_op jit(solution)/shard_map/ppermute | solution.py:361
  116.8 7.8 %collective-permute-start.27 = (bf16[1024,128]{1,0:T(8,128)(2,1)S(1)}, bf16[1024,128]{1,0:T(8,128)(2,1)S(1)}, u32[]{:S(2)}, u32[]{:S(2)}) collective-permute-start(bf16[1024,128]{1,0:T(8,128)(2,1)S(1)} %get-tuple-element.48), channel_id=1, source_target_pairs={{0,1},{1,0},{2,3},{3,2},{4,5},{5,4},{6,7},{7,6},{8,9},{9,8},{10,11... | collective-permute-start | bytes 786440 | tf_op jit(solution)/shard_map/ppermute | solution.py:360
  117.5 7.8 %collective-permute-start.17 = (bf16[1024,128]{1,0:T(8,128)(2,1)S(1)}, bf16[1024,128]{1,0:T(8,128)(2,1)S(1)}, u32[]{:S(2)}, u32[]{:S(2)}) collective-permute-start(bf16[1024,128]{1,0:T(8,128)(2,1)S(1)} %fusion.2.own_ref), channel_id=1, source_target_pairs={{0,2},{1,3},{2,0},{3,1},{4,6},{5,7},{6,4},{7,5},{8,10},{9,11},{10,... | collective-permute-start | bytes 786440 | tf_op jit(solution)/shard_map/ppermute | solution.py:371
  117.6 13.3 %collective-permute-start.18 = (bf16[1024,128]{1,0:T(8,128)(2,1)S(1)}, bf16[1024,128]{1,0:T(8,128)(2,1)S(1)}, u32[]{:S(2)}, u32[]{:S(2)}) collective-permute-start(bf16[1024,128]{1,0:T(8,128)(2,1)S(1)} %fusion.2.own_ref), channel_id=1, source_target_pairs={{2,4},{3,5},{6,8},{7,9},{10,12},{11,13},{14,16},{15,17},{18,20},{1... | collective-permute-start | bytes 786440 | tf_op jit(solution)/shard_map/ppermute | solution.py:372
  123.2 8.9 %collective-permute-start.26 = (bf16[1024,128]{1,0:T(8,128)(2,1)S(1)}, bf16[1024,128]{1,0:T(8,128)(2,1)S(1)}, u32[]{:S(2)}, u32[]{:S(2)}) collective-permute-start(bf16[1024,128]{1,0:T(8,128)(2,1)S(1)} %get-tuple-element.47), channel_id=1, source_target_pairs={{0,1},{1,0},{2,3},{3,2},{4,5},{5,4},{6,7},{7,6},{8,9},{9,8},{10,11... | collective-permute-start | bytes 786440 | tf_op jit(solution)/shard_map/ppermute | solution.py:364
  124.6 7.9 %collective-permute-start.28 = (bf16[1024,128]{1,0:T(8,128)(2,1)S(1)}, bf16[1024,128]{1,0:T(8,128)(2,1)S(1)}, u32[]{:S(2)}, u32[]{:S(2)}) collective-permute-start(bf16[1024,128]{1,0:T(8,128)(2,1)S(1)} %add_convert_fusion), channel_id=1, source_target_pairs={{0,2},{1,3},{2,0},{3,1},{4,6},{5,7},{6,4},{7,5},{8,10},{9,11},{10,... | collective-permute-start | bytes 786440 | tf_op jit(solution)/shard_map/ppermute | solution.py:361
  132.7 7.1 %collective-permute-start.29 = (bf16[1024,128]{1,0:T(8,128)(2,1)S(1)}, bf16[1024,128]{1,0:T(8,128)(2,1)S(1)}, u32[]{:S(2)}, u32[]{:S(2)}) collective-permute-start(bf16[1024,128]{1,0:T(8,128)(2,1)S(1)} %fusion.3), channel_id=1, source_target_pairs={{0,2},{1,3},{2,0},{3,1},{4,6},{5,7},{6,4},{7,5},{8,10},{9,11},{10,... | collective-permute-start | bytes 786440 | tf_op jit(solution)/shard_map/ppermute | solution.py:383
  (19 other events, 269.1 us)

commit v3 on v2

--- a/solution.py
+++ b/solution.py
@@ -77,16 +77,21 @@
 
 
 VMEM = pl.BlockSpec(memory_space=pltpu.VMEM)
+HBM = pl.BlockSpec(memory_space=pltpu.HBM)
 
 
 def near(value):
     return pltpu.with_memory_space_constraint(value, pltpu.VMEM)
+
+
+def far_away(value):
+    return pltpu.with_memory_space_constraint(value, pltpu.HBM)
 
 
 def call(kernel, scalars, args, specs, out_shape, out_specs=None, grid=(1,), scratch=(), aliases=None):
     if out_specs is None:
         out_specs = [VMEM] * len(out_shape)
-    args = [near(a) if spec is VMEM else a for a, spec in zip(args, specs)]
+    args = [near(a) if spec is VMEM else far_away(a) if spec is HBM else a for a, spec in zip(args, specs)]
     out_shape = [pltpu.VMEM(o.shape, o.dtype) if spec is VMEM else o for o, spec in zip(out_shape, out_specs)]
     return pl.pallas_call(
         kernel,
@@ -107,7 +112,7 @@
     size = row.shape[1]
     diag = lax.broadcasted_iota(jnp.int32, (size, size), 0) == lax.broadcasted_iota(jnp.int32, (size, size), 1)
     spread = jnp.broadcast_to(row.astype(F32), (size, size))
-    return jnp.sum(jnp.where(diag, spread, 0.0), axis=1, keepdims=True).astype(jnp.int32)
+    return jnp.sum(jnp.where(diag, spread, 0.0), axis=1, keepdims=True).astype(row.dtype)
 
 
 def selection(column, start, width):
@@ -117,6 +122,43 @@
 
 def all_columns(rows_ref):
     return jnp.concatenate([as_column(rows_ref[p]) for p in range(4)], axis=0)
+
+
+def index_kernel(ids_ref, count_ref, where_ref, meta_ref, start_ref):
+    block, core, slab = ids_ref[0], ids_ref[1], ids_ref[3]
+    my_y, my_x, my_z = slab // 16, (slab // 4) % 4, slab % 4
+    start_ref[0] = 0
+
+    def add(n, carry):
+        start_ref[n + 1] = start_ref[n] + count_ref[block, n]
+        return carry
+
+    lax.fori_loop(0, 64, add, 0)
+    for n in range(4):
+        meta_ref[n] = ids_ref[n]
+    lane = lax.broadcasted_iota(jnp.int32, (1, TILE), 1)
+    for outer in range(4):
+        for inner in range(4):
+            y_step, x_step = jnp.where(core == 0, outer, inner), jnp.where(core == 0, inner, outer)
+            first = (((my_y + y_step) % 4) * 4 + (my_x + x_step) % 4) * 4
+            base = start_ref[first] // 8 * 8
+            meta_ref[4 + outer * 4 + inner] = base
+            row = jnp.full((1, TILE), -1, jnp.int32)
+            for d in range(4):
+                slab_d = first + (my_z + d) % 4
+                begin = start_ref[slab_d]
+                size = start_ref[slab_d + 1] - begin
+                slot = lane - d * CAP
+                row = jnp.where((slot >= 0) & (slot < size), begin - base + slot, row)
+            where_ref[pl.ds(outer * 4 + inner, 1), :] = row
+
+
+def index(ids, counts):
+    smem = pl.BlockSpec(memory_space=pltpu.SMEM)
+    return call(
+        index_kernel, ids, (counts,), [smem], [array((16, TILE), jnp.int32), array((20,), jnp.int32)],
+        [VMEM, smem], scratch=[pltpu.SMEM((72,), jnp.int32)],
+    )
 
 
 def pick_own_kernel(meta_ref, rows_ref, field_ref, out_ref):
@@ -138,21 +180,20 @@
         hot_ref[...] = selection(all_columns(rows_ref), 0, ROWS)
         orb_out[...] = jnp.dot(hot_ref[...], field_ref[...], preferred_element_type=F32).astype(BF)
 
-    fit_out[...] = jnp.dot(hot_ref[...], fit_ref[...], preferred_element_type=F32).astype(BF)
+    at = pl.ds(pl.multiple_of(pl.program_id(0) * 512, 512), 512)
+    fit_out[:, at] = jnp.dot(hot_ref[...], fit_ref[:, at], preferred_element_type=F32).astype(BF)
 
 
 def pick_all(meta, rows, field, fit):
     return call(
-        pick_all_kernel, meta, (rows, field, fit),
-        [VMEM, VMEM, pl.BlockSpec((ROWS, 512), lambda i, m: (0, i))],
-        [array((ALL, NB), BF), array((ALL, PTS), BF)],
-        [pl.BlockSpec((ALL, NB), lambda i, m: (0, 0)), pl.BlockSpec((ALL, 512), lambda i, m: (0, i))],
-        grid=(4,), scratch=[pltpu.VMEM((ALL, ROWS), BF)],
+        pick_all_kernel, meta, (rows, field, fit), [VMEM] * 3,
+        [array((ALL, NB), BF), array((ALL, PTS), BF)], grid=(4,), scratch=[pltpu.VMEM((ALL, ROWS), BF)],
     )
 
 
 def stencil_kernel(meta_ref, rows_ref, own_ref, inner_ref, outer_ref, pot_ref, table_ref, local_ref, *picked):
     first = meta_ref[2] == 0
+    pot = pot_ref[pl.ds(pl.multiple_of(meta_ref[2] * 8, 8), 8), :]
     planes = []
     for k in range(4):
         part = pl.ds(k * PLANE, PLANE)
@@ -170,7 +211,8 @@
         total += 3.0 * stencil_coef[0] * center
         for offset in range(1, 5):
             total += stencil_coef[offset] * (planes[4 + k + offset] + planes[4 + k - offset])
-        local_ref[part, :] = -0.5 * total + pot_ref[part, :] * center
+        scale = jnp.concatenate([as_column(pot[2 * k + n : 2 * k + n + 1, :]) for n in (0, 1)], axis=0)
+        local_ref[part, :] = -0.5 * total + scale * center
     if picked:
         hot = selection(all_columns(rows_ref), meta_ref[2] * SHARE, SHARE)
         picked[0][...] = jnp.dot(hot, local_ref[...].astype(BF), preferred_element_type=F32)
@@ -213,22 +255,82 @@
 
 
 def listed_kernel(meta_ref, where_ref, left_ref, right_ref, early_ref, orb_ref, fit_ref, local_ref,
-                  sum_ref, psi_ref, pick_ref):
+                  sum_ref, psi_ref, keep_ref, gone_ref):
     place_late(meta_ref, where_ref, left_ref, right_ref, sum_ref, psi_ref)
     density = lax.dot_general(orb_ref[...], psi_ref[...], (((1,), (1,)), ((), ())), preferred_element_type=F32)
     kern = (fit_ref[...].astype(F32) * density).astype(BF)
     part = -jnp.dot(kern, psi_ref[...], preferred_element_type=F32)
     core = meta_ref[1]
+    first = meta_ref[2] == 0
     local = local_ref[...]
-    pick_ref[:, :HALF] = (part[:, :HALF] + jnp.where(core == 0, local, 0.0)).astype(BF)
-    pick_ref[:, HALF:] = (part[:, HALF:] + jnp.where(core == 0, 0.0, local)).astype(BF)
+    part = jnp.concatenate(
+        [part[:, :HALF] + jnp.where(core == 0, local, 0.0), part[:, HALF:] + jnp.where(core == 0, 0.0, local)], axis=1
+    )
+    mine = [jnp.where(core == 0, part[c * 128 : c * 128 + CAP], part[c * 128 + CAP : c * 128 + 128]) for c in (0, 1)]
+    other = [jnp.where(core == 0, part[c * 128 + CAP : c * 128 + 128], part[c * 128 : c * 128 + CAP]) for c in (0, 1)]
+    keep_ref[:CAP, :] = jnp.where(first, mine[0], mine[1])
+    keep_ref[CAP:, :] = jnp.where(first, mine[1], mine[0])
+    gone_ref[:CAP, :] = jnp.where(first, other[0], other[1]).astype(BF)
+    gone_ref[CAP:, :] = jnp.where(first, other[1], other[0]).astype(BF)
 
 
 def listed(meta, where, left, right, early, orb, fit, local):
     return call(
         listed_kernel, meta, (where, left, right, early, orb, fit, local), [VMEM] * 7,
-        [array((PTS + WIN, NB), F32), array((PTS, NB), BF), array((ALL, NB), BF)], aliases={4: 0},
+        [array((PTS + WIN, NB), F32), array((PTS, NB), BF), array((2 * CAP, NB), F32), array((2 * CAP, NB), BF)],
+        aliases={4: 0},
     )[1:]
+
+
+def pair_kernel(meta_ref, keep_ref, got_ref, near_ref, far_ref):
+    near_ref[...] = keep_ref[:CAP, :] + got_ref[:CAP, :].astype(F32)
+    far_ref[...] = (keep_ref[CAP:, :] + got_ref[CAP:, :].astype(F32)).astype(BF)
+
+
+def pair_up(meta, keep, got):
+    return call(pair_kernel, meta, (keep, got), [VMEM] * 2, [array((CAP, NB), F32), array((CAP, NB), BF)])
+
+
+def update_kernel(meta_ref, near_ref, far_ref, old_ref, new_ref):
+    applied = near_ref[...] + far_ref[...].astype(F32)
+    new_ref[...] = ((applied - 3.5 * old_ref[...].astype(F32)) / 4.0).astype(BF)
+
+
+def update_points(meta, near_part, far_part, old):
+    return call(update_kernel, meta, (near_part, far_part, old), [VMEM] * 3, [array((CAP, NB), BF)])[0]
+
+
+def stage_kernel(meta_ref, fit_ref, out_ref, sem):
+    copy = pltpu.make_async_copy(fit_ref, out_ref, sem)
+    copy.start()
+    copy.wait()
+
+
+def stage(meta, fit):
+    return call(
+        stage_kernel, meta, (fit,), [HBM], [array((ROWS, PTS), BF)],
+        scratch=[pltpu.SemaphoreType.DMA],
+    )[0]
+
+
+def join_kernel(meta_ref, *refs):
+    size = refs[0].shape[0]
+    for n, ref in enumerate(refs[:-1]):
+        refs[-1][pl.ds(n * size, size), :] = ref[...]
+
+
+def join(meta, parts):
+    shape = (len(parts) * parts[0].shape[0], NB)
+    return call(join_kernel, meta, parts, [VMEM] * len(parts), [array(shape, BF)])[0]
+
+
+def halves_kernel(meta_ref, up_ref, down_ref, left_ref, right_ref):
+    left_ref[...] = up_ref[: 2 * TILE, :]
+    right_ref[...] = down_ref[2 * TILE :, :]
+
+
+def halves(meta, up, down):
+    return call(halves_kernel, meta, (up, down), [VMEM] * 2, [array((2 * TILE, NB), BF)] * 2)
 
 
 def finish_points(meta, where, left, right, early):
@@ -245,21 +347,25 @@
     send_ref[at, :] = jnp.where(core == 0, right, left).astype(BF)
 
 
-def build_kernel(meta_ref, psi_ref, orb_ref, fit_ref, kern_ref, keep_ref, send_ref):
-    at = pl.ds(pl.multiple_of(pl.program_id(0) * TILE, TILE), TILE)
-    density = lax.dot_general(orb_ref[...], psi_ref[...], (((1,), (1,)), ((), ())), preferred_element_type=F32)
-    kern = (fit_ref[...].astype(F32) * density).astype(BF)
-    kern_ref[at, :] = kern
-    emit(meta_ref, -jnp.dot(kern, psi_ref[...], preferred_element_type=F32), keep_ref, send_ref, at)
+def build_with(away):
+    def build_kernel(meta_ref, psi_ref, orb_ref, fit_ref, kern_ref, keep_ref, send_ref):
+        step = pl.program_id(0)
+        half = 1 - meta_ref[2] if away else meta_ref[2]
+        at = pl.ds(pl.multiple_of(step * TILE, TILE), TILE)
+        rows = pl.ds(pl.multiple_of(half * SHARE + step * TILE, TILE), TILE)
+        density = lax.dot_general(
+            orb_ref[rows, :], psi_ref[...], (((1,), (1,)), ((), ())), preferred_element_type=F32
+        )
+        kern = (fit_ref[rows, :].astype(F32) * density).astype(BF)
+        kern_ref[at, :] = kern
+        emit(meta_ref, -jnp.dot(kern, psi_ref[...], preferred_element_type=F32), keep_ref, send_ref, at)
+
+    return build_kernel
 
 
 def build(meta, psi, orb, fit, away):
-    def mapped(i, m):
-        return (i + 4 * (1 - m[2] if away else m[2]), 0)
-
-    return call(
-        build_kernel, meta, (psi, orb, fit),
-        [VMEM, pl.BlockSpec((TILE, NB), mapped), pl.BlockSpec((TILE, PTS), mapped)],
+    return call(
+        build_with(away), meta, (psi, orb, fit), [VMEM] * 3,
         [array((SHARE, PTS), BF), array((SHARE, HALF), F32), array((SHARE, HALF), BF)], grid=(4,),
     )
 
@@ -278,27 +384,53 @@
     )
 
 
+def sum_kernel(meta_ref, keep_ref, got_ref, sum_ref):
+    sum_ref[...] = (keep_ref[...] + got_ref[...].astype(F32)).astype(BF)
+
+
+def sum_away(meta, keep, got):
+    return call(sum_kernel, meta, (keep, got), [VMEM] * 2, [array((SHARE, HALF), BF)])[0]
+
+
+def field_kernel(meta_ref, local_ref, keep_ref, core_ref, chip_ref, field_ref, *rest):
+    current = field_ref[...].astype(F32)
+    applied = local_ref[...] + (keep_ref[...] + core_ref[...].astype(F32) + chip_ref[...].astype(F32))
+    scaled = applied - 3.5 * current
+    if len(rest) == 1:
+        rest[0][...] = (scaled / 4.0).astype(BF)
+    else:
+        rest[1][...] = (0.5 * scaled - rest[0][...].astype(F32)).astype(BF)
+
+
+def next_field(meta, local, parts, *fields):
+    return call(
+        field_kernel, meta, (local, *parts, *fields), [VMEM] * (4 + len(fields)),
+        [array((SHARE, HALF), BF)],
+    )[0]
+
+
 def after(value, *earlier):
     return lax.optimization_barrier((value,) + earlier)[0]
 
 
-def gather_column(own):
+def gather_column(meta, own):
     parts = [own] + [lax.ppermute(own, "slab", z_shift(d)) for d in (1, 2, 3)]
-    return jnp.concatenate(parts, axis=0)
-
-
-def gather_line(column):
+    return join(meta, parts)
+
+
+def gather_line(meta, column):
     parts = [column] + [lax.ppermute(column, BOTH, plane_shift(d, False)) for d in (1, 2, 3)]
-    return jnp.concatenate(parts, axis=0)
+    return join(meta, parts)
 
 
 def gather_sides(line):
     return (lax.ppermute(line, BOTH, plane_shift(1, True)), lax.ppermute(line, BOTH, plane_shift(-1, True)))
 
 
-def gather_far(up, down):
-    left = lax.ppermute(up[: 2 * TILE], BOTH, plane_shift(1, True))
-    right = lax.ppermute(down[2 * TILE :], BOTH, plane_shift(-1, True))
+def gather_far(meta, up, down):
+    near_up, near_down = halves(meta, up, down)
+    left = lax.ppermute(near_up, BOTH, plane_shift(1, True))
+    right = lax.ppermute(near_down, BOTH, plane_shift(-1, True))
     return left, right
 
 
@@ -307,78 +439,58 @@
     slab = lax.axis_index("slab")
     core = point_block % 2
     chip = point_block // 2
-    my_z = slab % 4
-    my_x = (slab // 4) % 4
-    my_y = slab // 16
-
-    counts = lax.dynamic_index_in_dim(owner_count, point_block, 0, keepdims=False)
-    four = jnp.arange(4, dtype=jnp.int32)
-    outer_step = four[:, None, None]
-    inner_step = four[None, :, None]
-    y_id = jnp.where(core == 0, my_y + outer_step, my_y + inner_step) % 4
-    x_id = jnp.where(core == 0, my_x + inner_step, my_x + outer_step) % 4
-    z_id = (my_z + four[None, None, :]) % 4
-    column_id = y_id * 4 + x_id
-    slabs = (column_id * 4 + z_id).reshape(16, 4)
-    first = (column_id * 4).reshape(16)
-    every = jnp.arange(64, dtype=jnp.int32)
-    start = jnp.sum(jnp.where(every < slabs[:, :, None], counts, 0), axis=2)
-    size = jnp.sum(jnp.where(every == slabs[:, :, None], counts, 0), axis=2)
-    base = jnp.sum(jnp.where(every[None, :] < first[:, None], counts, 0), axis=1) // 8 * 8
-    slot = jnp.arange(CAP, dtype=jnp.int32)
-    where = jnp.where(slot < size[:, :, None], start[:, :, None] - base[:, None, None] + slot, -1).reshape(16, TILE)
     ids = jnp.stack([point_block, core, chip, slab]).astype(jnp.int32)
-    meta = jnp.concatenate([ids, base.astype(jnp.int32)])
     table = split_table()
     row0 = chip * SHARE
 
     own0 = pick_own(ids, owner_rows, orbitals)
-    column0 = gather_column(own0)
-    line0 = gather_line(column0)
+    early_orbitals = after(orbitals, own0)
+    field0 = lax.dynamic_slice(early_orbitals, (row0, core * HALF), (SHARE, HALF))
+    inner0 = lax.dynamic_slice(early_orbitals, (SHARE - row0, core * HALF), (SHARE, HALF))
+    potential_rows = potential.reshape(16, 128)
+    column0 = gather_column(ids, own0)
+    fit = stage(ids, after(fit_matrix, column0, inner0))
+    line0 = gather_line(ids, column0)
     up0, down0 = gather_sides(line0)
-    left0, right0 = gather_far(up0, down0)
-
-    field0 = lax.dynamic_slice(orbitals, (row0, core * HALF), (SHARE, HALF))
-    inner0 = lax.dynamic_slice(orbitals, (SHARE - row0, core * HALF), (SHARE, HALF))
-    potential_piece = lax.dynamic_slice(potential, (row0,), (SHARE,)).reshape(SHARE, 1)
-    outer0 = lax.ppermute(after(field0, column0), BOTH, EDGE_SWAP)
-    orb_listed, fit_listed = pick_all(ids, after(owner_rows, column0), orbitals, fit_matrix)
-    local0, local_listed = stencil(ids, owner_rows, field0, inner0, outer0, potential_piece, table, True)
+    where, meta = index(ids, after(owner_count, up0))
+    left0, right0 = gather_far(ids, up0, down0)
+
+    outer0 = lax.ppermute(field0, BOTH, EDGE_SWAP)
+    orb_listed, fit_listed = pick_all(ids, after(owner_rows, line0), orbitals, fit)
+    local0, local_listed = stencil(ids, owner_rows, field0, inner0, outer0, potential_rows, table, True)
 
     early0 = place_early(meta, where, line0, up0, down0)
-    psi0, picked = listed(meta, where, left0, right0, early0, orb_listed, fit_listed, local_listed)
-
-    pieces = lax.all_to_all(picked.reshape(4, CAP, NB), "pt", 0, 0)
-    applied = jnp.sum(pieces.astype(F32), axis=0)
-    own1 = ((applied - 3.5 * own0.astype(F32)) / 4.0).astype(BF)
-    column1 = gather_column(own1)
-    line1 = gather_line(column1)
+    psi0, keep, gone = listed(meta, where, left0, right0, early0, orb_listed, fit_listed, local_listed)
+
+    near_part, far_part = pair_up(ids, keep, lax.ppermute(gone, "pt", CORE_SWAP))
+    other_part = lax.ppermute(far_part, "pt", CHIP_SWAP)
+    own1 = update_points(ids, near_part, other_part, own0)
+    column1 = gather_column(ids, own1)
+    line1 = gather_line(ids, column1)
     up1, down1 = gather_sides(line1)
-    left1, right1 = gather_far(up1, down1)
+    left1, right1 = gather_far(ids, up1, down1)
 
     def send_away(keep, gone):
-        total = keep + lax.ppermute(gone, "pt", CORE_SWAP).astype(F32)
-        return lax.ppermute(total.astype(BF), "pt", CHIP_SWAP)
-
-    def join_own(keep, gone, away):
-        return keep + lax.ppermute(gone, "pt", CORE_SWAP).astype(F32) + away.astype(F32)
-
-    kern_away, keep, gone = build(meta, after(psi0, own1), orbitals, fit_matrix, True)
+        total = sum_away(ids, keep, lax.ppermute(gone, "pt", CORE_SWAP))
+        return lax.ppermute(total, "pt", CHIP_SWAP)
+
+    def own_parts(keep, gone, away):
+        return keep, lax.ppermute(gone, "pt", CORE_SWAP), away
+
+    kern_away, keep, gone = build(meta, after(psi0, far_part), orbitals, fit, True)
     away = send_away(keep, gone)
-    kern_own, keep, gone = build(meta, after(psi0, column1), orbitals, fit_matrix, False)
-    applied0 = local0 + join_own(keep, gone, away)
-    field1 = ((applied0 - 3.5 * field0.astype(F32)) / 4.0).astype(BF)
+    kern_own, keep, gone = build(meta, after(psi0, own1), orbitals, fit, False)
+    field1 = next_field(ids, local0, own_parts(keep, gone, away), field0)
     inner1 = lax.ppermute(field1, "pt", CHIP_SWAP)
     outer1 = lax.ppermute(field1, BOTH, EDGE_SWAP)
-    local1 = stencil(ids, owner_rows, field1, inner1, outer1, potential_piece, table, False)[0]
+    local1 = stencil(ids, owner_rows, field1, inner1, outer1, potential_rows, table, False)[0]
 
     early1 = place_early(meta, where, line1, up1, down1)
     psi1 = finish_points(meta, where, left1, right1, early1)
     keep, gone = apply(meta, psi1, kern_away)
     away = send_away(keep, gone)
     keep, gone = apply(meta, after(psi1, keep), kern_own)
-    applied1 = local1 + join_own(keep, gone, away)
-    field2 = (0.5 * (applied1 - 3.5 * field1.astype(F32)) - field0.astype(F32)).astype(BF)
+    field2 = next_field(ids, local1, own_parts(keep, gone, away), field1, field0)
 
     other = lax.ppermute(field2, "pt", CHIP_SWAP)
     column = jnp.concatenate([jnp.where(chip == 0, field2, other), jnp.where(chip == 0, other, field2)], axis=0)

time: 145 us -> 151 us (1.041)
  blocking collectives: 11.2 us -> 0 us
  Pallas kernels: 27.7 us -> 38.8 us
  starting transfers between devices: 44.1 us -> 54.9 us
  local copies, waits for them, and re-layouts: 8.35 us -> 1.97 us
  waiting for transfers between devices: 50.1 us -> 53.5 us
    all_to_all x1 -> x0, blocking collectives: 11.2 us -> none  [body(): pieces = lax.all_to_all(picked.reshape(4, CAP, NB), 'pt', 0, 0)]
    pallas_call x12 -> x26, Pallas kernels: 27.7 us -> 38.8 us  [call(): pl.pallas_call(kernel, grid_spec=pltpu.PrefetchScalarGridSpec(num_scalar_...]
    ppermute x11 -> x13, starting transfers between devices: 16.2 us -> 25.8 us  [the longest x2 5.98 us: send_away(): total = sum_away(ids, keep, lax.ppermute(gone, 'pt', CORE_SWAP))]
    ppermute x11 -> x13, waiting for transfers between devices: 5.35 us -> 10.1 us  [the longest x2 6.38 us: send_away(): return lax.ppermute(total, 'pt', CHIP_SWAP)]
    unnamed x33 -> x14, local copies, waits for them, and re-layouts: 5.38 us -> 1.93 us
    ppermute x2, waiting for transfers between devices: 0.01 us -> 2.6 us  [gather_sides(): lax.ppermute(line, BOTH, plane_shift(1, True))]
    ppermute x2, waiting for transfers between devices: 11.2 us -> 9.02 us  [gather_sides(): lax.ppermute(line, BOTH, plane_shift(-1, True))]
    ppermute x1, waiting for transfers between devices: 5.53 us -> 3.69 us  [body(): outer1 = lax.ppermute(field1, BOTH, EDGE_SWAP)]
  transfers between devices with their start and end apart: 31 -> 33, of which waited for: 18 -> 19; matrix products, arithmetic and copies ran while one was open for 3% -> 0% of each run, Pallas kernels for 17% -> 21%
where the time goes in v3:
time: 151 us
  starting transfers between devices  54.9 us (36%)
  waiting for transfers between devices  53.5 us (35%)
  Pallas kernels  38.8 us (26%)
  local copies, waits for them, and re-layouts  1.97 us (1%)
    pallas_call x26, Pallas kernels, call(): pl.pallas_call(kernel, grid_spec=pltpu.PrefetchScalarGridSpec(num_scalar_...  38.8 us
    ppermute x6, starting transfers between devices, gather_column(): parts = [own] + [lax.ppermute(own, 'slab', z_shift(d)) for d in (1, 2, 3)]  12.6 us
    ppermute x6, waiting for transfers between devices, gather_line(): lax.ppermute(column, BOTH, plane_shift(d, False))  11.3 us
    ppermute x2, waiting for transfers between devices, gather_sides(): lax.ppermute(line, BOTH, plane_shift(-1, True))  9.02 us
    ppermute x6, waiting for transfers between devices, gather_column(): parts = [own] + [lax.ppermute(own, 'slab', z_shift(d)) for d in (1, 2, 3)]  8.55 us
    ppermute x1, waiting for transfers between devices, body(): other = lax.ppermute(field2, 'pt', CHIP_SWAP)  6.7 us
    ppermute x2, waiting for transfers between devices, send_away(): return lax.ppermute(total, 'pt', CHIP_SWAP)  6.38 us
    ppermute x2, starting transfers between devices, send_away(): total = sum_away(ids, keep, lax.ppermute(gone, 'pt', CORE_SWAP))  5.98 us
  transfers between devices with their start and end apart: 33, of which 19 were waited for; matrix products, arithmetic and copies ran while one was open for 0% of the time, Pallas kernels for 21%

profile of v3, /device:TPU:1, one launch (start us, length us, event | category | flops | bytes accessed | tf_op | source)
XLA Modules:
  0.0 150.9 jit_solution(9762113282596802865)
XLA Ops:
  2.9 6.9 %collective-permute-start.1 = (bf16[64,256]{1,0:T(8,128)(2,1)S(1)}, bf16[64,256]{1,0:T(8,128)(2,1)S(1)}, u32[]{:S(2)}, u32[]{:S(2)}) collective-permute-start(bf16[64,256]{1,0:T(8,128)(2,1)S(1)} %shard_map.64.refs_0_.old_ref), channel_id=1, source_target_pairs={{0,12},{4,0},{8,4},{12,8},{16,28},{20,16},{24,20},{28,24},{32,44},... | collective-permute-start | bytes 98312 | tf_op jit(solution)/shard_map/ppermute | solution.py:417
  13.1 3.4 %collective-permute-done.2.refs_2_ = bf16[64,256]{1,0:T(8,128)(2,1)S(1)} collective-permute-done((bf16[64,256]{1,0:T(8,128)(2,1)S(1)}, bf16[64,256]{1,0:T(8,128)(2,1)S(1)}, u32[]{:S(2)}, u32[]{:S(2)}) %collective-permute-start.2) | collective-permute-done | bytes 32800 | tf_op jit(solution)/shard_map/ppermute | solution.py:417
  17.0 2.8 %collective-permute-start.4 = (bf16[256,256]{1,0:T(8,128)(2,1)S(1)}, bf16[256,256]{1,0:T(8,128)(2,1)S(1)}, u32[]{:S(2)}, u32[]{:S(2)}) collective-permute-start(bf16[256,256]{1,0:T(8,128)(2,1)S(1)} %shard_map.66.refs_0_), channel_id=1, source_target_pairs={{0,48},{1,193},{2,50},{3,195},{4,52},{5,197},{6,54},{7,199},{8,56}... | collective-permute-start | bytes 393224 | tf_op jit(solution)/shard_map/ppermute | solution.py:422
  29.8 3.5 %collective-permute-start = (bf16[1024,128]{1,0:T(8,128)(2,1)S(1)}, bf16[1024,128]{1,0:T(8,128)(2,1)S(1)}, u32[]{:S(2)}, u32[]{:S(2)}) collective-permute-start(bf16[1024,128]{1,0:T(8,128)(2,1)S(1)} %get-tuple-element.74.own_ref.field_ref.rest_0_), channel_id=1, source_target_pairs={{2,4},{3,5},{6,8},{7,9},{10,12},{11,13},{14,16},{15,17},{18,20},{1... | collective-permute-start | bytes 786440 | tf_op jit(solution)/shard_map/ppermute | solution.py:458
  33.3 2.6 %collective-permute-done.7.up_ref = bf16[1024,256]{1,0:T(8,128)(2,1)S(1)} collective-permute-done((bf16[1024,256]{1,0:T(8,128)(2,1)S(1)}, bf16[1024,256]{1,0:T(8,128)(2,1)S(1)}, u32[]{:S(2)}, u32[]{:S(2)}) %collective-permute-start.7) | collective-permute-done | bytes 524320 | tf_op jit(solution)/shard_map/ppermute | solution.py:427
  35.9 9.0 %collective-permute-done.8.down_ref = bf16[1024,256]{1,0:T(8,128)(2,1)S(1)} collective-permute-done((bf16[1024,256]{1,0:T(8,128)(2,1)S(1)}, bf16[1024,256]{1,0:T(8,128)(2,1)S(1)}, u32[]{:S(2)}, u32[]{:S(2)}) %collective-permute-start.8) | collective-permute-done | bytes 524320 | tf_op jit(solution)/shard_map/ppermute | solution.py:427
  45.5 2.7 %collective-permute-start.9 = (bf16[512,256]{1,0:T(8,128)(2,1)S(1)}, bf16[512,256]{1,0:T(8,128)(2,1)S(1)}, u32[]{:S(2)}, u32[]{:S(2)}) collective-permute-start(bf16[512,256]{1,0:T(8,128)(2,1)S(1)} %get-tuple-element.43), channel_id=1, source_target_pairs={{0,192},{1,49},{2,194},{3,51},{4,196},{5,53},{6,198},{7,55},{8,200... | collective-permute-start | bytes 786440 | tf_op jit(solution)/shard_map/ppermute | solution.py:432
  48.2 3.9 %shard_map.71.fit_ref = bf16[2048,2048]{1,0:T(8,128)(2,1)S(1)} custom-call(s32[4]{0:T(128)S(1)} %pad_add_fusion.meta_ref.ids_ref, bf16[2048,2048]{1,0:T(8,128)(2,1)} %fit_ref), custom_call_target="tpu_custom_call" | custom-call | tf_op jit(solution)/shard_map/pallas_call | solution.py:96
  52.2 4.3 %shard_map.72 = (bf16[256,256]{1,0:T(8,128)(2,1)S(1)}, bf16[256,2048]{1,0:T(8,128)(2,1)S(1)}) custom-call(s32[4]{0:T(128)S(1)} %pad_add_fusion.meta_ref.ids_ref, s32[4,1,64]{2,1,0:T(1,128)S(1)} %copy-done.5, bf16[2048,256]{1,0:T(8,128)(2,1)S(1)} %copy-done.1, bf16[2048,2048]{1,0:T(8,128)(2,1)S(1)} %shard_map.71.fit_ref), custom_call_target="tpu_custom_call" | custom-call | tf_op jit(solution)/shard_map/pallas_call | solution.py:96
  58.1 2.5 %shard_map.68 = (s32[16,256]{1,0:T(8,128)S(1)}, s32[20]{0:T(128)S(1)}) custom-call(s32[4]{0:T(128)S(1)} %pad_add_fusion.meta_ref.ids_ref, s32[4,64]{1,0:T(4,128)S(1)} %copy-done.6), custom_call_target="tpu_custom_call" | custom-call | tf_op jit(solution)/shard_map/pallas_call | solution.py:96
  63.9 5.5 %collective-permute-start.11 = (bf16[128,256]{1,0:T(8,128)(2,1)S(1)}, bf16[128,256]{1,0:T(8,128)(2,1)S(1)}, u32[]{:S(2)}, u32[]{:S(2)}) collective-permute-start(bf16[128,256]{1,0:T(8,128)(2,1)S(1)} %get-tuple-element.52), channel_id=1, source_target_pairs={{0,1},{1,0},{2,3},{3,2},{4,5},{5,4},{6,7},{7,6},{8,9},{9,8},{10,11... | collective-permute-start | bytes 196616 | tf_op jit(solution)/shard_map/ppermute | solution.py:465
  70.9 2.8 %collective-permute-done.12.far_ref = bf16[64,256]{1,0:T(8,128)(2,1)S(1)} collective-permute-done((bf16[64,256]{1,0:T(8,128)(2,1)S(1)}, bf16[64,256]{1,0:T(8,128)(2,1)S(1)}, u32[]{:S(2)}, u32[]{:S(2)}) %collective-permute-start.12) | collective-permute-done | bytes 32800 | tf_op jit(solution)/shard_map/ppermute | solution.py:466
  78.4 3.0 %collective-permute-done.19.refs_2_ = bf16[64,256]{1,0:T(8,128)(2,1)S(1)} collective-permute-done((bf16[64,256]{1,0:T(8,128)(2,1)S(1)}, bf16[64,256]{1,0:T(8,128)(2,1)S(1)}, u32[]{:S(2)}, u32[]{:S(2)}) %collective-permute-start.19) | collective-permute-done | bytes 32800 | tf_op jit(solution)/shard_map/ppermute | solution.py:417
  83.9 2.3 %collective-permute-done.21.refs_1_ = bf16[256,256]{1,0:T(8,128)(2,1)S(1)} collective-permute-done((bf16[256,256]{1,0:T(8,128)(2,1)S(1)}, bf16[256,256]{1,0:T(8,128)(2,1)S(1)}, u32[]{:S(2)}, u32[]{:S(2)}) %collective-permute-start.21) | collective-permute-done | bytes 131104 | tf_op jit(solution)/shard_map/ppermute | solution.py:422
  91.4 4.0 %shard_map.77 = (bf16[1024,2048]{1,0:T(8,128)(2,1)S(1)}, f32[1024,128]{1,0:T(8,128)S(1)}, bf16[1024,128]{1,0:T(8,128)(2,1)S(1)}) custom-call(s32[20]{0:T(128)S(1)} %get-tuple-element.41.meta_ref, bf16[2048,256]{1,0:T(8,128)(2,1)S(1)} %get-tuple-element.58.psi_ref, bf16[2048,256]{1,0:T(8,128)(2,1)S(1)} %copy-done.1, bf16[2048,2048]{1,0:T(8,128)(2,1)S(1)} %shard_map.71.fit_ref), custom_call_target="tpu_custom_call" | custom-call | tf_op jit(solution)/shard_map/pallas_call | solution.py:96
  95.4 5.9 %collective-permute-start.14 = (bf16[1024,128]{1,0:T(8,128)(2,1)S(1)}, bf16[1024,128]{1,0:T(8,128)(2,1)S(1)}, u32[]{:S(2)}, u32[]{:S(2)}) collective-permute-start(bf16[1024,128]{1,0:T(8,128)(2,1)S(1)} %get-tuple-element.60), channel_id=1, source_target_pairs={{0,1},{1,0},{2,3},{3,2},{4,5},{5,4},{6,7},{7,6},{8,9},{9,8},{10,11... | collective-permute-start | bytes 786440 | tf_op jit(solution)/shard_map/ppermute | solution.py:474
  101.9 2.5 %collective-permute-start.26 = (bf16[512,256]{1,0:T(8,128)(2,1)S(1)}, bf16[512,256]{1,0:T(8,128)(2,1)S(1)}, u32[]{:S(2)}, u32[]{:S(2)}) collective-permute-start(bf16[512,256]{1,0:T(8,128)(2,1)S(1)} %get-tuple-element.61), channel_id=1, source_target_pairs={{0,192},{1,49},{2,194},{3,51},{4,196},{5,53},{6,198},{7,55},{8,200... | collective-permute-start | bytes 786440 | tf_op jit(solution)/shard_map/ppermute | solution.py:432
  104.4 4.0 %shard_map.76 = (bf16[1024,2048]{1,0:T(8,128)(2,1)S(1)}, f32[1024,128]{1,0:T(8,128)S(1)}, bf16[1024,128]{1,0:T(8,128)(2,1)S(1)}) custom-call(s32[20]{0:T(128)S(1)} %get-tuple-element.41.meta_ref, bf16[2048,256]{1,0:T(8,128)(2,1)S(1)} %get-tuple-element.58.psi_ref, bf16[2048,256]{1,0:T(8,128)(2,1)S(1)} %copy-done.1, bf16[2048,2048]{1,0:T(8,128)(2,1)S(1)} %shard_map.71.fit_ref), custom_call_target="tpu_custom_call" | custom-call | tf_op jit(solution)/shard_map/pallas_call | solution.py:96
  108.4 3.8 %collective-permute-start.13 = (bf16[1024,128]{1,0:T(8,128)(2,1)S(1)}, bf16[1024,128]{1,0:T(8,128)(2,1)S(1)}, u32[]{:S(2)}, u32[]{:S(2)}) collective-permute-start(bf16[1024,128]{1,0:T(8,128)(2,1)S(1)} %get-tuple-element.57), channel_id=1, source_target_pairs={{0,1},{1,0},{2,3},{3,2},{4,5},{5,4},{6,7},{7,6},{8,9},{9,8},{10,11... | collective-permute-start | bytes 786440 | tf_op jit(solution)/shard_map/ppermute | solution.py:478
  117.2 3.6 %collective-permute-done.15.chip_ref = bf16[1024,128]{1,0:T(8,128)(2,1)S(1)} collective-permute-done((bf16[1024,128]{1,0:T(8,128)(2,1)S(1)}, bf16[1024,128]{1,0:T(8,128)(2,1)S(1)}, u32[]{:S(2)}, u32[]{:S(2)}) %collective-permute-start.15) | collective-permute-done | bytes 262176 | tf_op jit(solution)/shard_map/ppermute | solution.py:475
  121.8 4.7 %collective-permute-start.17 = (bf16[1024,128]{1,0:T(8,128)(2,1)S(1)}, bf16[1024,128]{1,0:T(8,128)(2,1)S(1)}, u32[]{:S(2)}, u32[]{:S(2)}) collective-permute-start(bf16[1024,128]{1,0:T(8,128)(2,1)S(1)} %shard_map.79.own_ref.field_ref), channel_id=1, source_target_pairs={{2,4},{3,5},{6,8},{7,9},{10,12},{11,13},{14,16},{15,17},{18,20},{1... | collective-permute-start | bytes 786440 | tf_op jit(solution)/shard_map/ppermute | solution.py:485
  130.5 3.7 %collective-permute-done.17.outer_ref = bf16[1024,128]{1,0:T(8,128)(2,1)S(1)} collective-permute-done((bf16[1024,128]{1,0:T(8,128)(2,1)S(1)}, bf16[1024,128]{1,0:T(8,128)(2,1)S(1)}, u32[]{:S(2)}, u32[]{:S(2)}) %collective-permute-start.17) | collective-permute-done | bytes 262176 | tf_op jit(solution)/shard_map/ppermute | solution.py:485
  135.5 2.8 %collective-permute-done.30.chip_ref = bf16[1024,128]{1,0:T(8,128)(2,1)S(1)} collective-permute-done((bf16[1024,128]{1,0:T(8,128)(2,1)S(1)}, bf16[1024,128]{1,0:T(8,128)(2,1)S(1)}, u32[]{:S(2)}, u32[]{:S(2)}) %collective-permute-start.30) | collective-permute-done | bytes 262176 | tf_op jit(solution)/shard_map/ppermute | solution.py:475
  139.5 6.7 %collective-permute-done.31 = bf16[1024,128]{1,0:T(8,128)(2,1)S(1)} collective-permute-done((bf16[1024,128]{1,0:T(8,128)(2,1)S(1)}, bf16[1024,128]{1,0:T(8,128)(2,1)S(1)}, u32[]{:S(2)}, u32[]{:S(2)}) %collective-permute-start.31) | collective-permute-done | bytes 262176 | tf_op jit(solution)/shard_map/ppermute | solution.py:495
  (88 shorter events, 53.6 us)
Async XLA Ops:
  2.9 10.2 %collective-permute-start.1 = (bf16[64,256]{1,0:T(8,128)(2,1)S(1)}, bf16[64,256]{1,0:T(8,128)(2,1)S(1)}, u32[]{:S(2)}, u32[]{:S(2)}) collective-permute-start(bf16[64,256]{1,0:T(8,128)(2,1)S(1)} %shard_map.64.refs_0_.old_ref), channel_id=1, source_target_pairs={{0,12},{4,0},{8,4},{12,8},{16,28},{20,16},{24,20},{28,24},{32,44},... | collective-permute-start | bytes 98312 | tf_op jit(solution)/shard_map/ppermute | solution.py:417
  9.8 6.7 %collective-permute-start.2 = (bf16[64,256]{1,0:T(8,128)(2,1)S(1)}, bf16[64,256]{1,0:T(8,128)(2,1)S(1)}, u32[]{:S(2)}, u32[]{:S(2)}) collective-permute-start(bf16[64,256]{1,0:T(8,128)(2,1)S(1)} %shard_map.64.refs_0_.old_ref), channel_id=1, source_target_pairs={{0,8},{4,12},{8,0},{12,4},{16,24},{20,28},{24,16},{28,20},{32,40},... | collective-permute-start | bytes 98312 | tf_op jit(solution)/shard_map/ppermute | solution.py:417
  20.2 6.7 %collective-permute-start.6 = (bf16[256,256]{1,0:T(8,128)(2,1)S(1)}, bf16[256,256]{1,0:T(8,128)(2,1)S(1)}, u32[]{:S(2)}, u32[]{:S(2)}) collective-permute-start(bf16[256,256]{1,0:T(8,128)(2,1)S(1)} %shard_map.66.refs_0_), channel_id=1, source_target_pairs={{0,16},{1,65},{2,18},{3,67},{4,20},{5,69},{6,22},{7,71},{8,24},{9,... | collective-permute-start | bytes 393224 | tf_op jit(solution)/shard_map/ppermute | solution.py:422
  27.5 8.4 %collective-permute-start.7 = (bf16[1024,256]{1,0:T(8,128)(2,1)S(1)}, bf16[1024,256]{1,0:T(8,128)(2,1)S(1)}, u32[]{:S(2)}, u32[]{:S(2)}) collective-permute-start(bf16[1024,256]{1,0:T(8,128)(2,1)S(1)} %shard_map.67.line_ref), channel_id=1, source_target_pairs={{0,192},{1,49},{2,194},{3,51},{4,196},{5,53},{6,198},{7,55},{8,200... | collective-permute-start | bytes 1572872 | tf_op jit(solution)/shard_map/ppermute | solution.py:427
  29.7 15.2 %collective-permute-start.8 = (bf16[1024,256]{1,0:T(8,128)(2,1)S(1)}, bf16[1024,256]{1,0:T(8,128)(2,1)S(1)}, u32[]{:S(2)}, u32[]{:S(2)}) collective-permute-start(bf16[1024,256]{1,0:T(8,128)(2,1)S(1)} %shard_map.67.line_ref), channel_id=1, source_target_pairs={{0,64},{1,17},{2,66},{3,19},{4,68},{5,21},{6,70},{7,23},{8,72},{9,... | collective-permute-start | bytes 1572872 | tf_op jit(solution)/shard_map/ppermute | solution.py:427
  29.8 26.7 %collective-permute-start = (bf16[1024,128]{1,0:T(8,128)(2,1)S(1)}, bf16[1024,128]{1,0:T(8,128)(2,1)S(1)}, u32[]{:S(2)}, u32[]{:S(2)}) collective-permute-start(bf16[1024,128]{1,0:T(8,128)(2,1)S(1)} %get-tuple-element.74.own_ref.field_ref.rest_0_), channel_id=1, source_target_pairs={{2,4},{3,5},{6,8},{7,9},{10,12},{11,13},{14,16},{15,17},{18,20},{1... | collective-permute-start | bytes 786440 | tf_op jit(solution)/shard_map/ppermute | solution.py:458
  45.5 16.6 %collective-permute-start.10 = (bf16[512,256]{1,0:T(8,128)(2,1)S(1)}, bf16[512,256]{1,0:T(8,128)(2,1)S(1)}, u32[]{:S(2)}, u32[]{:S(2)}) collective-permute-start(bf16[512,256]{1,0:T(8,128)(2,1)S(1)} %get-tuple-element.44), channel_id=1, source_target_pairs={{0,64},{1,17},{2,66},{3,19},{4,68},{5,21},{6,70},{7,23},{8,72},{9,... | collective-permute-start | bytes 786440 | tf_op jit(solution)/shard_map/ppermute | solution.py:433
  45.5 16.5 %collective-permute-start.9 = (bf16[512,256]{1,0:T(8,128)(2,1)S(1)}, bf16[512,256]{1,0:T(8,128)(2,1)S(1)}, u32[]{:S(2)}, u32[]{:S(2)}) collective-permute-start(bf16[512,256]{1,0:T(8,128)(2,1)S(1)} %get-tuple-element.43), channel_id=1, source_target_pairs={{0,192},{1,49},{2,194},{3,51},{4,196},{5,53},{6,198},{7,55},{8,200... | collective-permute-start | bytes 786440 | tf_op jit(solution)/shard_map/ppermute | solution.py:432
  63.9 6.4 %collective-permute-start.11 = (bf16[128,256]{1,0:T(8,128)(2,1)S(1)}, bf16[128,256]{1,0:T(8,128)(2,1)S(1)}, u32[]{:S(2)}, u32[]{:S(2)}) collective-permute-start(bf16[128,256]{1,0:T(8,128)(2,1)S(1)} %get-tuple-element.52), channel_id=1, source_target_pairs={{0,1},{1,0},{2,3},{3,2},{4,5},{5,4},{6,7},{7,6},{8,9},{9,8},{10,11... | collective-permute-start | bytes 196616 | tf_op jit(solution)/shard_map/ppermute | solution.py:465
  74.3 7.1 %collective-permute-start.19 = (bf16[64,256]{1,0:T(8,128)(2,1)S(1)}, bf16[64,256]{1,0:T(8,128)(2,1)S(1)}, u32[]{:S(2)}, u32[]{:S(2)}) collective-permute-start(bf16[64,256]{1,0:T(8,128)(2,1)S(1)} %shard_map.75.refs_0_), channel_id=1, source_target_pairs={{0,8},{4,12},{8,0},{12,4},{16,24},{20,28},{24,16},{28,20},{32,40},... | collective-permute-start | bytes 98312 | tf_op jit(solution)/shard_map/ppermute | solution.py:417
  74.4 7.4 %collective-permute-start.20 = (bf16[64,256]{1,0:T(8,128)(2,1)S(1)}, bf16[64,256]{1,0:T(8,128)(2,1)S(1)}, u32[]{:S(2)}, u32[]{:S(2)}) collective-permute-start(bf16[64,256]{1,0:T(8,128)(2,1)S(1)} %shard_map.75.refs_0_), channel_id=1, source_target_pairs={{0,4},{4,8},{8,12},{12,0},{16,20},{20,24},{24,28},{28,16},{32,36},... | collective-permute-start | bytes 98312 | tf_op jit(solution)/shard_map/ppermute | solution.py:417
  89.8 11.4 %collective-permute-start.24 = (bf16[1024,256]{1,0:T(8,128)(2,1)S(1)}, bf16[1024,256]{1,0:T(8,128)(2,1)S(1)}, u32[]{:S(2)}, u32[]{:S(2)}) collective-permute-start(bf16[1024,256]{1,0:T(8,128)(2,1)S(1)} %shard_map.82.line_ref), channel_id=1, source_target_pairs={{0,192},{1,49},{2,194},{3,51},{4,196},{5,53},{6,198},{7,55},{8,200... | collective-permute-start | bytes 1572872 | tf_op jit(solution)/shard_map/ppermute | solution.py:427
  89.9 11.4 %collective-permute-start.25 = (bf16[1024,256]{1,0:T(8,128)(2,1)S(1)}, bf16[1024,256]{1,0:T(8,128)(2,1)S(1)}, u32[]{:S(2)}, u32[]{:S(2)}) collective-permute-start(bf16[1024,256]{1,0:T(8,128)(2,1)S(1)} %shard_map.82.line_ref), channel_id=1, source_target_pairs={{0,64},{1,17},{2,66},{3,19},{4,68},{5,21},{6,70},{7,23},{8,72},{9,... | collective-permute-start | bytes 1572872 | tf_op jit(solution)/shard_map/ppermute | solution.py:427
  95.4 16.8 %collective-permute-start.14 = (bf16[1024,128]{1,0:T(8,128)(2,1)S(1)}, bf16[1024,128]{1,0:T(8,128)(2,1)S(1)}, u32[]{:S(2)}, u32[]{:S(2)}) collective-permute-start(bf16[1024,128]{1,0:T(8,128)(2,1)S(1)} %get-tuple-element.60), channel_id=1, source_target_pairs={{0,1},{1,0},{2,3},{3,2},{4,5},{5,4},{6,7},{7,6},{8,9},{9,8},{10,11... | collective-permute-start | bytes 786440 | tf_op jit(solution)/shard_map/ppermute | solution.py:474
  101.9 12.4 %collective-permute-start.26 = (bf16[512,256]{1,0:T(8,128)(2,1)S(1)}, bf16[512,256]{1,0:T(8,128)(2,1)S(1)}, u32[]{:S(2)}, u32[]{:S(2)}) collective-permute-start(bf16[512,256]{1,0:T(8,128)(2,1)S(1)} %get-tuple-element.61), channel_id=1, source_target_pairs={{0,192},{1,49},{2,194},{3,51},{4,196},{5,53},{6,198},{7,55},{8,200... | collective-permute-start | bytes 786440 | tf_op jit(solution)/shard_map/ppermute | solution.py:432
  104.4 9.8 %collective-permute-start.27 = (bf16[512,256]{1,0:T(8,128)(2,1)S(1)}, bf16[512,256]{1,0:T(8,128)(2,1)S(1)}, u32[]{:S(2)}, u32[]{:S(2)}) collective-permute-start(bf16[512,256]{1,0:T(8,128)(2,1)S(1)} %get-tuple-element.62), channel_id=1, source_target_pairs={{0,64},{1,17},{2,66},{3,19},{4,68},{5,21},{6,70},{7,23},{8,72},{9,... | collective-permute-start | bytes 786440 | tf_op jit(solution)/shard_map/ppermute | solution.py:433
  108.4 8.7 %collective-permute-start.13 = (bf16[1024,128]{1,0:T(8,128)(2,1)S(1)}, bf16[1024,128]{1,0:T(8,128)(2,1)S(1)}, u32[]{:S(2)}, u32[]{:S(2)}) collective-permute-start(bf16[1024,128]{1,0:T(8,128)(2,1)S(1)} %get-tuple-element.57), channel_id=1, source_target_pairs={{0,1},{1,0},{2,3},{3,2},{4,5},{5,4},{6,7},{7,6},{8,9},{9,8},{10,11... | collective-permute-start | bytes 786440 | tf_op jit(solution)/shard_map/ppermute | solution.py:478
  112.8 7.9 %collective-permute-start.15 = (bf16[1024,128]{1,0:T(8,128)(2,1)S(1)}, bf16[1024,128]{1,0:T(8,128)(2,1)S(1)}, u32[]{:S(2)}, u32[]{:S(2)}) collective-permute-start(bf16[1024,128]{1,0:T(8,128)(2,1)S(1)} %shard_map.78), channel_id=1, source_target_pairs={{0,2},{1,3},{2,0},{3,1},{4,6},{5,7},{6,4},{7,5},{8,10},{9,11},{10,... | collective-permute-start | bytes 786440 | tf_op jit(solution)/shard_map/ppermute | solution.py:475
  117.1 12.8 %collective-permute-start.29 = (bf16[1024,128]{1,0:T(8,128)(2,1)S(1)}, bf16[1024,128]{1,0:T(8,128)(2,1)S(1)}, u32[]{:S(2)}, u32[]{:S(2)}) collective-permute-start(bf16[1024,128]{1,0:T(8,128)(2,1)S(1)} %get-tuple-element.70), channel_id=1, source_target_pairs={{0,1},{1,0},{2,3},{3,2},{4,5},{5,4},{6,7},{7,6},{8,9},{9,8},{10,11... | collective-permute-start | bytes 786440 | tf_op jit(solution)/shard_map/ppermute | solution.py:474
  121.4 9.1 %collective-permute-start.16 = (bf16[1024,128]{1,0:T(8,128)(2,1)S(1)}, bf16[1024,128]{1,0:T(8,128)(2,1)S(1)}, u32[]{:S(2)}, u32[]{:S(2)}) collective-permute-start(bf16[1024,128]{1,0:T(8,128)(2,1)S(1)} %shard_map.79.own_ref.field_ref), channel_id=1, source_target_pairs={{0,2},{1,3},{2,0},{3,1},{4,6},{5,7},{6,4},{7,5},{8,10},{9,11},{10,... | collective-permute-start | bytes 786440 | tf_op jit(solution)/shard_map/ppermute | solution.py:484
  121.8 12.4 %collective-permute-start.17 = (bf16[1024,128]{1,0:T(8,128)(2,1)S(1)}, bf16[1024,128]{1,0:T(8,128)(2,1)S(1)}, u32[]{:S(2)}, u32[]{:S(2)}) collective-permute-start(bf16[1024,128]{1,0:T(8,128)(2,1)S(1)} %shard_map.79.own_ref.field_ref), channel_id=1, source_target_pairs={{2,4},{3,5},{6,8},{7,9},{10,12},{11,13},{14,16},{15,17},{18,20},{1... | collective-permute-start | bytes 786440 | tf_op jit(solution)/shard_map/ppermute | solution.py:485
  128.3 7.2 %collective-permute-start.28 = (bf16[1024,128]{1,0:T(8,128)(2,1)S(1)}, bf16[1024,128]{1,0:T(8,128)(2,1)S(1)}, u32[]{:S(2)}, u32[]{:S(2)}) collective-permute-start(bf16[1024,128]{1,0:T(8,128)(2,1)S(1)} %get-tuple-element.69), channel_id=1, source_target_pairs={{0,1},{1,0},{2,3},{3,2},{4,5},{5,4},{6,7},{7,6},{8,9},{9,8},{10,11... | collective-permute-start | bytes 786440 | tf_op jit(solution)/shard_map/ppermute | solution.py:478
  130.4 7.9 %collective-permute-start.30 = (bf16[1024,128]{1,0:T(8,128)(2,1)S(1)}, bf16[1024,128]{1,0:T(8,128)(2,1)S(1)}, u32[]{:S(2)}, u32[]{:S(2)}) collective-permute-start(bf16[1024,128]{1,0:T(8,128)(2,1)S(1)} %shard_map.88), channel_id=1, source_target_pairs={{0,2},{1,3},{2,0},{3,1},{4,6},{5,7},{6,4},{7,5},{8,10},{9,11},{10,... | collective-permute-start | bytes 786440 | tf_op jit(solution)/shard_map/ppermute | solution.py:475
  139.1 7.1 %collective-permute-start.31 = (bf16[1024,128]{1,0:T(8,128)(2,1)S(1)}, bf16[1024,128]{1,0:T(8,128)(2,1)S(1)}, u32[]{:S(2)}, u32[]{:S(2)}) collective-permute-start(bf16[1024,128]{1,0:T(8,128)(2,1)S(1)} %shard_map.89), channel_id=1, source_target_pairs={{0,2},{1,3},{2,0},{3,1},{4,6},{5,7},{6,4},{7,5},{8,10},{9,11},{10,... | collective-permute-start | bytes 786440 | tf_op jit(solution)/shard_map/ppermute | solution.py:495
  (16 other events, 91.4 us)

commit v4 on v3

--- a/solution.py
+++ b/solution.py
@@ -161,17 +161,21 @@
     )
 
 
-def pick_own_kernel(meta_ref, rows_ref, field_ref, out_ref):
+def pick_own_kernel(meta_ref, rows_ref, field_ref, out_ref, own_ref, inner_ref):
+    core = meta_ref[1]
     hot = selection(as_column(rows_ref[0]), 0, ROWS)
     out_ref[...] = jnp.dot(hot, field_ref[...], preferred_element_type=F32).astype(BF)
+    for half, ref in ((meta_ref[2], own_ref), (1 - meta_ref[2], inner_ref)):
+        block = field_ref[pl.ds(pl.multiple_of(half * SHARE, SHARE), SHARE), :]
+        ref[...] = jnp.where(core == 0, block[:, :HALF], block[:, HALF:])
 
 
 def pick_own(meta, rows, field):
     return call(
-        pick_own_kernel, meta, (rows, field),
+        pick_own_kernel, meta, (far_away(rows), far_away(field)),
         [pl.BlockSpec((1, 1, CAP), lambda i, m: (m[0], 0, 0)), pl.BlockSpec((ROWS, NB), lambda i, m: (0, 0))],
-        [array((CAP, NB), BF)],
-    )[0]
+        [array((CAP, NB), BF), array((SHARE, HALF), BF), array((SHARE, HALF), BF)],
+    )
 
 
 def pick_all_kernel(meta_ref, rows_ref, field_ref, fit_ref, orb_out, fit_out, hot_ref):
@@ -227,7 +231,7 @@
 
 def place(meta_ref, where_ref, sum_ref, group, rows):
     line = lax.broadcasted_iota(jnp.int32, (WIN, TILE), 0)
-    hot = jnp.where(where_ref[group : group + 1, :] == line, 1.0, 0.0).astype(BF)
+    hot = jnp.where(where_ref[pl.ds(group, 1), :] == line, 1.0, 0.0).astype(BF)
     at = pl.multiple_of(meta_ref[4 + group], 8)
     sum_ref[pl.ds(at, WIN), :] += jnp.dot(hot, rows, preferred_element_type=F32)
 
@@ -235,8 +239,12 @@
 def place_early_kernel(meta_ref, where_ref, line_ref, up_ref, down_ref, sum_ref):
     sum_ref[...] = jnp.zeros_like(sum_ref)
     for part, ref in ((0, line_ref), (1, up_ref), (3, down_ref)):
-        for e in range(4):
-            place(meta_ref, where_ref, sum_ref, part * 4 + e, ref[pl.ds(e * TILE, TILE), :])
+        def step(e, carry):
+            rows = ref[pl.ds(pl.multiple_of(e * TILE, TILE), TILE), :]
+            place(meta_ref, where_ref, sum_ref, part * 4 + e, rows)
+            return carry
+
+        lax.fori_loop(0, 4, step, 0)
 
 
 def place_early(meta, where, line, up, down):
@@ -370,17 +378,24 @@
     )
 
 
-def apply_kernel(meta_ref, psi_ref, kern_ref, keep_ref, send_ref):
-    for step in range(4):
-        at = pl.ds(step * TILE, TILE)
-        part = -jnp.dot(kern_ref[at, :], psi_ref[...], preferred_element_type=F32)
-        emit(meta_ref, part, keep_ref, send_ref, at)
-
-
-def apply(meta, psi, kern):
-    return call(
-        apply_kernel, meta, (psi, kern), [VMEM, VMEM],
-        [array((SHARE, HALF), F32), array((SHARE, HALF), BF)],
+def apply_with(first, count):
+    def apply_kernel(meta_ref, psi_ref, kern_ref, keep_ref, send_ref):
+        def rows(step, carry):
+            at = pl.ds(pl.multiple_of((first + step) * TILE, TILE), TILE)
+            part = -jnp.dot(kern_ref[at, :], psi_ref[...], preferred_element_type=F32)
+            emit(meta_ref, part, keep_ref, send_ref, pl.ds(pl.multiple_of(step * TILE, TILE), TILE))
+            return carry
+
+        lax.fori_loop(0, count, rows, 0)
+
+    return apply_kernel
+
+
+def apply(meta, psi, kern, first, count):
+    rows = count * TILE
+    return call(
+        apply_with(first, count), meta, (psi, kern), [VMEM, VMEM],
+        [array((rows, HALF), F32), array((rows, HALF), BF)],
     )
 
 
@@ -389,23 +404,49 @@
 
 
 def sum_away(meta, keep, got):
-    return call(sum_kernel, meta, (keep, got), [VMEM] * 2, [array((SHARE, HALF), BF)])[0]
-
-
-def field_kernel(meta_ref, local_ref, keep_ref, core_ref, chip_ref, field_ref, *rest):
-    current = field_ref[...].astype(F32)
-    applied = local_ref[...] + (keep_ref[...] + core_ref[...].astype(F32) + chip_ref[...].astype(F32))
-    scaled = applied - 3.5 * current
-    if len(rest) == 1:
-        rest[0][...] = (scaled / 4.0).astype(BF)
-    else:
-        rest[1][...] = (0.5 * scaled - rest[0][...].astype(F32)).astype(BF)
-
-
-def next_field(meta, local, parts, *fields):
-    return call(
-        field_kernel, meta, (local, *parts, *fields), [VMEM] * (4 + len(fields)),
-        [array((SHARE, HALF), BF)],
+    return call(sum_kernel, meta, (keep, got), [VMEM] * 2, [array(keep.shape, BF)])[0]
+
+
+def field_with(rows):
+    def field_kernel(meta_ref, local_ref, keep_ref, core_ref, chip_ref, field_ref, *rest):
+        current = field_ref[rows, :].astype(F32)
+        reduced = keep_ref[rows, :] + core_ref[rows, :].astype(F32) + chip_ref[...].astype(F32)
+        scaled = local_ref[rows, :] + reduced - 3.5 * current
+        if len(rest) == 1:
+            rest[0][...] = (scaled / 4.0).astype(BF)
+        else:
+            rest[1][...] = (0.5 * scaled - rest[0][rows, :].astype(F32)).astype(BF)
+
+    return field_kernel
+
+
+def next_field(meta, local, parts, fields, first):
+    size = parts[2].shape[0]
+    return call(
+        field_with(pl.ds(first, size)), meta, (local, *parts, *fields), [VMEM] * (4 + len(fields)),
+        [array((size, HALF), BF)],
+    )[0]
+
+
+def assemble_kernel(meta_ref, *refs):
+    out_ref = refs[8]
+    row = pl.program_id(0)
+    first = meta_ref[1] == 0
+    mine = (row // 2) == meta_ref[2]
+    for part in (0, 1):
+        for chunk in (0, 1):
+            @pl.when((mine if part == 0 else jnp.logical_not(mine)) & (row % 2 == chunk))
+            def _():
+                own = refs[part * 4 + chunk][...]
+                theirs = refs[part * 4 + 2 + chunk][...]
+                out_ref[:, :HALF] = jnp.where(first, own, theirs)
+                out_ref[:, HALF:] = jnp.where(first, theirs, own)
+
+
+def assemble(meta, parts):
+    return call(
+        assemble_kernel, meta, parts, [VMEM] * 8, [array((ROWS, NB), BF)],
+        [pl.BlockSpec((512, NB), lambda i, m: (i, 0))], grid=(4,),
     )[0]
 
 
@@ -441,12 +482,8 @@
     chip = point_block // 2
     ids = jnp.stack([point_block, core, chip, slab]).astype(jnp.int32)
     table = split_table()
-    row0 = chip * SHARE
-
-    own0 = pick_own(ids, owner_rows, orbitals)
-    early_orbitals = after(orbitals, own0)
-    field0 = lax.dynamic_slice(early_orbitals, (row0, core * HALF), (SHARE, HALF))
-    inner0 = lax.dynamic_slice(early_orbitals, (SHARE - row0, core * HALF), (SHARE, HALF))
+
+    own0, field0, inner0 = pick_own(ids, owner_rows, orbitals)
     potential_rows = potential.reshape(16, 128)
     column0 = gather_column(ids, own0)
     fit = stage(ids, after(fit_matrix, column0, inner0))
@@ -479,23 +516,28 @@
 
     kern_away, keep, gone = build(meta, after(psi0, far_part), orbitals, fit, True)
     away = send_away(keep, gone)
-    kern_own, keep, gone = build(meta, after(psi0, own1), orbitals, fit, False)
-    field1 = next_field(ids, local0, own_parts(keep, gone, away), field0)
+    kern_own, keep, gone = build(meta, after(psi0, line1), orbitals, fit, False)
+    field1 = next_field(ids, local0, own_parts(keep, gone, away), (field0,), 0)
     inner1 = lax.ppermute(field1, "pt", CHIP_SWAP)
     outer1 = lax.ppermute(field1, BOTH, EDGE_SWAP)
     local1 = stencil(ids, owner_rows, field1, inner1, outer1, potential_rows, table, False)[0]
 
     early1 = place_early(meta, where, line1, up1, down1)
     psi1 = finish_points(meta, where, left1, right1, early1)
-    keep, gone = apply(meta, psi1, kern_away)
-    away = send_away(keep, gone)
-    keep, gone = apply(meta, after(psi1, keep), kern_own)
-    field2 = next_field(ids, local1, own_parts(keep, gone, away), field1, field0)
-
-    other = lax.ppermute(field2, "pt", CHIP_SWAP)
-    column = jnp.concatenate([jnp.where(chip == 0, field2, other), jnp.where(chip == 0, other, field2)], axis=0)
-    other = lax.ppermute(column, "pt", CORE_SWAP)
-    return jnp.concatenate([jnp.where(core == 0, column, other), jnp.where(core == 0, other, column)], axis=1)
+    keep_a, gone_a = apply(meta, psi1, kern_away, 0, 2)
+    keep_b, gone_b = apply(meta, after(psi1, keep_a), kern_away, 2, 2)
+    away_a = send_away(keep_a, gone_a)
+    away_b = send_away(keep_b, gone_b)
+    keep, gone = apply(meta, after(psi1, keep_b), kern_own, 0, 4)
+    got = lax.ppermute(gone, "pt", CORE_SWAP)
+    mine, theirs = [], []
+    for n, away in enumerate((away_a, away_b)):
+        field2 = next_field(ids, local1, (keep, got, away), (field1, field0), 512 * n)
+        other = lax.ppermute(field2, "pt", CHIP_SWAP)
+        mine += [field2, lax.ppermute(field2, "pt", CORE_SWAP)]
+        theirs += [other, lax.ppermute(other, "pt", CORE_SWAP)]
+    parts = [mine[0], mine[2], mine[1], mine[3], theirs[0], theirs[2], theirs[1], theirs[3]]
+    return assemble(ids, parts)
 
 
 def solution(mesh):

time: 151 us -> 151 us (level)
  Pallas kernels: 38.8 us -> 48.3 us
  waiting for transfers between devices: 53.5 us -> 45.4 us
  local copies, waits for them, and re-layouts: 1.97 us -> 0.03 us
  starting transfers between devices: 54.9 us -> 56.7 us
    pallas_call x26 -> x30, Pallas kernels: 38.8 us -> 48.3 us  [call(): pl.pallas_call(kernel, grid_spec=pltpu.PrefetchScalarGridSpec(num_scalar_...]
    ppermute x1 -> x2, waiting for transfers between devices: 6.7 us -> 0.99 us  [body(): other = lax.ppermute(field2, 'pt', CHIP_SWAP)]
    ppermute x2 -> x1, starting transfers between devices: 5.28 us -> 0.1 us  [own_parts(): return (keep, lax.ppermute(gone, 'pt', CORE_SWAP), away)]
    ppermute x1, waiting for transfers between devices: 3.69 us -> 0.01 us  [body(): outer1 = lax.ppermute(field1, BOTH, EDGE_SWAP)]
    ppermute x1 -> x5, starting transfers between devices: 1.82 us -> 5.3 us  [the longest x2 4.01 us: body(): theirs += [other, lax.ppermute(other, 'pt', CORE_SWAP)]]
    ppermute x2 -> x3, starting transfers between devices: 5.98 us -> 8.09 us  [send_away(): total = sum_away(ids, keep, lax.ppermute(gone, 'pt', CORE_SWAP))]
    unnamed x14 -> x10, local copies, waits for them, and re-layouts: 1.93 us -> 0.03 us
    ppermute x2 -> x3, waiting for transfers between devices: 6.38 us -> 7.55 us  [send_away(): return lax.ppermute(total, 'pt', CHIP_SWAP)]
  transfers between devices with their start and end apart: 33 -> 39, of which waited for: 19 -> 20; matrix products, arithmetic and copies ran while one was open for 0% -> 0% of each run, Pallas kernels for 21% -> 26%
where the time goes in v4:
time: 151 us
  starting transfers between devices  56.7 us (38%)
  Pallas kernels  48.3 us (32%)
  waiting for transfers between devices  45.4 us (30%)
    pallas_call x30, Pallas kernels, call(): pl.pallas_call(kernel, grid_spec=pltpu.PrefetchScalarGridSpec(num_scalar_...  48.3 us
    ppermute x6, starting transfers between devices, gather_column(): parts = [own] + [lax.ppermute(own, 'slab', z_shift(d)) for d in (1, 2, 3)]  12.6 us
    ppermute x6, waiting for transfers between devices, gather_line(): lax.ppermute(column, BOTH, plane_shift(d, False))  11.3 us
    ppermute x2, waiting for transfers between devices, gather_sides(): lax.ppermute(line, BOTH, plane_shift(-1, True))  9.02 us
    ppermute x6, waiting for transfers between devices, gather_column(): parts = [own] + [lax.ppermute(own, 'slab', z_shift(d)) for d in (1, 2, 3)]  8.55 us
    ppermute x3, starting transfers between devices, send_away(): total = sum_away(ids, keep, lax.ppermute(gone, 'pt', CORE_SWAP))  8.09 us
    ppermute x3, waiting for transfers between devices, send_away(): return lax.ppermute(total, 'pt', CHIP_SWAP)  7.55 us
    ppermute x1, starting transfers between devices, body(): lax.ppermute(gone, 'pt', CORE_SWAP)  5.54 us
  transfers between devices with their start and end apart: 39, of which 20 were waited for; matrix products, arithmetic and copies ran while one was open for 0% of the time, Pallas kernels for 26%

profile of v4, /device:TPU:1, one launch (start us, length us, event | category | flops | bytes accessed | tf_op | source)
XLA Modules:
  0.0 150.8 jit_solution(8426754141535214465)
XLA Ops:
  2.3 6.9 %collective-permute-start.1 = (bf16[64,256]{1,0:T(8,128)(2,1)S(1)}, bf16[64,256]{1,0:T(8,128)(2,1)S(1)}, u32[]{:S(2)}, u32[]{:S(2)}) collective-permute-start(bf16[64,256]{1,0:T(8,128)(2,1)S(1)} %get-tuple-element.46.refs_0_.old_ref), channel_id=1, source_target_pairs={{0,12},{4,0},{8,4},{12,8},{16,28},{20,16},{24,20},{28,24},{32,44},... | collective-permute-start | bytes 98312 | tf_op jit(solution)/shard_map/ppermute | solution.py:458
  12.5 3.4 %collective-permute-done.2.refs_2_ = bf16[64,256]{1,0:T(8,128)(2,1)S(1)} collective-permute-done((bf16[64,256]{1,0:T(8,128)(2,1)S(1)}, bf16[64,256]{1,0:T(8,128)(2,1)S(1)}, u32[]{:S(2)}, u32[]{:S(2)}) %collective-permute-start.2) | collective-permute-done | bytes 32800 | tf_op jit(solution)/shard_map/ppermute | solution.py:458
  16.5 2.8 %collective-permute-start.4 = (bf16[256,256]{1,0:T(8,128)(2,1)S(1)}, bf16[256,256]{1,0:T(8,128)(2,1)S(1)}, u32[]{:S(2)}, u32[]{:S(2)}) collective-permute-start(bf16[256,256]{1,0:T(8,128)(2,1)S(1)} %shard_map.66.refs_0_), channel_id=1, source_target_pairs={{0,48},{1,193},{2,50},{3,195},{4,52},{5,197},{6,54},{7,199},{8,56}... | collective-permute-start | bytes 393224 | tf_op jit(solution)/shard_map/ppermute | solution.py:463
  29.2 3.4 %collective-permute-start = (bf16[1024,128]{1,0:T(8,128)(2,1)S(1)}, bf16[1024,128]{1,0:T(8,128)(2,1)S(1)}, u32[]{:S(2)}, u32[]{:S(2)}) collective-permute-start(bf16[1024,128]{1,0:T(8,128)(2,1)S(1)} %get-tuple-element.43.own_ref.field_ref.rest_0_), channel_id=1, source_target_pairs={{2,4},{3,5},{6,8},{7,9},{10,12},{11,13},{14,16},{15,17},{18,20},{1... | collective-permute-start | bytes 786440 | tf_op jit(solution)/shard_map/ppermute | solution.py:495
  32.6 2.7 %collective-permute-done.7.up_ref = bf16[1024,256]{1,0:T(8,128)(2,1)S(1)} collective-permute-done((bf16[1024,256]{1,0:T(8,128)(2,1)S(1)}, bf16[1024,256]{1,0:T(8,128)(2,1)S(1)}, u32[]{:S(2)}, u32[]{:S(2)}) %collective-permute-start.7) | collective-permute-done | bytes 524320 | tf_op jit(solution)/shard_map/ppermute | solution.py:468
  35.3 9.0 %collective-permute-done.8.down_ref = bf16[1024,256]{1,0:T(8,128)(2,1)S(1)} collective-permute-done((bf16[1024,256]{1,0:T(8,128)(2,1)S(1)}, bf16[1024,256]{1,0:T(8,128)(2,1)S(1)}, u32[]{:S(2)}, u32[]{:S(2)}) %collective-permute-start.8) | collective-permute-done | bytes 524320 | tf_op jit(solution)/shard_map/ppermute | solution.py:468
  45.0 2.7 %collective-permute-start.9 = (bf16[512,256]{1,0:T(8,128)(2,1)S(1)}, bf16[512,256]{1,0:T(8,128)(2,1)S(1)}, u32[]{:S(2)}, u32[]{:S(2)}) collective-permute-start(bf16[512,256]{1,0:T(8,128)(2,1)S(1)} %get-tuple-element.50), channel_id=1, source_target_pairs={{0,192},{1,49},{2,194},{3,51},{4,196},{5,53},{6,198},{7,55},{8,200... | collective-permute-start | bytes 786440 | tf_op jit(solution)/shard_map/ppermute | solution.py:473
  47.7 3.9 %shard_map.71.fit_ref = bf16[2048,2048]{1,0:T(8,128)(2,1)S(1)} custom-call(s32[4]{0:T(128)S(1)} %pad_add_fusion.meta_ref.ids_ref, bf16[2048,2048]{1,0:T(8,128)(2,1)} %fit_ref), custom_call_target="tpu_custom_call" | custom-call | tf_op jit(solution)/shard_map/pallas_call | solution.py:96
  51.6 4.3 %shard_map.72 = (bf16[256,256]{1,0:T(8,128)(2,1)S(1)}, bf16[256,2048]{1,0:T(8,128)(2,1)S(1)}) custom-call(s32[4]{0:T(128)S(1)} %pad_add_fusion.meta_ref.ids_ref, s32[4,1,64]{2,1,0:T(1,128)S(1)} %copy-done.3, bf16[2048,256]{1,0:T(8,128)(2,1)S(1)} %copy-done, bf16[2048,2048]{1,0:T(8,128)(2,1)S(1)} %shard_map.71.fit_ref), custom_call_target="tpu_custom_call" | custom-call | tf_op jit(solution)/shard_map/pallas_call | solution.py:96
  57.5 2.5 %shard_map.68 = (s32[16,256]{1,0:T(8,128)S(1)}, s32[20]{0:T(128)S(1)}) custom-call(s32[4]{0:T(128)S(1)} %pad_add_fusion.meta_ref.ids_ref, s32[4,64]{1,0:T(4,128)S(1)} %copy-done.4), custom_call_target="tpu_custom_call" | custom-call | tf_op jit(solution)/shard_map/pallas_call | solution.py:96
  60.1 3.1 %shard_map.70.early_ref = f32[2320,256]{1,0:T(8,128)S(1)} custom-call(s32[20]{0:T(128)S(1)} %get-tuple-element.48.meta_ref, s32[16,256]{1,0:T(8,128)S(1)} %get-tuple-element.49.where_ref, bf16[1024,256]{1,0:T(8,128)(2,1)S(1)} %shard_map.67.line_ref, bf16[1024,256]{1,0:T(8,128)(2,1)S(1)} %collective-permute-done.7.up_ref, ...), custom_call_target="tpu_custom_call" | custom-call | tf_op jit(solution)/shard_map/pallas_call | solution.py:96
  65.0 5.5 %collective-permute-start.11 = (bf16[128,256]{1,0:T(8,128)(2,1)S(1)}, bf16[128,256]{1,0:T(8,128)(2,1)S(1)}, u32[]{:S(2)}, u32[]{:S(2)}) collective-permute-start(bf16[128,256]{1,0:T(8,128)(2,1)S(1)} %get-tuple-element.59), channel_id=1, source_target_pairs={{0,1},{1,0},{2,3},{3,2},{4,5},{5,4},{6,7},{7,6},{8,9},{9,8},{10,11... | collective-permute-start | bytes 196616 | tf_op jit(solution)/shard_map/ppermute | solution.py:502
  72.1 2.8 %collective-permute-done.12.far_ref = bf16[64,256]{1,0:T(8,128)(2,1)S(1)} collective-permute-done((bf16[64,256]{1,0:T(8,128)(2,1)S(1)}, bf16[64,256]{1,0:T(8,128)(2,1)S(1)}, u32[]{:S(2)}, u32[]{:S(2)}) %collective-permute-start.12) | collective-permute-done | bytes 32800 | tf_op jit(solution)/shard_map/ppermute | solution.py:503
  79.6 3.0 %collective-permute-done.14.refs_2_ = bf16[64,256]{1,0:T(8,128)(2,1)S(1)} collective-permute-done((bf16[64,256]{1,0:T(8,128)(2,1)S(1)}, bf16[64,256]{1,0:T(8,128)(2,1)S(1)}, u32[]{:S(2)}, u32[]{:S(2)}) %collective-permute-start.14) | collective-permute-done | bytes 32800 | tf_op jit(solution)/shard_map/ppermute | solution.py:458
  85.1 2.3 %collective-permute-done.16.refs_1_ = bf16[256,256]{1,0:T(8,128)(2,1)S(1)} collective-permute-done((bf16[256,256]{1,0:T(8,128)(2,1)S(1)}, bf16[256,256]{1,0:T(8,128)(2,1)S(1)}, u32[]{:S(2)}, u32[]{:S(2)}) %collective-permute-start.16) | collective-permute-done | bytes 131104 | tf_op jit(solution)/shard_map/ppermute | solution.py:463
  92.6 4.0 %shard_map.79 = (bf16[1024,2048]{1,0:T(8,128)(2,1)S(1)}, f32[1024,128]{1,0:T(8,128)S(1)}, bf16[1024,128]{1,0:T(8,128)(2,1)S(1)}) custom-call(s32[20]{0:T(128)S(1)} %get-tuple-element.48.meta_ref, bf16[2048,256]{1,0:T(8,128)(2,1)S(1)} %get-tuple-element.65.psi_ref, bf16[2048,256]{1,0:T(8,128)(2,1)S(1)} %copy-done, bf16[2048,2048]{1,0:T(8,128)(2,1)S(1)} %shard_map.71.fit_ref), custom_call_target="tpu_custom_call" | custom-call | tf_op jit(solution)/shard_map/pallas_call | solution.py:96
  96.6 5.6 %collective-permute-start.20 = (bf16[1024,128]{1,0:T(8,128)(2,1)S(1)}, bf16[1024,128]{1,0:T(8,128)(2,1)S(1)}, u32[]{:S(2)}, u32[]{:S(2)}) collective-permute-start(bf16[1024,128]{1,0:T(8,128)(2,1)S(1)} %get-tuple-element.67), channel_id=1, source_target_pairs={{0,1},{1,0},{2,3},{3,2},{4,5},{5,4},{6,7},{7,6},{8,9},{9,8},{10,11... | collective-permute-start | bytes 786440 | tf_op jit(solution)/shard_map/ppermute | solution.py:511
  102.2 4.0 %shard_map.78 = (bf16[1024,2048]{1,0:T(8,128)(2,1)S(1)}, f32[1024,128]{1,0:T(8,128)S(1)}, bf16[1024,128]{1,0:T(8,128)(2,1)S(1)}) custom-call(s32[20]{0:T(128)S(1)} %get-tuple-element.48.meta_ref, bf16[2048,256]{1,0:T(8,128)(2,1)S(1)} %get-tuple-element.65.psi_ref, bf16[2048,256]{1,0:T(8,128)(2,1)S(1)} %copy-done, bf16[2048,2048]{1,0:T(8,128)(2,1)S(1)} %shard_map.71.fit_ref), custom_call_target="tpu_custom_call" | custom-call | tf_op jit(solution)/shard_map/pallas_call | solution.py:96
  107.6 2.5 %collective-permute-start.26 = (bf16[512,256]{1,0:T(8,128)(2,1)S(1)}, bf16[512,256]{1,0:T(8,128)(2,1)S(1)}, u32[]{:S(2)}, u32[]{:S(2)}) collective-permute-start(bf16[512,256]{1,0:T(8,128)(2,1)S(1)} %get-tuple-element.68), channel_id=1, source_target_pairs={{0,192},{1,49},{2,194},{3,51},{4,196},{5,53},{6,198},{7,55},{8,200... | collective-permute-start | bytes 786440 | tf_op jit(solution)/shard_map/ppermute | solution.py:473
  110.1 4.2 %collective-permute-done.21.chip_ref = bf16[1024,128]{1,0:T(8,128)(2,1)S(1)} collective-permute-done((bf16[1024,128]{1,0:T(8,128)(2,1)S(1)}, bf16[1024,128]{1,0:T(8,128)(2,1)S(1)}, u32[]{:S(2)}, u32[]{:S(2)}) %collective-permute-start.21) | collective-permute-done | bytes 262176 | tf_op jit(solution)/shard_map/ppermute | solution.py:512
  115.4 4.8 %collective-permute-start.23 = (bf16[1024,128]{1,0:T(8,128)(2,1)S(1)}, bf16[1024,128]{1,0:T(8,128)(2,1)S(1)}, u32[]{:S(2)}, u32[]{:S(2)}) collective-permute-start(bf16[1024,128]{1,0:T(8,128)(2,1)S(1)} %shard_map.81.own_ref.field_ref), channel_id=1, source_target_pairs={{2,4},{3,5},{6,8},{7,9},{10,12},{11,13},{14,16},{15,17},{18,20},{1... | collective-permute-start | bytes 786440 | tf_op jit(solution)/shard_map/ppermute | solution.py:522
  120.2 3.1 %shard_map.84.early_ref = f32[2320,256]{1,0:T(8,128)S(1)} custom-call(s32[20]{0:T(128)S(1)} %get-tuple-element.48.meta_ref, s32[16,256]{1,0:T(8,128)S(1)} %get-tuple-element.49.where_ref, bf16[1024,256]{1,0:T(8,128)(2,1)S(1)} %shard_map.77.line_ref, bf16[1024,256]{1,0:T(8,128)(2,1)S(1)} %collective-permute-done.24.up_ref, ...), custom_call_target="tpu_custom_call" | custom-call | tf_op jit(solution)/shard_map/pallas_call | solution.py:96
  129.1 2.3 %shard_map.88 = (f32[1024,128]{1,0:T(8,128)S(1)}, bf16[1024,128]{1,0:T(8,128)(2,1)S(1)}) custom-call(s32[20]{0:T(128)S(1)} %get-tuple-element.48.meta_ref, bf16[2048,256]{1,0:T(8,128)(2,1)S(1)} %get-tuple-element.75.psi_ref, bf16[1024,2048]{1,0:T(8,128)(2,1)S(1)} %get-tuple-element.76.kern_ref), custom_call_target="tpu_custom_call" | custom-call | tf_op jit(solution)/shard_map/pallas_call | solution.py:96
  142.7 2.8 %collective-permute-start.38 = (bf16[512,128]{1,0:T(8,128)(2,1)S(1)}, bf16[512,128]{1,0:T(8,128)(2,1)S(1)}, u32[]{:S(2)}, u32[]{:S(2)}) collective-permute-start(bf16[512,128]{1,0:T(8,128)(2,1)S(1)} %collective-permute-done.36.refs_5_), channel_id=1, source_target_pairs={{0,1},{1,0},{2,3},{3,2},{4,5},{5,4},{6,7},{7,6},{8,9},{9,8},{10,11... | collective-permute-start | bytes 393224 | tf_op jit(solution)/shard_map/ppermute | solution.py:538
  (95 shorter events, 58.8 us)
Async XLA Ops:
  2.3 10.2 %collective-permute-start.1 = (bf16[64,256]{1,0:T(8,128)(2,1)S(1)}, bf16[64,256]{1,0:T(8,128)(2,1)S(1)}, u32[]{:S(2)}, u32[]{:S(2)}) collective-permute-start(bf16[64,256]{1,0:T(8,128)(2,1)S(1)} %get-tuple-element.46.refs_0_.old_ref), channel_id=1, source_target_pairs={{0,12},{4,0},{8,4},{12,8},{16,28},{20,16},{24,20},{28,24},{32,44},... | collective-permute-start | bytes 98312 | tf_op jit(solution)/shard_map/ppermute | solution.py:458
  9.2 6.7 %collective-permute-start.2 = (bf16[64,256]{1,0:T(8,128)(2,1)S(1)}, bf16[64,256]{1,0:T(8,128)(2,1)S(1)}, u32[]{:S(2)}, u32[]{:S(2)}) collective-permute-start(bf16[64,256]{1,0:T(8,128)(2,1)S(1)} %get-tuple-element.46.refs_0_.old_ref), channel_id=1, source_target_pairs={{0,8},{4,12},{8,0},{12,4},{16,24},{20,28},{24,16},{28,20},{32,40},... | collective-permute-start | bytes 98312 | tf_op jit(solution)/shard_map/ppermute | solution.py:458
  10.2 5.7 %collective-permute-start.3 = (bf16[64,256]{1,0:T(8,128)(2,1)S(1)}, bf16[64,256]{1,0:T(8,128)(2,1)S(1)}, u32[]{:S(2)}, u32[]{:S(2)}) collective-permute-start(bf16[64,256]{1,0:T(8,128)(2,1)S(1)} %get-tuple-element.46.refs_0_.old_ref), channel_id=1, source_target_pairs={{0,4},{4,8},{8,12},{12,0},{16,20},{20,24},{24,28},{28,16},{32,36},... | collective-permute-start | bytes 98312 | tf_op jit(solution)/shard_map/ppermute | solution.py:458
  16.5 6.1 %collective-permute-start.4 = (bf16[256,256]{1,0:T(8,128)(2,1)S(1)}, bf16[256,256]{1,0:T(8,128)(2,1)S(1)}, u32[]{:S(2)}, u32[]{:S(2)}) collective-permute-start(bf16[256,256]{1,0:T(8,128)(2,1)S(1)} %shard_map.66.refs_0_), channel_id=1, source_target_pairs={{0,48},{1,193},{2,50},{3,195},{4,52},{5,197},{6,54},{7,199},{8,56}... | collective-permute-start | bytes 393224 | tf_op jit(solution)/shard_map/ppermute | solution.py:463
  19.6 6.7 %collective-permute-start.6 = (bf16[256,256]{1,0:T(8,128)(2,1)S(1)}, bf16[256,256]{1,0:T(8,128)(2,1)S(1)}, u32[]{:S(2)}, u32[]{:S(2)}) collective-permute-start(bf16[256,256]{1,0:T(8,128)(2,1)S(1)} %shard_map.66.refs_0_), channel_id=1, source_target_pairs={{0,16},{1,65},{2,18},{3,67},{4,20},{5,69},{6,22},{7,71},{8,24},{9,... | collective-permute-start | bytes 393224 | tf_op jit(solution)/shard_map/ppermute | solution.py:463
  26.9 8.4 %collective-permute-start.7 = (bf16[1024,256]{1,0:T(8,128)(2,1)S(1)}, bf16[1024,256]{1,0:T(8,128)(2,1)S(1)}, u32[]{:S(2)}, u32[]{:S(2)}) collective-permute-start(bf16[1024,256]{1,0:T(8,128)(2,1)S(1)} %shard_map.67.line_ref), channel_id=1, source_target_pairs={{0,192},{1,49},{2,194},{3,51},{4,196},{5,53},{6,198},{7,55},{8,200... | collective-permute-start | bytes 1572872 | tf_op jit(solution)/shard_map/ppermute | solution.py:468
  29.2 15.2 %collective-permute-start.8 = (bf16[1024,256]{1,0:T(8,128)(2,1)S(1)}, bf16[1024,256]{1,0:T(8,128)(2,1)S(1)}, u32[]{:S(2)}, u32[]{:S(2)}) collective-permute-start(bf16[1024,256]{1,0:T(8,128)(2,1)S(1)} %shard_map.67.line_ref), channel_id=1, source_target_pairs={{0,64},{1,17},{2,66},{3,19},{4,68},{5,21},{6,70},{7,23},{8,72},{9,... | collective-permute-start | bytes 1572872 | tf_op jit(solution)/shard_map/ppermute | solution.py:468
  29.2 26.8 %collective-permute-start = (bf16[1024,128]{1,0:T(8,128)(2,1)S(1)}, bf16[1024,128]{1,0:T(8,128)(2,1)S(1)}, u32[]{:S(2)}, u32[]{:S(2)}) collective-permute-start(bf16[1024,128]{1,0:T(8,128)(2,1)S(1)} %get-tuple-element.43.own_ref.field_ref.rest_0_), channel_id=1, source_target_pairs={{2,4},{3,5},{6,8},{7,9},{10,12},{11,13},{14,16},{15,17},{18,20},{1... | collective-permute-start | bytes 786440 | tf_op jit(solution)/shard_map/ppermute | solution.py:495
  44.9 18.3 %collective-permute-start.10 = (bf16[512,256]{1,0:T(8,128)(2,1)S(1)}, bf16[512,256]{1,0:T(8,128)(2,1)S(1)}, u32[]{:S(2)}, u32[]{:S(2)}) collective-permute-start(bf16[512,256]{1,0:T(8,128)(2,1)S(1)} %get-tuple-element.51), channel_id=1, source_target_pairs={{0,64},{1,17},{2,66},{3,19},{4,68},{5,21},{6,70},{7,23},{8,72},{9,... | collective-permute-start | bytes 786440 | tf_op jit(solution)/shard_map/ppermute | solution.py:474
  45.0 18.2 %collective-permute-start.9 = (bf16[512,256]{1,0:T(8,128)(2,1)S(1)}, bf16[512,256]{1,0:T(8,128)(2,1)S(1)}, u32[]{:S(2)}, u32[]{:S(2)}) collective-permute-start(bf16[512,256]{1,0:T(8,128)(2,1)S(1)} %get-tuple-element.50), channel_id=1, source_target_pairs={{0,192},{1,49},{2,194},{3,51},{4,196},{5,53},{6,198},{7,55},{8,200... | collective-permute-start | bytes 786440 | tf_op jit(solution)/shard_map/ppermute | solution.py:473
  65.0 6.4 %collective-permute-start.11 = (bf16[128,256]{1,0:T(8,128)(2,1)S(1)}, bf16[128,256]{1,0:T(8,128)(2,1)S(1)}, u32[]{:S(2)}, u32[]{:S(2)}) collective-permute-start(bf16[128,256]{1,0:T(8,128)(2,1)S(1)} %get-tuple-element.59), channel_id=1, source_target_pairs={{0,1},{1,0},{2,3},{3,2},{4,5},{5,4},{6,7},{7,6},{8,9},{9,8},{10,11... | collective-permute-start | bytes 196616 | tf_op jit(solution)/shard_map/ppermute | solution.py:502
  75.5 7.1 %collective-permute-start.14 = (bf16[64,256]{1,0:T(8,128)(2,1)S(1)}, bf16[64,256]{1,0:T(8,128)(2,1)S(1)}, u32[]{:S(2)}, u32[]{:S(2)}) collective-permute-start(bf16[64,256]{1,0:T(8,128)(2,1)S(1)} %shard_map.75.refs_0_), channel_id=1, source_target_pairs={{0,8},{4,12},{8,0},{12,4},{16,24},{20,28},{24,16},{28,20},{32,40},... | collective-permute-start | bytes 98312 | tf_op jit(solution)/shard_map/ppermute | solution.py:458
  75.6 7.4 %collective-permute-start.15 = (bf16[64,256]{1,0:T(8,128)(2,1)S(1)}, bf16[64,256]{1,0:T(8,128)(2,1)S(1)}, u32[]{:S(2)}, u32[]{:S(2)}) collective-permute-start(bf16[64,256]{1,0:T(8,128)(2,1)S(1)} %shard_map.75.refs_0_), channel_id=1, source_target_pairs={{0,4},{4,8},{8,12},{12,0},{16,20},{20,24},{24,28},{28,16},{32,36},... | collective-permute-start | bytes 98312 | tf_op jit(solution)/shard_map/ppermute | solution.py:458
  84.0 6.4 %collective-permute-start.18 = (bf16[256,256]{1,0:T(8,128)(2,1)S(1)}, bf16[256,256]{1,0:T(8,128)(2,1)S(1)}, u32[]{:S(2)}, u32[]{:S(2)}) collective-permute-start(bf16[256,256]{1,0:T(8,128)(2,1)S(1)} %shard_map.76.refs_0_), channel_id=1, source_target_pairs={{0,16},{1,65},{2,18},{3,67},{4,20},{5,69},{6,22},{7,71},{8,24},{9,... | collective-permute-start | bytes 393224 | tf_op jit(solution)/shard_map/ppermute | solution.py:463
  91.0 15.9 %collective-permute-start.24 = (bf16[1024,256]{1,0:T(8,128)(2,1)S(1)}, bf16[1024,256]{1,0:T(8,128)(2,1)S(1)}, u32[]{:S(2)}, u32[]{:S(2)}) collective-permute-start(bf16[1024,256]{1,0:T(8,128)(2,1)S(1)} %shard_map.77.line_ref), channel_id=1, source_target_pairs={{0,192},{1,49},{2,194},{3,51},{4,196},{5,53},{6,198},{7,55},{8,200... | collective-permute-start | bytes 1572872 | tf_op jit(solution)/shard_map/ppermute | solution.py:468
  91.1 15.8 %collective-permute-start.25 = (bf16[1024,256]{1,0:T(8,128)(2,1)S(1)}, bf16[1024,256]{1,0:T(8,128)(2,1)S(1)}, u32[]{:S(2)}, u32[]{:S(2)}) collective-permute-start(bf16[1024,256]{1,0:T(8,128)(2,1)S(1)} %shard_map.77.line_ref), channel_id=1, source_target_pairs={{0,64},{1,17},{2,66},{3,19},{4,68},{5,21},{6,70},{7,23},{8,72},{9,... | collective-permute-start | bytes 1572872 | tf_op jit(solution)/shard_map/ppermute | solution.py:468
  96.6 9.7 %collective-permute-start.20 = (bf16[1024,128]{1,0:T(8,128)(2,1)S(1)}, bf16[1024,128]{1,0:T(8,128)(2,1)S(1)}, u32[]{:S(2)}, u32[]{:S(2)}) collective-permute-start(bf16[1024,128]{1,0:T(8,128)(2,1)S(1)} %get-tuple-element.67), channel_id=1, source_target_pairs={{0,1},{1,0},{2,3},{3,2},{4,5},{5,4},{6,7},{7,6},{8,9},{9,8},{10,11... | collective-permute-start | bytes 786440 | tf_op jit(solution)/shard_map/ppermute | solution.py:511
  106.9 7.5 %collective-permute-start.21 = (bf16[1024,128]{1,0:T(8,128)(2,1)S(1)}, bf16[1024,128]{1,0:T(8,128)(2,1)S(1)}, u32[]{:S(2)}, u32[]{:S(2)}) collective-permute-start(bf16[1024,128]{1,0:T(8,128)(2,1)S(1)} %shard_map.80), channel_id=1, source_target_pairs={{0,2},{1,3},{2,0},{3,1},{4,6},{5,7},{6,4},{7,5},{8,10},{9,11},{10,... | collective-permute-start | bytes 786440 | tf_op jit(solution)/shard_map/ppermute | solution.py:512
  107.6 15.7 %collective-permute-start.26 = (bf16[512,256]{1,0:T(8,128)(2,1)S(1)}, bf16[512,256]{1,0:T(8,128)(2,1)S(1)}, u32[]{:S(2)}, u32[]{:S(2)}) collective-permute-start(bf16[512,256]{1,0:T(8,128)(2,1)S(1)} %get-tuple-element.68), channel_id=1, source_target_pairs={{0,192},{1,49},{2,194},{3,51},{4,196},{5,53},{6,198},{7,55},{8,200... | collective-permute-start | bytes 786440 | tf_op jit(solution)/shard_map/ppermute | solution.py:473
  110.1 13.2 %collective-permute-start.27 = (bf16[512,256]{1,0:T(8,128)(2,1)S(1)}, bf16[512,256]{1,0:T(8,128)(2,1)S(1)}, u32[]{:S(2)}, u32[]{:S(2)}) collective-permute-start(bf16[512,256]{1,0:T(8,128)(2,1)S(1)} %get-tuple-element.69), channel_id=1, source_target_pairs={{0,64},{1,17},{2,66},{3,19},{4,68},{5,21},{6,70},{7,23},{8,72},{9,... | collective-permute-start | bytes 786440 | tf_op jit(solution)/shard_map/ppermute | solution.py:474
  115.0 19.8 %collective-permute-start.22 = (bf16[1024,128]{1,0:T(8,128)(2,1)S(1)}, bf16[1024,128]{1,0:T(8,128)(2,1)S(1)}, u32[]{:S(2)}, u32[]{:S(2)}) collective-permute-start(bf16[1024,128]{1,0:T(8,128)(2,1)S(1)} %shard_map.81.own_ref.field_ref), channel_id=1, source_target_pairs={{0,2},{1,3},{2,0},{3,1},{4,6},{5,7},{6,4},{7,5},{8,10},{9,11},{10,... | collective-permute-start | bytes 786440 | tf_op jit(solution)/shard_map/ppermute | solution.py:521
  115.4 19.4 %collective-permute-start.23 = (bf16[1024,128]{1,0:T(8,128)(2,1)S(1)}, bf16[1024,128]{1,0:T(8,128)(2,1)S(1)}, u32[]{:S(2)}, u32[]{:S(2)}) collective-permute-start(bf16[1024,128]{1,0:T(8,128)(2,1)S(1)} %shard_map.81.own_ref.field_ref), channel_id=1, source_target_pairs={{2,4},{3,5},{6,8},{7,9},{10,12},{11,13},{14,16},{15,17},{18,20},{1... | collective-permute-start | bytes 786440 | tf_op jit(solution)/shard_map/ppermute | solution.py:522
  133.8 6.6 %collective-permute-start.30 = (bf16[512,128]{1,0:T(8,128)(2,1)S(1)}, bf16[512,128]{1,0:T(8,128)(2,1)S(1)}, u32[]{:S(2)}, u32[]{:S(2)}) collective-permute-start(bf16[512,128]{1,0:T(8,128)(2,1)S(1)} %shard_map.89), channel_id=1, source_target_pairs={{0,2},{1,3},{2,0},{3,1},{4,6},{5,7},{6,4},{7,5},{8,10},{9,11},{10,... | collective-permute-start | bytes 393224 | tf_op jit(solution)/shard_map/ppermute | solution.py:512
  141.5 6.2 %collective-permute-start.34 = (bf16[512,128]{1,0:T(8,128)(2,1)S(1)}, bf16[512,128]{1,0:T(8,128)(2,1)S(1)}, u32[]{:S(2)}, u32[]{:S(2)}) collective-permute-start(bf16[512,128]{1,0:T(8,128)(2,1)S(1)} %shard_map.92.refs_1_), channel_id=1, source_target_pairs={{0,1},{1,0},{2,3},{3,2},{4,5},{5,4},{6,7},{7,6},{8,9},{9,8},{10,11... | collective-permute-start | bytes 393224 | tf_op jit(solution)/shard_map/ppermute | solution.py:537
  (20 other events, 86.5 us)

commit v5 on v4

--- a/solution.py
+++ b/solution.py
@@ -248,7 +248,10 @@
 
 
 def place_early(meta, where, line, up, down):
-    return call(place_early_kernel, meta, (where, line, up, down), [VMEM] * 4, [array((PTS + WIN, NB), F32)])[0]
+    return call(
+        place_early_kernel, meta, (where, line, up, down),
+        [VMEM] * 4, [array((PTS + WIN, NB), F32)],
+    )[0]
 
 
 def place_late(meta_ref, where_ref, left_ref, right_ref, sum_ref, psi_ref):
@@ -378,15 +381,22 @@
     )
 
 
+def tile_start(step):
+    return step * TILE if isinstance(step, int) else pl.multiple_of(step * TILE, TILE)
+
+
 def apply_with(first, count):
     def apply_kernel(meta_ref, psi_ref, kern_ref, keep_ref, send_ref):
         def rows(step, carry):
-            at = pl.ds(pl.multiple_of((first + step) * TILE, TILE), TILE)
+            at = pl.ds(tile_start(first + step), TILE)
             part = -jnp.dot(kern_ref[at, :], psi_ref[...], preferred_element_type=F32)
-            emit(meta_ref, part, keep_ref, send_ref, pl.ds(pl.multiple_of(step * TILE, TILE), TILE))
+            emit(meta_ref, part, keep_ref, send_ref, pl.ds(tile_start(step), TILE))
             return carry
 
-        lax.fori_loop(0, count, rows, 0)
+        if count == 2:
+            rows(1, rows(0, 0))
+        else:
+            lax.fori_loop(0, count, rows, 0)
 
     return apply_kernel
 
@@ -405,6 +415,21 @@
 
 def sum_away(meta, keep, got):
     return call(sum_kernel, meta, (keep, got), [VMEM] * 2, [array(keep.shape, BF)])[0]
+
+
+def join_field_kernel(meta_ref, local_ref, keep_ref, core_ref, chip_ref, field_ref, old_ref, done_ref, new_ref, whole_ref):
+    field_with(pl.ds(512, 512))(
+        meta_ref, local_ref, keep_ref, core_ref, chip_ref, field_ref, old_ref, new_ref
+    )
+    whole_ref[:512, :] = done_ref[...]
+    whole_ref[512:, :] = new_ref[...]
+
+
+def join_field(meta, local, parts, fields):
+    return call(
+        join_field_kernel, meta, (local, *parts, *fields), [VMEM] * 7,
+        [array((512, HALF), BF), array((SHARE, HALF), BF)],
+    )
 
 
 def field_with(rows):
@@ -428,25 +453,31 @@
     )[0]
 
 
-def assemble_kernel(meta_ref, *refs):
-    out_ref = refs[8]
-    row = pl.program_id(0)
+def put_own_kernel(meta_ref, own_ref, mirror_ref, out_ref):
     first = meta_ref[1] == 0
-    mine = (row // 2) == meta_ref[2]
-    for part in (0, 1):
-        for chunk in (0, 1):
-            @pl.when((mine if part == 0 else jnp.logical_not(mine)) & (row % 2 == chunk))
-            def _():
-                own = refs[part * 4 + chunk][...]
-                theirs = refs[part * 4 + 2 + chunk][...]
-                out_ref[:, :HALF] = jnp.where(first, own, theirs)
-                out_ref[:, HALF:] = jnp.where(first, theirs, own)
-
-
-def assemble(meta, parts):
-    return call(
-        assemble_kernel, meta, parts, [VMEM] * 8, [array((ROWS, NB), BF)],
-        [pl.BlockSpec((512, NB), lambda i, m: (i, 0))], grid=(4,),
+    out_ref[:, :HALF] = jnp.where(first, own_ref[...], mirror_ref[...])
+    out_ref[:, HALF:] = jnp.where(first, mirror_ref[...], own_ref[...])
+
+
+def put_own(meta, own, mirror):
+    return call(
+        put_own_kernel, meta, (own, mirror), [VMEM] * 2, [array((ROWS, NB), BF)],
+        [pl.BlockSpec((SHARE, NB), lambda i, m: (m[2], 0))],
+    )[0]
+
+
+def put_other_kernel(meta_ref, done_ref, own_a, own_b, mirror_a, mirror_b, out_ref):
+    first = meta_ref[1] == 0
+    for n, own, mirror in ((0, own_a, mirror_a), (1, own_b, mirror_b)):
+        at = pl.ds(n * 512, 512)
+        out_ref[at, :HALF] = jnp.where(first, own[...], mirror[...])
+        out_ref[at, HALF:] = jnp.where(first, mirror[...], own[...])
+
+
+def put_other(meta, done, *parts):
+    return call(
+        put_other_kernel, meta, (done, *parts), [HBM] + [VMEM] * 4, [array((ROWS, NB), BF)],
+        [pl.BlockSpec((SHARE, NB), lambda i, m: (1 - m[2], 0))], aliases={1: 0},
     )[0]
 
 
@@ -488,8 +519,8 @@
     column0 = gather_column(ids, own0)
     fit = stage(ids, after(fit_matrix, column0, inner0))
     line0 = gather_line(ids, column0)
+    where, meta = index(ids, after(owner_count, column0))
     up0, down0 = gather_sides(line0)
-    where, meta = index(ids, after(owner_count, up0))
     left0, right0 = gather_far(ids, up0, down0)
 
     outer0 = lax.ppermute(field0, BOTH, EDGE_SWAP)
@@ -530,14 +561,14 @@
     away_b = send_away(keep_b, gone_b)
     keep, gone = apply(meta, after(psi1, keep_b), kern_own, 0, 4)
     got = lax.ppermute(gone, "pt", CORE_SWAP)
-    mine, theirs = [], []
-    for n, away in enumerate((away_a, away_b)):
-        field2 = next_field(ids, local1, (keep, got, away), (field1, field0), 512 * n)
-        other = lax.ppermute(field2, "pt", CHIP_SWAP)
-        mine += [field2, lax.ppermute(field2, "pt", CORE_SWAP)]
-        theirs += [other, lax.ppermute(other, "pt", CORE_SWAP)]
-    parts = [mine[0], mine[2], mine[1], mine[3], theirs[0], theirs[2], theirs[1], theirs[3]]
-    return assemble(ids, parts)
+    new_a = next_field(ids, local1, (keep, got, away_a), (field1, field0), 0)
+    other_a = lax.ppermute(new_a, "pt", CHIP_SWAP)
+    new_b, whole = join_field(ids, local1, (keep, got, away_b), (field1, field0, new_a))
+    other_b = lax.ppermute(new_b, "pt", CHIP_SWAP)
+    out = put_own(ids, whole, lax.ppermute(whole, "pt", CORE_SWAP))
+    mirror_a = lax.ppermute(other_a, "pt", CORE_SWAP)
+    mirror_b = lax.ppermute(other_b, "pt", CORE_SWAP)
+    return put_other(ids, out, other_a, other_b, mirror_a, mirror_b)
 
 
 def solution(mesh):

time: 151 us -> 154 us (1.020)
  waiting for transfers between devices: 45.4 us -> 48.6 us
    ppermute x6 -> x5, waiting for transfers between devices: 1.98 us -> 4.78 us  [the longest x1 3.49 us: body(): other_b = lax.ppermute(new_b, 'pt', CHIP_SWAP)]
    ppermute x6 -> x5, starting transfers between devices: 5.95 us -> 4.99 us  [the longest x1 1.52 us: body(): mirror_b = lax.ppermute(other_b, 'pt', CORE_SWAP)]
    pallas_call x30 -> x31, Pallas kernels: 48.3 us -> 48.7 us  [call(): pl.pallas_call(kernel, grid_spec=pltpu.PrefetchScalarGridSpec(num_scalar_...]
  transfers between devices with their start and end apart: 39 -> 38, of which waited for: 20 -> 20; matrix products, arithmetic and copies ran while one was open for 0% -> 0% of each run, Pallas kernels for 26% -> 25%
where the time goes in v5:
time: 154 us; the launch traced here: 153 us
  starting transfers between devices  55.7 us (36%)
  Pallas kernels  48.7 us (32%)
  waiting for transfers between devices  48.6 us (32%)
    pallas_call x31, Pallas kernels, call(): pl.pallas_call(kernel, grid_spec=pltpu.PrefetchScalarGridSpec(num_scalar_...  48.7 us
    ppermute x6, starting transfers between devices, gather_column(): parts = [own] + [lax.ppermute(own, 'slab', z_shift(d)) for d in (1, 2, 3)]  12.6 us
    ppermute x6, waiting for transfers between devices, gather_line(): lax.ppermute(column, BOTH, plane_shift(d, False))  11.3 us
    ppermute x2, waiting for transfers between devices, gather_sides(): lax.ppermute(line, BOTH, plane_shift(-1, True))  9.02 us
    ppermute x6, waiting for transfers between devices, gather_column(): parts = [own] + [lax.ppermute(own, 'slab', z_shift(d)) for d in (1, 2, 3)]  8.55 us
    ppermute x3, starting transfers between devices, send_away(): total = sum_away(ids, keep, lax.ppermute(gone, 'pt', CORE_SWAP))  8.09 us
    ppermute x3, waiting for transfers between devices, send_away(): return lax.ppermute(total, 'pt', CHIP_SWAP)  7.92 us
    ppermute x1, starting transfers between devices, body(): lax.ppermute(gone, 'pt', CORE_SWAP)  5.54 us
  transfers between devices with their start and end apart: 38, of which 20 were waited for; matrix products, arithmetic and copies ran while one was open for 0% of the time, Pallas kernels for 25%

profile of v5, /device:TPU:1, one launch (start us, length us, event | category | flops | bytes accessed | tf_op | source)
XLA Modules:
  0.0 153.4 jit_solution(565966165873273700)
XLA Ops:
  2.3 6.9 %collective-permute-start.1 = (bf16[64,256]{1,0:T(8,128)(2,1)S(1)}, bf16[64,256]{1,0:T(8,128)(2,1)S(1)}, u32[]{:S(2)}, u32[]{:S(2)}) collective-permute-start(bf16[64,256]{1,0:T(8,128)(2,1)S(1)} %get-tuple-element.48.refs_0_.old_ref), channel_id=1, source_target_pairs={{0,12},{4,0},{8,4},{12,8},{16,28},{20,16},{24,20},{28,24},{32,44},... | collective-permute-start | bytes 98312 | tf_op jit(solution)/shard_map/ppermute | solution.py:489
  12.5 3.4 %collective-permute-done.2.refs_2_ = bf16[64,256]{1,0:T(8,128)(2,1)S(1)} collective-permute-done((bf16[64,256]{1,0:T(8,128)(2,1)S(1)}, bf16[64,256]{1,0:T(8,128)(2,1)S(1)}, u32[]{:S(2)}, u32[]{:S(2)}) %collective-permute-start.2) | collective-permute-done | bytes 32800 | tf_op jit(solution)/shard_map/ppermute | solution.py:489
  16.5 2.8 %collective-permute-start.4 = (bf16[256,256]{1,0:T(8,128)(2,1)S(1)}, bf16[256,256]{1,0:T(8,128)(2,1)S(1)}, u32[]{:S(2)}, u32[]{:S(2)}) collective-permute-start(bf16[256,256]{1,0:T(8,128)(2,1)S(1)} %shard_map.66.refs_0_), channel_id=1, source_target_pairs={{0,48},{1,193},{2,50},{3,195},{4,52},{5,197},{6,54},{7,199},{8,56}... | collective-permute-start | bytes 393224 | tf_op jit(solution)/shard_map/ppermute | solution.py:494
  29.2 3.4 %collective-permute-start = (bf16[1024,128]{1,0:T(8,128)(2,1)S(1)}, bf16[1024,128]{1,0:T(8,128)(2,1)S(1)}, u32[]{:S(2)}, u32[]{:S(2)}) collective-permute-start(bf16[1024,128]{1,0:T(8,128)(2,1)S(1)} %get-tuple-element.45.own_ref.field_ref.rest_0_.old_ref), channel_id=1, source_target_pairs={{2,4},{3,5},{6,8},{7,9},{10,12},{11,13},{14,16},{15,17},{18,20},{1... | collective-permute-start | bytes 786440 | tf_op jit(solution)/shard_map/ppermute | solution.py:526
  32.6 2.7 %collective-permute-done.7.up_ref = bf16[1024,256]{1,0:T(8,128)(2,1)S(1)} collective-permute-done((bf16[1024,256]{1,0:T(8,128)(2,1)S(1)}, bf16[1024,256]{1,0:T(8,128)(2,1)S(1)}, u32[]{:S(2)}, u32[]{:S(2)}) %collective-permute-start.7) | collective-permute-done | bytes 524320 | tf_op jit(solution)/shard_map/ppermute | solution.py:499
  35.3 9.0 %collective-permute-done.8.down_ref = bf16[1024,256]{1,0:T(8,128)(2,1)S(1)} collective-permute-done((bf16[1024,256]{1,0:T(8,128)(2,1)S(1)}, bf16[1024,256]{1,0:T(8,128)(2,1)S(1)}, u32[]{:S(2)}, u32[]{:S(2)}) %collective-permute-start.8) | collective-permute-done | bytes 524320 | tf_op jit(solution)/shard_map/ppermute | solution.py:499
  45.0 2.7 %collective-permute-start.9 = (bf16[512,256]{1,0:T(8,128)(2,1)S(1)}, bf16[512,256]{1,0:T(8,128)(2,1)S(1)}, u32[]{:S(2)}, u32[]{:S(2)}) collective-permute-start(bf16[512,256]{1,0:T(8,128)(2,1)S(1)} %get-tuple-element.52), channel_id=1, source_target_pairs={{0,192},{1,49},{2,194},{3,51},{4,196},{5,53},{6,198},{7,55},{8,200... | collective-permute-start | bytes 786440 | tf_op jit(solution)/shard_map/ppermute | solution.py:504
  47.7 3.9 %shard_map.71.fit_ref = bf16[2048,2048]{1,0:T(8,128)(2,1)S(1)} custom-call(s32[4]{0:T(128)S(1)} %pad_add_fusion.meta_ref.ids_ref, bf16[2048,2048]{1,0:T(8,128)(2,1)} %fit_ref), custom_call_target="tpu_custom_call" | custom-call | tf_op jit(solution)/shard_map/pallas_call | solution.py:96
  51.6 2.5 %shard_map.67 = (s32[16,256]{1,0:T(8,128)S(1)}, s32[20]{0:T(128)S(1)}) custom-call(s32[4]{0:T(128)S(1)} %pad_add_fusion.meta_ref.ids_ref, s32[4,64]{1,0:T(4,128)S(1)} %copy-done.4), custom_call_target="tpu_custom_call" | custom-call | tf_op jit(solution)/shard_map/pallas_call | solution.py:96
  54.2 4.3 %shard_map.72 = (bf16[256,256]{1,0:T(8,128)(2,1)S(1)}, bf16[256,2048]{1,0:T(8,128)(2,1)S(1)}) custom-call(s32[4]{0:T(128)S(1)} %pad_add_fusion.meta_ref.ids_ref, s32[4,1,64]{2,1,0:T(1,128)S(1)} %copy-done.3, bf16[2048,256]{1,0:T(8,128)(2,1)S(1)} %copy-done, bf16[2048,2048]{1,0:T(8,128)(2,1)S(1)} %shard_map.71.fit_ref), custom_call_target="tpu_custom_call" | custom-call | tf_op jit(solution)/shard_map/pallas_call | solution.py:96
  60.1 3.1 %shard_map.70.early_ref = f32[2320,256]{1,0:T(8,128)S(1)} custom-call(s32[20]{0:T(128)S(1)} %get-tuple-element.50.meta_ref, s32[16,256]{1,0:T(8,128)S(1)} %get-tuple-element.51.where_ref, bf16[1024,256]{1,0:T(8,128)(2,1)S(1)} %shard_map.68.line_ref, bf16[1024,256]{1,0:T(8,128)(2,1)S(1)} %collective-permute-done.7.up_ref, ...), custom_call_target="tpu_custom_call" | custom-call | tf_op jit(solution)/shard_map/pallas_call | solution.py:96
  65.0 5.5 %collective-permute-start.11 = (bf16[128,256]{1,0:T(8,128)(2,1)S(1)}, bf16[128,256]{1,0:T(8,128)(2,1)S(1)}, u32[]{:S(2)}, u32[]{:S(2)}) collective-permute-start(bf16[128,256]{1,0:T(8,128)(2,1)S(1)} %get-tuple-element.61), channel_id=1, source_target_pairs={{0,1},{1,0},{2,3},{3,2},{4,5},{5,4},{6,7},{7,6},{8,9},{9,8},{10,11... | collective-permute-start | bytes 196616 | tf_op jit(solution)/shard_map/ppermute | solution.py:533
  72.1 2.8 %collective-permute-done.12.far_ref = bf16[64,256]{1,0:T(8,128)(2,1)S(1)} collective-permute-done((bf16[64,256]{1,0:T(8,128)(2,1)S(1)}, bf16[64,256]{1,0:T(8,128)(2,1)S(1)}, u32[]{:S(2)}, u32[]{:S(2)}) %collective-permute-start.12) | collective-permute-done | bytes 32800 | tf_op jit(solution)/shard_map/ppermute | solution.py:534
  79.6 3.0 %collective-permute-done.14.refs_2_ = bf16[64,256]{1,0:T(8,128)(2,1)S(1)} collective-permute-done((bf16[64,256]{1,0:T(8,128)(2,1)S(1)}, bf16[64,256]{1,0:T(8,128)(2,1)S(1)}, u32[]{:S(2)}, u32[]{:S(2)}) %collective-permute-start.14) | collective-permute-done | bytes 32800 | tf_op jit(solution)/shard_map/ppermute | solution.py:489
  85.1 2.3 %collective-permute-done.16.refs_1_ = bf16[256,256]{1,0:T(8,128)(2,1)S(1)} collective-permute-done((bf16[256,256]{1,0:T(8,128)(2,1)S(1)}, bf16[256,256]{1,0:T(8,128)(2,1)S(1)}, u32[]{:S(2)}, u32[]{:S(2)}) %collective-permute-start.16) | collective-permute-done | bytes 131104 | tf_op jit(solution)/shard_map/ppermute | solution.py:494
  92.6 4.0 %shard_map.79 = (bf16[1024,2048]{1,0:T(8,128)(2,1)S(1)}, f32[1024,128]{1,0:T(8,128)S(1)}, bf16[1024,128]{1,0:T(8,128)(2,1)S(1)}) custom-call(s32[20]{0:T(128)S(1)} %get-tuple-element.50.meta_ref, bf16[2048,256]{1,0:T(8,128)(2,1)S(1)} %get-tuple-element.67.psi_ref, bf16[2048,256]{1,0:T(8,128)(2,1)S(1)} %copy-done, bf16[2048,2048]{1,0:T(8,128)(2,1)S(1)} %shard_map.71.fit_ref), custom_call_target="tpu_custom_call" | custom-call | tf_op jit(solution)/shard_map/pallas_call | solution.py:96
  96.6 5.6 %collective-permute-start.20 = (bf16[1024,128]{1,0:T(8,128)(2,1)S(1)}, bf16[1024,128]{1,0:T(8,128)(2,1)S(1)}, u32[]{:S(2)}, u32[]{:S(2)}) collective-permute-start(bf16[1024,128]{1,0:T(8,128)(2,1)S(1)} %get-tuple-element.69), channel_id=1, source_target_pairs={{0,1},{1,0},{2,3},{3,2},{4,5},{5,4},{6,7},{7,6},{8,9},{9,8},{10,11... | collective-permute-start | bytes 786440 | tf_op jit(solution)/shard_map/ppermute | solution.py:542
  102.2 4.0 %shard_map.78 = (bf16[1024,2048]{1,0:T(8,128)(2,1)S(1)}, f32[1024,128]{1,0:T(8,128)S(1)}, bf16[1024,128]{1,0:T(8,128)(2,1)S(1)}) custom-call(s32[20]{0:T(128)S(1)} %get-tuple-element.50.meta_ref, bf16[2048,256]{1,0:T(8,128)(2,1)S(1)} %get-tuple-element.67.psi_ref, bf16[2048,256]{1,0:T(8,128)(2,1)S(1)} %copy-done, bf16[2048,2048]{1,0:T(8,128)(2,1)S(1)} %shard_map.71.fit_ref), custom_call_target="tpu_custom_call" | custom-call | tf_op jit(solution)/shard_map/pallas_call | solution.py:96
  107.6 2.5 %collective-permute-start.26 = (bf16[512,256]{1,0:T(8,128)(2,1)S(1)}, bf16[512,256]{1,0:T(8,128)(2,1)S(1)}, u32[]{:S(2)}, u32[]{:S(2)}) collective-permute-start(bf16[512,256]{1,0:T(8,128)(2,1)S(1)} %get-tuple-element.70), channel_id=1, source_target_pairs={{0,192},{1,49},{2,194},{3,51},{4,196},{5,53},{6,198},{7,55},{8,200... | collective-permute-start | bytes 786440 | tf_op jit(solution)/shard_map/ppermute | solution.py:504
  110.1 4.2 %collective-permute-done.21.chip_ref = bf16[1024,128]{1,0:T(8,128)(2,1)S(1)} collective-permute-done((bf16[1024,128]{1,0:T(8,128)(2,1)S(1)}, bf16[1024,128]{1,0:T(8,128)(2,1)S(1)}, u32[]{:S(2)}, u32[]{:S(2)}) %collective-permute-start.21) | collective-permute-done | bytes 262176 | tf_op jit(solution)/shard_map/ppermute | solution.py:543
  115.4 4.8 %collective-permute-start.23 = (bf16[1024,128]{1,0:T(8,128)(2,1)S(1)}, bf16[1024,128]{1,0:T(8,128)(2,1)S(1)}, u32[]{:S(2)}, u32[]{:S(2)}) collective-permute-start(bf16[1024,128]{1,0:T(8,128)(2,1)S(1)} %shard_map.81.own_ref.field_ref), channel_id=1, source_target_pairs={{2,4},{3,5},{6,8},{7,9},{10,12},{11,13},{14,16},{15,17},{18,20},{1... | collective-permute-start | bytes 786440 | tf_op jit(solution)/shard_map/ppermute | solution.py:553
  120.2 3.1 %shard_map.84.early_ref = f32[2320,256]{1,0:T(8,128)S(1)} custom-call(s32[20]{0:T(128)S(1)} %get-tuple-element.50.meta_ref, s32[16,256]{1,0:T(8,128)S(1)} %get-tuple-element.51.where_ref, bf16[1024,256]{1,0:T(8,128)(2,1)S(1)} %shard_map.77.line_ref, bf16[1024,256]{1,0:T(8,128)(2,1)S(1)} %collective-permute-done.24.up_ref, ...), custom_call_target="tpu_custom_call" | custom-call | tf_op jit(solution)/shard_map/pallas_call | solution.py:96
  128.7 2.3 %shard_map.88 = (f32[1024,128]{1,0:T(8,128)S(1)}, bf16[1024,128]{1,0:T(8,128)(2,1)S(1)}) custom-call(s32[20]{0:T(128)S(1)} %get-tuple-element.50.meta_ref, bf16[2048,256]{1,0:T(8,128)(2,1)S(1)} %get-tuple-element.77.psi_ref, bf16[1024,2048]{1,0:T(8,128)(2,1)S(1)} %get-tuple-element.78.kern_ref), custom_call_target="tpu_custom_call" | custom-call | tf_op jit(solution)/shard_map/pallas_call | solution.py:96
  143.3 3.5 %collective-permute-done.35.own_b = bf16[512,128]{1,0:T(8,128)(2,1)S(1)} collective-permute-done((bf16[512,128]{1,0:T(8,128)(2,1)S(1)}, bf16[512,128]{1,0:T(8,128)(2,1)S(1)}, u32[]{:S(2)}, u32[]{:S(2)}) %collective-permute-start.35) | collective-permute-done | bytes 131104 | tf_op jit(solution)/shard_map/ppermute | solution.py:567
  (94 shorter events, 60.7 us)
Async XLA Ops:
  2.3 10.2 %collective-permute-start.1 = (bf16[64,256]{1,0:T(8,128)(2,1)S(1)}, bf16[64,256]{1,0:T(8,128)(2,1)S(1)}, u32[]{:S(2)}, u32[]{:S(2)}) collective-permute-start(bf16[64,256]{1,0:T(8,128)(2,1)S(1)} %get-tuple-element.48.refs_0_.old_ref), channel_id=1, source_target_pairs={{0,12},{4,0},{8,4},{12,8},{16,28},{20,16},{24,20},{28,24},{32,44},... | collective-permute-start | bytes 98312 | tf_op jit(solution)/shard_map/ppermute | solution.py:489
  9.2 6.7 %collective-permute-start.2 = (bf16[64,256]{1,0:T(8,128)(2,1)S(1)}, bf16[64,256]{1,0:T(8,128)(2,1)S(1)}, u32[]{:S(2)}, u32[]{:S(2)}) collective-permute-start(bf16[64,256]{1,0:T(8,128)(2,1)S(1)} %get-tuple-element.48.refs_0_.old_ref), channel_id=1, source_target_pairs={{0,8},{4,12},{8,0},{12,4},{16,24},{20,28},{24,16},{28,20},{32,40},... | collective-permute-start | bytes 98312 | tf_op jit(solution)/shard_map/ppermute | solution.py:489
  19.6 6.7 %collective-permute-start.6 = (bf16[256,256]{1,0:T(8,128)(2,1)S(1)}, bf16[256,256]{1,0:T(8,128)(2,1)S(1)}, u32[]{:S(2)}, u32[]{:S(2)}) collective-permute-start(bf16[256,256]{1,0:T(8,128)(2,1)S(1)} %shard_map.66.refs_0_), channel_id=1, source_target_pairs={{0,16},{1,65},{2,18},{3,67},{4,20},{5,69},{6,22},{7,71},{8,24},{9,... | collective-permute-start | bytes 393224 | tf_op jit(solution)/shard_map/ppermute | solution.py:494
  26.9 8.4 %collective-permute-start.7 = (bf16[1024,256]{1,0:T(8,128)(2,1)S(1)}, bf16[1024,256]{1,0:T(8,128)(2,1)S(1)}, u32[]{:S(2)}, u32[]{:S(2)}) collective-permute-start(bf16[1024,256]{1,0:T(8,128)(2,1)S(1)} %shard_map.68.line_ref), channel_id=1, source_target_pairs={{0,192},{1,49},{2,194},{3,51},{4,196},{5,53},{6,198},{7,55},{8,200... | collective-permute-start | bytes 1572872 | tf_op jit(solution)/shard_map/ppermute | solution.py:499
  29.2 15.2 %collective-permute-start.8 = (bf16[1024,256]{1,0:T(8,128)(2,1)S(1)}, bf16[1024,256]{1,0:T(8,128)(2,1)S(1)}, u32[]{:S(2)}, u32[]{:S(2)}) collective-permute-start(bf16[1024,256]{1,0:T(8,128)(2,1)S(1)} %shard_map.68.line_ref), channel_id=1, source_target_pairs={{0,64},{1,17},{2,66},{3,19},{4,68},{5,21},{6,70},{7,23},{8,72},{9,... | collective-permute-start | bytes 1572872 | tf_op jit(solution)/shard_map/ppermute | solution.py:499
  29.2 29.3 %collective-permute-start = (bf16[1024,128]{1,0:T(8,128)(2,1)S(1)}, bf16[1024,128]{1,0:T(8,128)(2,1)S(1)}, u32[]{:S(2)}, u32[]{:S(2)}) collective-permute-start(bf16[1024,128]{1,0:T(8,128)(2,1)S(1)} %get-tuple-element.45.own_ref.field_ref.rest_0_.old_ref), channel_id=1, source_target_pairs={{2,4},{3,5},{6,8},{7,9},{10,12},{11,13},{14,16},{15,17},{18,20},{1... | collective-permute-start | bytes 786440 | tf_op jit(solution)/shard_map/ppermute | solution.py:526
  44.9 18.2 %collective-permute-start.10 = (bf16[512,256]{1,0:T(8,128)(2,1)S(1)}, bf16[512,256]{1,0:T(8,128)(2,1)S(1)}, u32[]{:S(2)}, u32[]{:S(2)}) collective-permute-start(bf16[512,256]{1,0:T(8,128)(2,1)S(1)} %get-tuple-element.53), channel_id=1, source_target_pairs={{0,64},{1,17},{2,66},{3,19},{4,68},{5,21},{6,70},{7,23},{8,72},{9,... | collective-permute-start | bytes 786440 | tf_op jit(solution)/shard_map/ppermute | solution.py:505
  45.0 18.2 %collective-permute-start.9 = (bf16[512,256]{1,0:T(8,128)(2,1)S(1)}, bf16[512,256]{1,0:T(8,128)(2,1)S(1)}, u32[]{:S(2)}, u32[]{:S(2)}) collective-permute-start(bf16[512,256]{1,0:T(8,128)(2,1)S(1)} %get-tuple-element.52), channel_id=1, source_target_pairs={{0,192},{1,49},{2,194},{3,51},{4,196},{5,53},{6,198},{7,55},{8,200... | collective-permute-start | bytes 786440 | tf_op jit(solution)/shard_map/ppermute | solution.py:504
  65.0 6.4 %collective-permute-start.11 = (bf16[128,256]{1,0:T(8,128)(2,1)S(1)}, bf16[128,256]{1,0:T(8,128)(2,1)S(1)}, u32[]{:S(2)}, u32[]{:S(2)}) collective-permute-start(bf16[128,256]{1,0:T(8,128)(2,1)S(1)} %get-tuple-element.61), channel_id=1, source_target_pairs={{0,1},{1,0},{2,3},{3,2},{4,5},{5,4},{6,7},{7,6},{8,9},{9,8},{10,11... | collective-permute-start | bytes 196616 | tf_op jit(solution)/shard_map/ppermute | solution.py:533
  75.5 7.1 %collective-permute-start.14 = (bf16[64,256]{1,0:T(8,128)(2,1)S(1)}, bf16[64,256]{1,0:T(8,128)(2,1)S(1)}, u32[]{:S(2)}, u32[]{:S(2)}) collective-permute-start(bf16[64,256]{1,0:T(8,128)(2,1)S(1)} %shard_map.75.refs_0_), channel_id=1, source_target_pairs={{0,8},{4,12},{8,0},{12,4},{16,24},{20,28},{24,16},{28,20},{32,40},... | collective-permute-start | bytes 98312 | tf_op jit(solution)/shard_map/ppermute | solution.py:489
  75.6 7.4 %collective-permute-start.15 = (bf16[64,256]{1,0:T(8,128)(2,1)S(1)}, bf16[64,256]{1,0:T(8,128)(2,1)S(1)}, u32[]{:S(2)}, u32[]{:S(2)}) collective-permute-start(bf16[64,256]{1,0:T(8,128)(2,1)S(1)} %shard_map.75.refs_0_), channel_id=1, source_target_pairs={{0,4},{4,8},{8,12},{12,0},{16,20},{20,24},{24,28},{28,16},{32,36},... | collective-permute-start | bytes 98312 | tf_op jit(solution)/shard_map/ppermute | solution.py:489
  84.0 6.4 %collective-permute-start.18 = (bf16[256,256]{1,0:T(8,128)(2,1)S(1)}, bf16[256,256]{1,0:T(8,128)(2,1)S(1)}, u32[]{:S(2)}, u32[]{:S(2)}) collective-permute-start(bf16[256,256]{1,0:T(8,128)(2,1)S(1)} %shard_map.76.refs_0_), channel_id=1, source_target_pairs={{0,16},{1,65},{2,18},{3,67},{4,20},{5,69},{6,22},{7,71},{8,24},{9,... | collective-permute-start | bytes 393224 | tf_op jit(solution)/shard_map/ppermute | solution.py:494
  91.0 15.9 %collective-permute-start.24 = (bf16[1024,256]{1,0:T(8,128)(2,1)S(1)}, bf16[1024,256]{1,0:T(8,128)(2,1)S(1)}, u32[]{:S(2)}, u32[]{:S(2)}) collective-permute-start(bf16[1024,256]{1,0:T(8,128)(2,1)S(1)} %shard_map.77.line_ref), channel_id=1, source_target_pairs={{0,192},{1,49},{2,194},{3,51},{4,196},{5,53},{6,198},{7,55},{8,200... | collective-permute-start | bytes 1572872 | tf_op jit(solution)/shard_map/ppermute | solution.py:499
  91.1 15.8 %collective-permute-start.25 = (bf16[1024,256]{1,0:T(8,128)(2,1)S(1)}, bf16[1024,256]{1,0:T(8,128)(2,1)S(1)}, u32[]{:S(2)}, u32[]{:S(2)}) collective-permute-start(bf16[1024,256]{1,0:T(8,128)(2,1)S(1)} %shard_map.77.line_ref), channel_id=1, source_target_pairs={{0,64},{1,17},{2,66},{3,19},{4,68},{5,21},{6,70},{7,23},{8,72},{9,... | collective-permute-start | bytes 1572872 | tf_op jit(solution)/shard_map/ppermute | solution.py:499
  96.6 9.7 %collective-permute-start.20 = (bf16[1024,128]{1,0:T(8,128)(2,1)S(1)}, bf16[1024,128]{1,0:T(8,128)(2,1)S(1)}, u32[]{:S(2)}, u32[]{:S(2)}) collective-permute-start(bf16[1024,128]{1,0:T(8,128)(2,1)S(1)} %get-tuple-element.69), channel_id=1, source_target_pairs={{0,1},{1,0},{2,3},{3,2},{4,5},{5,4},{6,7},{7,6},{8,9},{9,8},{10,11... | collective-permute-start | bytes 786440 | tf_op jit(solution)/shard_map/ppermute | solution.py:542
  106.8 7.5 %collective-permute-start.21 = (bf16[1024,128]{1,0:T(8,128)(2,1)S(1)}, bf16[1024,128]{1,0:T(8,128)(2,1)S(1)}, u32[]{:S(2)}, u32[]{:S(2)}) collective-permute-start(bf16[1024,128]{1,0:T(8,128)(2,1)S(1)} %shard_map.80), channel_id=1, source_target_pairs={{0,2},{1,3},{2,0},{3,1},{4,6},{5,7},{6,4},{7,5},{8,10},{9,11},{10,... | collective-permute-start | bytes 786440 | tf_op jit(solution)/shard_map/ppermute | solution.py:543
  107.6 15.7 %collective-permute-start.26 = (bf16[512,256]{1,0:T(8,128)(2,1)S(1)}, bf16[512,256]{1,0:T(8,128)(2,1)S(1)}, u32[]{:S(2)}, u32[]{:S(2)}) collective-permute-start(bf16[512,256]{1,0:T(8,128)(2,1)S(1)} %get-tuple-element.70), channel_id=1, source_target_pairs={{0,192},{1,49},{2,194},{3,51},{4,196},{5,53},{6,198},{7,55},{8,200... | collective-permute-start | bytes 786440 | tf_op jit(solution)/shard_map/ppermute | solution.py:504
  110.1 13.2 %collective-permute-start.27 = (bf16[512,256]{1,0:T(8,128)(2,1)S(1)}, bf16[512,256]{1,0:T(8,128)(2,1)S(1)}, u32[]{:S(2)}, u32[]{:S(2)}) collective-permute-start(bf16[512,256]{1,0:T(8,128)(2,1)S(1)} %get-tuple-element.71), channel_id=1, source_target_pairs={{0,64},{1,17},{2,66},{3,19},{4,68},{5,21},{6,70},{7,23},{8,72},{9,... | collective-permute-start | bytes 786440 | tf_op jit(solution)/shard_map/ppermute | solution.py:505
  115.0 19.4 %collective-permute-start.22 = (bf16[1024,128]{1,0:T(8,128)(2,1)S(1)}, bf16[1024,128]{1,0:T(8,128)(2,1)S(1)}, u32[]{:S(2)}, u32[]{:S(2)}) collective-permute-start(bf16[1024,128]{1,0:T(8,128)(2,1)S(1)} %shard_map.81.own_ref.field_ref), channel_id=1, source_target_pairs={{0,2},{1,3},{2,0},{3,1},{4,6},{5,7},{6,4},{7,5},{8,10},{9,11},{10,... | collective-permute-start | bytes 786440 | tf_op jit(solution)/shard_map/ppermute | solution.py:552
  115.4 19.0 %collective-permute-start.23 = (bf16[1024,128]{1,0:T(8,128)(2,1)S(1)}, bf16[1024,128]{1,0:T(8,128)(2,1)S(1)}, u32[]{:S(2)}, u32[]{:S(2)}) collective-permute-start(bf16[1024,128]{1,0:T(8,128)(2,1)S(1)} %shard_map.81.own_ref.field_ref), channel_id=1, source_target_pairs={{2,4},{3,5},{6,8},{7,9},{10,12},{11,13},{14,16},{15,17},{18,20},{1... | collective-permute-start | bytes 786440 | tf_op jit(solution)/shard_map/ppermute | solution.py:553
  125.5 6.2 %collective-permute-start.31 = (bf16[512,128]{1,0:T(8,128)(2,1)S(1)}, bf16[512,128]{1,0:T(8,128)(2,1)S(1)}, u32[]{:S(2)}, u32[]{:S(2)}) collective-permute-start(bf16[512,128]{1,0:T(8,128)(2,1)S(1)} %get-tuple-element.82), channel_id=1, source_target_pairs={{0,1},{1,0},{2,3},{3,2},{4,5},{5,4},{6,7},{7,6},{8,9},{9,8},{10,11... | collective-permute-start | bytes 393224 | tf_op jit(solution)/shard_map/ppermute | solution.py:542
  133.4 6.6 %collective-permute-start.30 = (bf16[512,128]{1,0:T(8,128)(2,1)S(1)}, bf16[512,128]{1,0:T(8,128)(2,1)S(1)}, u32[]{:S(2)}, u32[]{:S(2)}) collective-permute-start(bf16[512,128]{1,0:T(8,128)(2,1)S(1)} %shard_map.89), channel_id=1, source_target_pairs={{0,2},{1,3},{2,0},{3,1},{4,6},{5,7},{6,4},{7,5},{8,10},{9,11},{10,... | collective-permute-start | bytes 393224 | tf_op jit(solution)/shard_map/ppermute | solution.py:543
  140.8 9.8 %collective-permute-start.33 = (bf16[1024,128]{1,0:T(8,128)(2,1)S(1)}, bf16[1024,128]{1,0:T(8,128)(2,1)S(1)}, u32[]{:S(2)}, u32[]{:S(2)}) collective-permute-start(bf16[1024,128]{1,0:T(8,128)(2,1)S(1)} %get-tuple-element.83.own_ref), channel_id=1, source_target_pairs={{0,1},{1,0},{2,3},{3,2},{4,5},{5,4},{6,7},{7,6},{8,9},{9,8},{10,11... | collective-permute-start | bytes 786440 | tf_op jit(solution)/shard_map/ppermute | solution.py:568
  141.8 7.8 %collective-permute-start.34 = (bf16[512,128]{1,0:T(8,128)(2,1)S(1)}, bf16[512,128]{1,0:T(8,128)(2,1)S(1)}, u32[]{:S(2)}, u32[]{:S(2)}) collective-permute-start(bf16[512,128]{1,0:T(8,128)(2,1)S(1)} %shard_map.91.done_ref), channel_id=1, source_target_pairs={{0,2},{1,3},{2,0},{3,1},{4,6},{5,7},{6,4},{7,5},{8,10},{9,11},{10,... | collective-permute-start | bytes 393224 | tf_op jit(solution)/shard_map/ppermute | solution.py:565
  (19 other events, 87.2 us)
